TPU v7x, 32 devices: a whole 2x2x4 slice. The times are simulated.
32 devices in a mesh: row: 4 (over z), col: 8 (over y, x, core).
Axes of the slice: x: 2, y: 2, z: 4, core: 2. Of those that a mesh axis runs over, the one named last changes fastest.
Arguments:
- features: bfloat16 [32, 64, 1024], P('row', 'col'), may hold values from -6 to 6
- gate_branch: bfloat16 [32, 64, 1024], P('row', 'col'), may hold values from -6 to 6
- w_row_proj: bfloat16 [1024, 128], replicated, may hold values from -0.1875 to 0.1875
- w_dt_row: bfloat16 [2, 32, 1024], P(None, None, 'col'), may hold values from -1 to 1
- dt_bias_row: float32 [2, 1024], P(None, 'col'), may hold values from -5 to -1
- rate_row: float32 [2, 1024, 16], P(None, 'col'), may hold values from 0.01 to 1
- skip_row: float32 [1024], P('col'), may hold values from 0.5 to 1.5
- conv_kernel: float32 [3, 3, 1024], P(None, None, 'col'), may hold values from -2 to 2
- conv_bias: float32 [1024], P('col'), may hold values from -3 to 3
- w_col_proj: bfloat16 [1024, 128], replicated, may hold values from -0.1875 to 0.1875
- w_dt_col: bfloat16 [2, 32, 1024], P(None, None, 'row'), may hold values from -1 to 1
- dt_bias_col: float32 [2, 1024], P(None, 'row'), may hold values from -5 to -1
- rate_col: float32 [2, 1024, 16], P(None, 'row'), may hold values from 0.01 to 1
Outputs:
- block_out: bfloat16 [32, 64, 1024], P(None, 'col', 'row')
All inputs are finite; a program needn't handle non-finite values.
Results may differ from a plain program's by a relative error of at most 0.0085.
The roundings to bfloat16 on the way count: a program that leaves them out, or rounds other values in their place, can miss the bound.
Values may be sent and summed in bfloat16 or wider, within the bound.
No kernel may reach another device: no remote copies, remote signals or barrier semaphores. Data moves between devices by JAX's collectives and lax.ppermute only.
A program may use at most 64 MiB of HBM per device.

v0:
```python
import math

import jax
import jax.numpy as jnp
from jax import lax
from jax.sharding import PartitionSpec as P


def extended(cells, sides, width):
    for axis, dim in sides:
        count = lax.axis_size(axis)
        ends = count - 1
        head = lax.slice_in_dim(cells, 0, width, axis=dim)
        tail = lax.slice_in_dim(cells, cells.shape[dim] - width, cells.shape[dim], axis=dim)
        cells = jnp.concatenate(
            [
                lax.ppermute(tail, axis, [(i, (i + 1) % count) for i in range(ends)]),
                cells,
                lax.ppermute(head, axis, [((i + 1) % count, i) for i in range(ends)]),
            ],
            axis=dim,
        )
    return cells


def block_scan(values, step_sizes, drive_in, read_out, decay_rates, reverse):
    if reverse:
        values = jnp.flip(values, 0)
        step_sizes = jnp.flip(step_sizes, 0)
        drive_in = jnp.flip(drive_in, 0)
        read_out = jnp.flip(read_out, 0)
    positions, line_count, channels = values.shape
    state_width = drive_in.shape[2]
    lanes = line_count * channels
    block_len = math.gcd(positions, 8)
    block_count = positions // block_len
    rates_wide = jnp.tile(jnp.transpose(decay_rates), (1, line_count))
    later = lax.broadcasted_iota(jnp.int32, (block_len, block_len), 0)
    earlier = lax.broadcasted_iota(jnp.int32, (block_len, block_len), 1)
    causal = (earlier <= later)[:, :, None, None]

    def widen(member):
        return jnp.repeat(jnp.swapaxes(member, 1, 2), channels, axis=2)

    def advance(carried, pieces):
        value_blk, step_blk, drive_blk, read_blk = pieces
        summed_rates = jnp.cumsum(step_blk[:, None, :] * rates_wide, axis=0)
        drives = (step_blk * value_blk)[:, None, :] * widen(drive_blk)
        spread = jnp.maximum(summed_rates[:, None] - summed_rates[None, :], 0.0)
        decay_pairs = jnp.where(causal, jnp.exp(-spread), 0.0)
        gathered = jnp.sum(decay_pairs * drives[None], axis=1)
        states = jnp.exp(-summed_rates) * carried[None] + gathered
        return (states[-1], jnp.sum(states * widen(read_blk), axis=1))

    flat_values = values.reshape(block_count, block_len, lanes)
    flat_steps = step_sizes.reshape(block_count, block_len, lanes)
    grouped_drive = drive_in.reshape(block_count, block_len, line_count, state_width)
    grouped_read = read_out.reshape(block_count, block_len, line_count, state_width)
    initial = jnp.zeros((state_width, lanes), jnp.float32)
    last_state, outputs = lax.scan(
        advance, initial, (flat_values, flat_steps, grouped_drive, grouped_read)
    )
    outputs = outputs.reshape(positions, line_count, channels)
    if reverse:
        outputs = jnp.flip(outputs, 0)
    return outputs


def both_ways(values, projections, step_weight, step_bias, decay_rates, skip_gain):
    low_rank = step_weight.shape[1]
    state_width = decay_rates.shape[2]
    segment = low_rank + 2 * state_width
    if skip_gain is None:
        summed = jnp.zeros(values.shape, jnp.float32)
    else:
        summed = skip_gain * values
    for direction in range(2):
        offset = direction * segment
        low_part = projections[:, :, offset : offset + low_rank]
        raw_steps = jnp.einsum(
            "plr,rc->plc", low_part, step_weight[direction], preferred_element_type=jnp.float32
        )
        step_sizes = jax.nn.softplus(raw_steps + step_bias[direction])
        drive_in = projections[:, :, offset + low_rank : offset + low_rank + state_width].astype(
            jnp.float32
        )
        read_out = projections[:, :, offset + low_rank + state_width : offset + segment].astype(
            jnp.float32
        )
        summed = summed + block_scan(
            values, step_sizes, drive_in, read_out, decay_rates[direction], direction == 1
        )
    return summed


def local(
    features,
    gate_branch,
    w_row_proj,
    w_dt_row,
    dt_bias_row,
    rate_row,
    skip_row,
    conv_kernel,
    conv_bias,
    w_col_proj,
    w_dt_col,
    dt_bias_col,
    rate_col,
):
    rows_here, cols_here, channels_all = features.shape
    tile_proj = jnp.dot(
        features.reshape(-1, channels_all), w_row_proj, preferred_element_type=jnp.float32
    )
    tile_proj = tile_proj.astype(jnp.bfloat16).reshape(rows_here, cols_here, -1)
    line_proj = lax.all_gather(tile_proj, "col", axis=1, tiled=True)
    line_values, line_gate = (
        lax.all_to_all(features, "col", split_axis=2, concat_axis=1, tiled=True),
        lax.all_to_all(gate_branch, "col", split_axis=2, concat_axis=1, tiled=True),
    )
    row_scanned = both_ways(
        jnp.swapaxes(line_values, 0, 1).astype(jnp.float32),
        jnp.swapaxes(line_proj, 0, 1),
        w_dt_row,
        dt_bias_row,
        rate_row,
        skip_row,
    )
    row_mix = jnp.swapaxes(row_scanned, 0, 1)
    gated_rows = (row_mix * jax.nn.silu(line_gate.astype(jnp.float32))).astype(jnp.bfloat16)
    padded = extended(gated_rows, (("row", 0),), 1)
    padded = jnp.pad(padded.astype(jnp.float32), ((0, 0), (1, 1), (0, 0)))
    width_all = gated_rows.shape[1]
    accumulated = jnp.zeros(gated_rows.shape, jnp.float32) + conv_bias
    for vertical in range(3):
        for lateral in range(3):
            accumulated = (
                accumulated
                + conv_kernel[vertical, lateral]
                * padded[vertical : vertical + rows_here, lateral : lateral + width_all]
            )
    mixed_cells = jax.nn.silu(accumulated).astype(jnp.bfloat16)
    tile_cells = lax.all_to_all(mixed_cells, "col", split_axis=1, concat_axis=2, tiled=True)
    tile_colproj = jnp.dot(
        tile_cells.reshape(-1, channels_all), w_col_proj, preferred_element_type=jnp.float32
    )
    tile_colproj = tile_colproj.astype(jnp.bfloat16).reshape(rows_here, cols_here, -1)
    column_cells = lax.all_to_all(tile_cells, "row", split_axis=2, concat_axis=0, tiled=True)
    column_proj = lax.all_gather(tile_colproj, "row", axis=0, tiled=True)
    column_out = both_ways(
        column_cells.astype(jnp.float32), column_proj, w_dt_col, dt_bias_col, rate_col, None
    )
    return column_out.astype(jnp.bfloat16)


def solution(mesh):
    return jax.shard_map(
        local,
        mesh=mesh,
        in_specs=(
            P("row", "col", None),
            P("row", "col", None),
            P(),
            P(None, None, "col"),
            P(None, "col"),
            P(None, "col", None),
            P("col"),
            P(None, None, "col"),
            P("col"),
            P(),
            P(None, None, "row"),
            P(None, "row"),
            P(None, "row", None),
        ),
        out_specs=P(None, "col", "row"),
        check_vma=False,
    )
```

profile of v0, /device:TPU:0, one launch (start us, length us, event | category | flops | bytes accessed | tf_op | source)
XLA Modules:
  0.0 235.7 jit_solution(3618847819257033381)
XLA Ops:
  0.0 2.4 %copy.98 = bf16[8,8,1024]{1,0,2:T(8,128)(2,1)S(1)} copy(bf16[8,8,1024]{2,1,0:T(8,128)(2,1)} %param.21) | data formatting | bytes 262144 | tf_op args[0]
  2.4 2.8 %reshape.358 = bf16[8,2,4096]{2,1,0:T(2,128)(2,1)} reshape(bf16[1024,8,8]{2,1,0:T(8,128)(2,1)S(1)} %bitcast.344) | data formatting | bytes 262144
  5.2 5.3 %all-to-all-start = ((bf16[8,2,4096]{2,1,0:T(2,128)(2,1)}), bf16[8,2,4096]{2,1,0:T(2,128)(2,1)S(1)}, u32[]{:S(2)}, u32[]{:S(2)}) async-start(bf16[8,2,4096]{2,1,0:T(2,128)(2,1)} %reshape.358), calls=%async_computation | async-start | bytes 262144 | tf_op jit(solution)/shard_map/all_to_all | solution.py:118
  10.8 9.7 %all_gather.6 = bf16[8,64,128]{2,0,1:T(8,128)(2,1)S(1)} all-gather(bf16[8,8,128]{2,0,1:T(8,128)(2,1)S(1)} %copy.100), channel_id=1, replica_groups=mesh['row'=4,'col'=8] {'col'}, dimensions={1}, use_global_device_ids=true | all-gather | bytes 147456 | tf_op jit(solution)/shard_map/all_gather | solution.py:116
  25.9 2.8 %reshape.356 = bf16[8,2,4096]{2,1,0:T(2,128)(2,1)} reshape(bf16[1024,8,8]{2,1,0:T(8,128)(2,1)S(1)} %bitcast.345) | data formatting | bytes 262144
  28.8 4.2 %all-to-all-start.1 = ((bf16[8,2,4096]{2,1,0:T(2,128)(2,1)}), bf16[8,2,4096]{2,1,0:T(2,128)(2,1)}, u32[]{:S(2)}, u32[]{:S(2)}) async-start(bf16[8,2,4096]{2,1,0:T(2,128)(2,1)} %reshape.356), calls=%async_computation.1 | async-start | bytes 262144 | tf_op jit(solution)/shard_map/all_to_all | solution.py:119
  33.0 2.5 %reshape.359 = bf16[1024,8,8]{2,1,0:T(8,128)(2,1)S(1)} reshape(bf16[8,2,4096]{2,1,0:T(2,128)(2,1)S(1)} %all-to-all-done) | data formatting | bytes 262144
  38.1 32.0 %while.53 = (s32[]{:T(128)}, f32[16,1024]{1,0:T(8,128)S(1)}, f32[8,8,1024]{2,1,0:T(8,128)S(1)}, f32[8,8,1024]{2,1,0:T(8,128)S(1)}, f32[8,8,1024]{2,1,0:T(8,128)}...) while((s32[]{:T(128)}, f32[16,1024]{1,0:T(8,128)S(1)}, ...), condition=%wide.region_9.10_spmd.clone, body=%wide.region_5.9_spmd.clone.sunk | while | flops 7995458 | bytes 9224429 | solution.py:60
  70.2 32.0 %while.52 = (s32[]{:T(128)}, f32[16,1024]{1,0:T(8,128)S(1)}, f32[8,8,1024]{2,1,0:T(8,128)S(1)}, f32[8,8,1024]{2,1,0:T(8,128)S(1)}, f32[8,8,1024]{2,1,0:T(8,128)}...) while((s32[]{:T(128)}, f32[16,1024]{1,0:T(8,128)S(1)}, ...), condition=%wide.region_4.5_spmd.clone, body=%wide.region_0.4_spmd.clone.sunk | while | flops 7995458 | bytes 9224429 | solution.py:60
  103.0 3.3 %reshape.357 = bf16[1024,8,8]{2,1,0:T(8,128)(2,1)S(1)} reshape(bf16[8,2,4096]{2,1,0:T(2,128)(2,1)} %all-to-all-done.1) | data formatting | bytes 262144
  107.7 3.5 %collective-permute-start = (bf16[1,64,128]{2,0,1:T(2,128)(2,1)S(1)}, bf16[1,64,128]{2,0,1:T(2,128)(2,1)S(1)}, u32[]{:S(2)}, u32[]{:S(2)}) collective-permute-start(bf16[1,64,128]{2,0,1:T(2,128)(2,1)S(1)} %get-tuple-element.357), channel_id=1, source_target_pairs={{0,8},{8,16},{16,24},{1,9},{9,17},{17,25},{2,10},{10,18},{18,26},{... | collective-permute-start | bytes 49160 | tf_op jit(solution)/shard_map/ppermute | solution.py:17
  112.8 4.2 %collective-permute-done.1 = bf16[1,64,128]{2,0,1:T(2,128)(2,1)S(1)} collective-permute-done((bf16[1,64,128]{2,0,1:T(2,128)(2,1)S(1)}, bf16[1,64,128]{2,0,1:T(2,128)(2,1)S(1)}, u32[]{:S(2)}, u32[]{:S(2)}) %collective-permute-start.1) | collective-permute-done | bytes 16416 | tf_op jit(solution)/shard_map/ppermute | solution.py:19
  118.1 3.9 %all-to-all-start.2 = ((bf16[8,64,128]{2,0,1:T(8,128)(2,1)}), bf16[8,64,128]{2,0,1:T(8,128)(2,1)S(1)}, u32[]{:S(2)}, u32[]{:S(2)}) async-start(bf16[8,64,128]{2,0,1:T(8,128)(2,1)} %multiply_convert_fusion), calls=%async_computation.2 | async-start | bytes 262144 | tf_op jit(solution)/shard_map/all_to_all | solution.py:143
  122.0 5.5 %all-to-all-done.2 = bf16[8,64,128]{2,0,1:T(8,128)(2,1)S(1)} async-done(((bf16[8,64,128]{2,0,1:T(8,128)(2,1)}), bf16[8,64,128]{2,0,1:T(8,128)(2,1)S(1)}, u32[]{:S(2)}, u32[]{:S(2)}) %all-to-all-start.2) | async-done | bytes 131104 | tf_op jit(solution)/shard_map/all_to_all | solution.py:143
  129.1 2.8 %reshape.360 = bf16[4,2,8192]{2,1,0:T(2,128)(2,1)} reshape(bf16[1024,8,8]{2,1,0:T(8,128)(2,1)S(1)} %bitcast.342) | data formatting | bytes 262144
  131.9 3.9 %all-to-all-start.3 = ((bf16[4,2,8192]{2,1,0:T(2,128)(2,1)}), bf16[4,2,8192]{2,1,0:T(2,128)(2,1)S(1)}, u32[]{:S(2)}, u32[]{:S(2)}) async-start(bf16[4,2,8192]{2,1,0:T(2,128)(2,1)} %reshape.360), calls=%async_computation.3 | async-start | bytes 262144 | tf_op jit(solution)/shard_map/all_to_all | solution.py:148
  136.0 13.9 %all_gather.7 = bf16[32,8,128]{2,1,0:T(8,128)(2,1)S(1)} all-gather(bf16[8,8,128]{2,1,0:T(8,128)(2,1)S(1)} %fusion.37), channel_id=1, replica_groups=mesh['row'=4,'col'=8] {'row'}, dimensions={0}, use_global_device_ids=true | all-gather | bytes 81920 | tf_op jit(solution)/shard_map/all_gather | solution.py:149
  152.9 2.4 %reshape.361 = bf16[1024,8,8]{2,1,0:T(8,128)(2,1)S(1)} reshape(bf16[4,2,8192]{2,1,0:T(2,128)(2,1)S(1)} %all-to-all-done.3) | data formatting | bytes 262144
  159.1 32.9 %while.55 = (s32[]{:T(128)}, f32[16,2048]{1,0:T(8,128)}, f32[4,8,2048]{2,1,0:T(8,128)}, f32[4,8,2048]{2,1,0:T(8,128)S(1)}, f32[4,8,2048]{2,1,0:T(8,128)S(1)}, /*...) while((s32[]{:T(128)}, f32[16,2048]{1,0:T(8,128)}, ...), condition=%wide.region_19.20_spmd.clone, body=%wide.region_15.19_spmd.clone.sunk | while | flops 15990850 | bytes 22864840 | solution.py:60
  160.6 2.3 multiply_reduce_fusion.22
  168.8 2.3 multiply_reduce_fusion.22
  177.0 2.3 multiply_reduce_fusion.22
  185.3 2.3 multiply_reduce_fusion.22
  195.1 37.9 %while.54 = (s32[]{:T(128)}, f32[16,2048]{1,0:T(8,128)}, f32[4,8,2048]{2,1,0:T(8,128)}, f32[4,8,2048]{2,1,0:T(8,128)}, f32[4,8,2048]{2,1,0:T(8,128)}, /*index=5*...) while((s32[]{:T(128)}, f32[16,2048]{1,0:T(8,128)}, ...), condition=%wide.region_14.15_spmd.clone, body=%wide.region_10.14_spmd.clone.sunk | while | flops 15990850 | bytes 19456772 | solution.py:60
  (592 shorter events, 150.2 us)
Async XLA Ops:
  0.0 10.6 %copy-start = (bf16[1024,128]{1,0:T(8,128)(2,1)S(1)}, bf16[1024,128]{1,0:T(8,128)(2,1)}, u32[]{:S(2)}) copy-start(bf16[1024,128]{1,0:T(8,128)(2,1)} %param.23) | copy-start | bytes 786436
  0.0 10.6 %copy-start.11 = (bf16[8,8,1024]{2,1,0:T(8,128)(2,1)S(1)}, bf16[8,8,1024]{2,1,0:T(8,128)(2,1)}, u32[]{:S(2)}) copy-start(bf16[8,8,1024]{2,1,0:T(8,128)(2,1)} %param.21) | copy-start | bytes 393220
  5.2 16.9 %copy-start.18 = (f32[2,128]{1,0:T(2,128)S(1)}, f32[2,128]{1,0:T(2,128)}, u32[]{:S(2)}) copy-start(f32[2,128]{1,0:T(2,128)} %param.25) | copy-start | bytes 3076
  5.2 17.0 %copy-start.22 = (bf16[2,32,128]{2,1,0:T(8,128)(2,1)S(1)}, bf16[2,32,128]{2,1,0:T(8,128)(2,1)}, u32[]{:S(2)}) copy-start(bf16[2,32,128]{2,1,0:T(8,128)(2,1)} %param.24) | copy-start | bytes 49156
  5.2 23.6 %all-to-all-start = ((bf16[8,2,4096]{2,1,0:T(2,128)(2,1)}), bf16[8,2,4096]{2,1,0:T(2,128)(2,1)S(1)}, u32[]{:S(2)}, u32[]{:S(2)}) async-start(bf16[8,2,4096]{2,1,0:T(2,128)(2,1)} %reshape.358), calls=%async_computation | async-start | bytes 262144 | tf_op jit(solution)/shard_map/all_to_all | solution.py:118
  24.4 4.4 %copy-start.14 = (f32[2,256,16]{1,2,0:T(8,128)S(1)}, f32[2,256,16]{1,2,0:T(8,128)}, u32[]{:S(2)}) copy-start(f32[2,256,16]{1,2,0:T(8,128)} %param.33) | copy-start | bytes 98308
  24.4 4.4 %copy-start.15 = (f32[2,128,16]{1,2,0:T(8,128)S(1)}, f32[2,128,16]{1,2,0:T(8,128)}, u32[]{:S(2)}) copy-start(f32[2,128,16]{1,2,0:T(8,128)} %param.26) | copy-start | bytes 49156
  28.8 74.2 %all-to-all-start.1 = ((bf16[8,2,4096]{2,1,0:T(2,128)(2,1)}), bf16[8,2,4096]{2,1,0:T(2,128)(2,1)}, u32[]{:S(2)}, u32[]{:S(2)}) async-start(bf16[8,2,4096]{2,1,0:T(2,128)(2,1)} %reshape.356), calls=%async_computation.1 | async-start | bytes 262144 | tf_op jit(solution)/shard_map/all_to_all | solution.py:119
  103.0 4.5 %copy-start.6 = (f32[8,8,8,128]{3,2,1,0:T(8,128)S(1)}, f32[8,8,8,128]{3,2,1,0:T(8,128)}, u32[]{:S(2)}) copy-start(f32[8,8,8,128]{3,2,1,0:T(8,128)} %copy.113) | copy-start | bytes 786436
  103.0 4.5 %copy-start.20 = (f32[128]{0:T(128)S(1)}, f32[128]{0:T(128)}, u32[]{:S(2)}) copy-start(f32[128]{0:T(128)} %param.27) | copy-start | bytes 1540
  106.4 6.1 %copy-start.16 = (f32[3,3,128]{2,1,0:T(4,128)S(1)}, f32[3,3,128]{2,1,0:T(4,128)}, u32[]{:S(2)}) copy-start(f32[3,3,128]{2,1,0:T(4,128)} %param.28) | copy-start | bytes 13828
  106.4 10.8 %copy-start.19 = (f32[128]{0:T(128)S(1)}, f32[128]{0:T(128)}, u32[]{:S(2)}) copy-start(f32[128]{0:T(128)} %param.29) | copy-start | bytes 1540
  107.5 14.5 %copy-start.17 = (f32[2,256]{1,0:T(2,128)S(1)}, f32[2,256]{1,0:T(2,128)}, u32[]{:S(2)}) copy-start(f32[2,256]{1,0:T(2,128)} %param.32) | copy-start | bytes 6148
  107.7 5.1 %collective-permute-start = (bf16[1,64,128]{2,0,1:T(2,128)(2,1)S(1)}, bf16[1,64,128]{2,0,1:T(2,128)(2,1)S(1)}, u32[]{:S(2)}, u32[]{:S(2)}) collective-permute-start(bf16[1,64,128]{2,0,1:T(2,128)(2,1)S(1)} %get-tuple-element.357), channel_id=1, source_target_pairs={{0,8},{8,16},{16,24},{1,9},{9,17},{17,25},{2,10},{10,18},{18,26},{... | collective-permute-start | bytes 49160 | tf_op jit(solution)/shard_map/ppermute | solution.py:17
  111.2 5.8 %collective-permute-start.1 = (bf16[1,64,128]{2,0,1:T(2,128)(2,1)S(1)}, bf16[1,64,128]{2,0,1:T(2,128)(2,1)S(1)}, u32[]{:S(2)}, u32[]{:S(2)}) collective-permute-start(bf16[1,64,128]{2,0,1:T(2,128)(2,1)S(1)} %get-tuple-element.358), channel_id=1, source_target_pairs={{8,0},{16,8},{24,16},{9,1},{17,9},{25,17},{10,2},{18,10},{26,18},{... | collective-permute-start | bytes 49160 | tf_op jit(solution)/shard_map/ppermute | solution.py:19
  118.1 9.4 %all-to-all-start.2 = ((bf16[8,64,128]{2,0,1:T(8,128)(2,1)}), bf16[8,64,128]{2,0,1:T(8,128)(2,1)S(1)}, u32[]{:S(2)}, u32[]{:S(2)}) async-start(bf16[8,64,128]{2,0,1:T(8,128)(2,1)} %multiply_convert_fusion), calls=%async_computation.2 | async-start | bytes 262144 | tf_op jit(solution)/shard_map/all_to_all | solution.py:143
  127.5 8.2 %copy-start.12 = (bf16[1024,128]{1,0:T(8,128)(2,1)S(1)}, bf16[1024,128]{1,0:T(8,128)(2,1)}, u32[]{:S(2)}) copy-start(bf16[1024,128]{1,0:T(8,128)(2,1)} %param.30) | copy-start | bytes 786436
  129.1 20.9 %copy-start.21 = (bf16[2,32,256]{2,1,0:T(8,128)(2,1)S(1)}, bf16[2,32,256]{2,1,0:T(8,128)(2,1)}, u32[]{:S(2)}) copy-start(bf16[2,32,256]{2,1,0:T(8,128)(2,1)} %param.31) | copy-start | bytes 98308
  131.9 20.9 %all-to-all-start.3 = ((bf16[4,2,8192]{2,1,0:T(2,128)(2,1)}), bf16[4,2,8192]{2,1,0:T(2,128)(2,1)S(1)}, u32[]{:S(2)}, u32[]{:S(2)}) async-start(bf16[4,2,8192]{2,1,0:T(2,128)(2,1)} %reshape.360), calls=%async_computation.3 | async-start | bytes 262144 | tf_op jit(solution)/shard_map/all_to_all | solution.py:148
  164.3 3.0 %copy-start.5 = (f32[4,8,2048]{2,1,0:T(8,128)S(1)}, f32[4,8,2048]{2,1,0:T(8,128)}, u32[]{:S(2)}) copy-start(f32[4,8,2048]{2,1,0:T(8,128)} %copy-done.4) | copy-start | bytes 786436 | tf_op jit(solution)/shard_map/while
  164.3 3.0 %copy-start.8 = (f32[4,8,8,16]{3,2,1,0:T(8,128)S(1)}, f32[4,8,8,16]{3,2,1,0:T(8,128)}, u32[]{:S(2)}) copy-start(f32[4,8,8,16]{3,2,1,0:T(8,128)} %copy-done.7) | copy-start | bytes 49156 | tf_op jit(solution)/shard_map/while
  164.3 3.0 %copy-start.10 = (f32[4,8,8,16]{3,2,1,0:T(8,128)S(1)}, f32[4,8,8,16]{3,2,1,0:T(8,128)}, u32[]{:S(2)}) copy-start(f32[4,8,8,16]{3,2,1,0:T(8,128)} %copy-done.9) | copy-start | bytes 49156 | tf_op jit(solution)/shard_map/while
  180.8 3.0 %copy-start.8 = (f32[4,8,8,16]{3,2,1,0:T(8,128)S(1)}, f32[4,8,8,16]{3,2,1,0:T(8,128)}, u32[]{:S(2)}) copy-start(f32[4,8,8,16]{3,2,1,0:T(8,128)} %copy-done.7) | copy-start | bytes 49156 | tf_op jit(solution)/shard_map/while
  180.8 3.0 %copy-start.10 = (f32[4,8,8,16]{3,2,1,0:T(8,128)S(1)}, f32[4,8,8,16]{3,2,1,0:T(8,128)}, u32[]{:S(2)}) copy-start(f32[4,8,8,16]{3,2,1,0:T(8,128)} %copy-done.9) | copy-start | bytes 49156 | tf_op jit(solution)/shard_map/while
  (32 other events, 53.9 us)
where the time goes:
time: 239 us; the launch traced here: 236 us
  local copies, waits for them, and re-layouts  92.6 us (39%)
  other arithmetic  82.7 us (35%)
  blocking collectives  23.6 us (10%)
  starting transfers between devices  22.1 us (9%)
  waiting for transfers between devices  9.97 us (4%)
  loops' own time  2.67 us (1%)
    reduce_sum x24, other arithmetic, advance(): gathered = jnp.sum(decay_pairs * drives[None], axis=1)  36.1 us
    unnamed x40, local copies, waits for them, and re-layouts  24.3 us
    broadcast_in_dim x72, local copies, waits for them, and re-layouts, widen(): return jnp.repeat(jnp.swapaxes(member, 1, 2), channels, axis=2)  20.4 us
    transpose x72, local copies, waits for them, and re-layouts, widen(): return jnp.repeat(jnp.swapaxes(member, 1, 2), channels, axis=2)  19.5 us
    mul x48, other arithmetic, advance(): drives = (step_blk * value_blk)[:, None, :] * widen(drive_blk)  17.5 us
    reduce_sum x24, other arithmetic, advance(): return (states[-1], jnp.sum(states * widen(read_blk), axis=1))  16.1 us
    all_gather x1, blocking collectives, local(): column_proj = lax.all_gather(tile_colproj, 'row', axis=0, tiled=True)  13.9 us
    all_gather x1, blocking collectives, local(): line_proj = lax.all_gather(tile_proj, 'col', axis=1, tiled=True)  9.72 us
  transfers between devices with their start and end apart: 6, of which 3 were waited for; matrix products, arithmetic and copies ran while one was open for 34% of the time, Pallas kernels for 0%

commit v1 on v0

v1 whole, which is shorter than its diff:
```python
import functools
import math

import jax
import jax.numpy as jnp
from jax import lax
from jax.experimental import pallas as pl
from jax.experimental.pallas import tpu as pltpu
from jax.sharding import PartitionSpec as P

LANES = 128
F32 = jnp.float32
BF16 = jnp.bfloat16
LOG2E = math.log2(math.e)


def dot(a, b):
    return jnp.dot(a, b, preferred_element_type=F32)


def silu(v):
    return v / (1.0 + jnp.exp(-v))


def softplus(v):
    return jnp.maximum(v, 0.0) + jnp.log1p(jnp.exp(-jnp.abs(v)))


def shuffle(tokens, outer, inner):
    shape = (tokens, tokens)
    to = lax.broadcasted_iota(jnp.int32, shape, 0).astype(F32)
    frm = lax.broadcasted_iota(jnp.int32, shape, 1).astype(F32)
    high = jnp.floor((to + 0.5) / inner)
    wanted = jnp.where(to < outer * inner, (to - high * inner) * outer + high, to)
    return jnp.where(frm == wanted, 1.0, 0.0).astype(BF16)


def pack_kernel(feat_ref, gate_ref, w_ref, out_ref):
    rows, cols, channels = feat_ref.shape
    tokens = rows * cols
    parts = out_ref.shape[0]
    share = channels // parts
    feats = feat_ref[...].reshape(tokens, channels)
    gates = gate_ref[...].reshape(tokens, channels)
    proj = dot(feats, w_ref[...]).astype(BF16)
    order = shuffle(tokens, cols, rows)
    feats = dot(order, feats).astype(BF16)
    gates = dot(order, gates).astype(BF16)
    proj = dot(order, proj).astype(BF16)
    for part in range(parts):
        out_ref[part, :, :share] = feats[:, part * share : (part + 1) * share]
        out_ref[part, :, share : 2 * share] = gates[:, part * share : (part + 1) * share]
        out_ref[part, :, 2 * share :] = proj


def prepare(proj, w_dt_ref, bias_ref, rate_ref, wide_ref, step_ref, rates_ref):
    _, rank, channels = w_dt_ref.shape
    state = rate_ref.shape[2]
    segment = rank + 2 * state
    lines = rates_ref.shape[2]
    wide_ref[...] = jnp.zeros_like(wide_ref)
    for k in range(2):
        wide_ref[pl.ds(k * segment, rank), pl.ds(k * channels, channels)] = w_dt_ref[k]
    raw = dot(proj, wide_ref[...])
    for k in range(2):
        part = raw[:, k * channels : (k + 1) * channels] + bias_ref[k : k + 1, :]
        step_ref[k] = softplus(part).reshape(step_ref.shape[1:])
        turned = jnp.transpose(rate_ref[k] * -LOG2E)
        for n in range(state):
            rates_ref[k, n] = jnp.broadcast_to(turned[n : n + 1, :], (lines, channels))


def scan(k, rank, step_ref, value_ref, proj_ref, rates_ref, out_ref, unroll):
    positions, lines, channels = out_ref.shape
    state = rates_ref.shape[1]
    base = k * (rank + 2 * state) + rank

    def advance(at, carried):
        pos = at if k == 0 else positions - 1 - at
        step = step_ref[k, pos]
        drive = step * value_ref[pos]
        proj = proj_ref[pos]
        total = out_ref[pos]
        states = []
        for n in range(state):
            b = jnp.broadcast_to(proj[:, base + n : base + n + 1], (lines, channels))
            c = jnp.broadcast_to(proj[:, base + state + n : base + state + n + 1], (lines, channels))
            s = jnp.exp2(step * rates_ref[k, n]) * carried[n] + drive * b
            states.append(s)
            total = total + c * s
        out_ref[pos] = total
        return tuple(states)

    zero = jnp.zeros((lines, channels), F32)
    lax.fori_loop(0, positions, advance, (zero,) * state, unroll=unroll)


def row_kernel(
    got_ref, w_dt_ref, bias_ref, rate_ref, skip_ref, out_ref, tail_ref,
    wide_ref, step_ref, rates_ref, value_ref, proj_ref, sum_ref, flat_ref,
):
    positions, lines, share = out_ref.shape
    rank = w_dt_ref.shape[1]
    width = got_ref.shape[2] - 2 * share
    proj = got_ref[:, :, 2 * share :].reshape(positions * lines, width)
    prepare(proj, w_dt_ref, bias_ref, rate_ref, wide_ref, step_ref, rates_ref)
    proj_ref[...] = proj.astype(F32).reshape(proj_ref.shape)
    values = got_ref[:, :, :share].astype(F32)
    value_ref[...] = values
    sum_ref[...] = values * skip_ref[...]
    for k in range(2):
        scan(k, rank, step_ref, value_ref, proj_ref, rates_ref, sum_ref, 4)
    gated = sum_ref[...] * silu(got_ref[:, :, share : 2 * share].astype(F32))
    out_ref[...] = gated.astype(BF16)
    flat_ref[...] = gated.reshape(flat_ref.shape)
    for j in range(2):
        tail_ref[j] = flat_ref[pl.ds(lines - 2 + j, positions, stride=lines), :].astype(BF16)


def conv_kernel(mid_ref, above_ref, taps_ref, bias_ref, out_ref, pad_ref, low_ref):
    positions, lines, share = mid_ref.shape
    parts = out_ref.shape[0]
    cols = positions // parts
    mid = mid_ref[...].astype(F32)
    zero_edge = jnp.zeros((1, lines + 8, share), F32)
    pad_ref[0:1] = zero_edge
    pad_ref[positions + 1 : positions + 2] = zero_edge
    pad_ref[1 : positions + 1, 8 : 8 + lines, :] = mid
    above = above_ref[...].astype(F32)
    pad_ref[1 : positions + 1, 6:7, :] = above[0][:, None, :]
    pad_ref[1 : positions + 1, 7:8, :] = above[1][:, None, :]
    total = jnp.zeros((positions, lines, share), F32) + bias_ref[...]
    for i in range(3):
        for j in range(3):
            total = total + taps_ref[i, j : j + 1, :] * pad_ref[j : j + positions, 6 + i : 6 + i + lines, :]
    main = silu(total).astype(BF16)
    out_ref[:, : cols * lines, :] = main.reshape(parts, cols * lines, share)
    low_ref[...] = jnp.zeros_like(low_ref)
    for j in range(2):
        low_ref[j, 8 : 8 + positions, :] = mid[:, lines - 2 + j, :]
    last = jnp.zeros((positions, share), F32) + bias_ref[...]
    for i in range(2):
        for j in range(3):
            last = last + taps_ref[i, j : j + 1, :] * low_ref[i, 7 + j : 7 + j + positions, :]
    out_ref[:, cols * lines :, :] = silu(last).astype(BF16).reshape(parts, cols, share)


def turn_kernel(me_ref, got_ref, w_ref, *out_refs, rows):
    parts, tokens, share = got_ref.shape
    width = w_ref.shape[1]
    count = len(out_refs)
    each = parts // count
    cols = tokens // (rows + 1)
    order = shuffle(tokens, rows, cols)
    total = jnp.zeros((tokens, width), F32)
    for part in range(parts):
        total = total + dot(got_ref[part], w_ref[pl.ds(part * share, share), :])
    proj = dot(order, total.astype(BF16)).astype(BF16)
    me = me_ref[0]
    for shift in range(count):
        to = lax.rem(me + shift, count)
        for j in range(each):
            moved = dot(order, got_ref[to * each + j]).astype(BF16)
            out_refs[shift][:, j * share : (j + 1) * share] = moved
        out_refs[shift][:, each * share :] = proj


def col_kernel(me_ref, *refs, count, rows):
    got_refs = refs[:count]
    (w_dt_ref, bias_ref, rate_ref, out_ref, wide_ref, step_ref, rates_ref, all_ref, value_ref, proj_ref, sum_ref) = refs[count:]
    positions, lines, share = out_ref.shape
    rank = w_dt_ref.shape[1]
    block = rows * lines
    me = me_ref[0]
    for shift in range(count):
        frm = lax.rem(me + count - shift, count)
        all_ref[pl.ds(pl.multiple_of(frm * block, block), block), :] = got_refs[shift][:block, :]

        @pl.when(frm == count - 1)
        def _():
            all_ref[pl.ds(count * block, lines), :] = got_refs[shift][block:, :]

    everything = all_ref[lines:, :]
    proj = everything[:, share:]
    prepare(proj, w_dt_ref, bias_ref, rate_ref, wide_ref, step_ref, rates_ref)
    proj_ref[...] = proj.astype(F32).reshape(proj_ref.shape)
    value_ref[...] = everything[:, :share].astype(F32).reshape(value_ref.shape)
    sum_ref[...] = jnp.zeros_like(sum_ref)
    for k in range(2):
        scan(k, rank, step_ref, value_ref, proj_ref, rates_ref, sum_ref, 4)
    out_ref[...] = sum_ref[...].astype(BF16)


def vmem():
    return pl.BlockSpec(memory_space=pltpu.VMEM)


def smem():
    return pl.BlockSpec(memory_space=pltpu.SMEM)


def call(kernel, name, outs, scratch, *args, scalars=0):
    many = isinstance(outs, (list, tuple))
    return pl.pallas_call(
        kernel,
        name=name,
        out_shape=outs,
        in_specs=[smem()] * scalars + [vmem()] * (len(args) - scalars),
        out_specs=[vmem()] * len(outs) if many else vmem(),
        scratch_shapes=scratch,
        compiler_params=pltpu.CompilerParams(vmem_limit_bytes=56 << 20),
    )(*args)


def array(shape, dtype=BF16):
    return jax.ShapeDtypeStruct(shape, dtype)


def scan_scratch(positions, lines, channels, width, state):
    return [
        pltpu.VMEM((width, 2 * channels), BF16),
        pltpu.VMEM((2, positions, lines, channels), F32),
        pltpu.VMEM((2, state, lines, channels), F32),
    ]


def local(
    features, gate_branch, w_row_proj, w_dt_row, dt_bias_row, rate_row, skip_row,
    conv_taps, conv_bias, w_col_proj, w_dt_col, dt_bias_col, rate_col,
):
    rows, cols, channels = features.shape
    width = w_row_proj.shape[1]
    state = rate_row.shape[2]
    n_col, n_row = lax.axis_size("col"), lax.axis_size("row")
    share, col_share = channels // n_col, channels // n_row
    line, column = cols * n_col, rows * n_row
    tokens, more = rows * cols, (rows + 1) * cols

    sent = call(pack_kernel, "pack", array((n_col, tokens, 2 * share + width)), [], features, gate_branch, w_row_proj)
    got = lax.all_to_all(sent, "col", 0, 0, tiled=True)
    gated, tail = call(
        row_kernel,
        "row_scan",
        [array((line, rows, share)), array((2, line, share))],
        scan_scratch(line, rows, share, width, state)
        + [
            pltpu.VMEM((line, rows, share), F32),
            pltpu.VMEM((line, rows, width), F32),
            pltpu.VMEM((line, rows, share), F32),
            pltpu.VMEM((line * rows, share), F32),
        ],
        got.reshape(line, rows, 2 * share + width),
        w_dt_row,
        dt_bias_row,
        rate_row,
        skip_row.reshape(1, share),
    )
    above = lax.ppermute(tail, "row", [(i, i + 1) for i in range(n_row - 1)])
    sent = call(
        conv_kernel,
        "conv",
        array((n_col, more, share)),
        [pltpu.VMEM((line + 2, rows + 8, share), F32), pltpu.VMEM((2, line + 16, share), F32)],
        gated,
        above,
        conv_taps,
        conv_bias.reshape(1, share),
    )
    got = lax.all_to_all(sent, "col", 0, 0, tiled=True)
    me = lax.axis_index("row").astype(jnp.int32).reshape(1)
    pieces = call(
        functools.partial(turn_kernel, rows=rows),
        "turn",
        [array((more, col_share + width))] * n_row,
        [],
        me,
        got,
        w_col_proj,
        scalars=1,
    )
    pieces = [pieces[0]] + [
        lax.ppermute(pieces[s], "row", [(i, (i + s) % n_row) for i in range(n_row)]) for s in range(1, n_row)
    ]
    return call(
        functools.partial(col_kernel, count=n_row, rows=rows),
        "col_scan",
        array((column, cols, col_share)),
        scan_scratch(column, cols, col_share, width, state)
        + [
            pltpu.VMEM(((column + 1) * cols, col_share + width), BF16),
            pltpu.VMEM((column, cols, col_share), F32),
            pltpu.VMEM((column, cols, width), F32),
            pltpu.VMEM((column, cols, col_share), F32),
        ],
        me,
        *pieces,
        w_dt_col,
        dt_bias_col,
        rate_col,
        scalars=1,
    )


def solution(mesh):
    return jax.shard_map(
        local,
        mesh=mesh,
        in_specs=(
            P("row", "col", None),
            P("row", "col", None),
            P(),
            P(None, None, "col"),
            P(None, "col"),
            P(None, "col", None),
            P("col"),
            P(None, None, "col"),
            P("col"),
            P(),
            P(None, None, "row"),
            P(None, "row"),
            P(None, "row", None),
        ),
        out_specs=P(None, "col", "row"),
        check_vma=False,
    )
```

time: 239 us -> 65.7 us (0.27); the launches traced: 236 us -> 65.3 us
  local copies, waits for them, and re-layouts: 92.6 us -> 4.25 us
  other arithmetic: 82.7 us -> 0 us
  Pallas kernels: 0 us -> 25.2 us
  blocking collectives: 23.6 us -> 0 us
  waiting for transfers between devices: 9.97 us -> 17.5 us
  starting transfers between devices: 22.1 us -> 18.3 us
  loops' own time: 2.67 us -> 0 us
    reduce_sum x48 -> x0, other arithmetic: 52.3 us -> none  [the longest x24 36.1 us: advance(): gathered = jnp.sum(decay_pairs * drives[None], axis=1)]
    pallas_call x0 -> x5, Pallas kernels: none -> 25.2 us  [call(): pl.pallas_call(kernel, name=name, out_shape=outs, in_specs=[smem()] * sca...]
    all_gather x2 -> x0, blocking collectives: 23.6 us -> none  [the longest x1 13.9 us: local(): column_proj = lax.all_gather(tile_colproj, 'row', axis=0, tiled=True)]
    broadcast_in_dim x72 -> x0, local copies, waits for them, and re-layouts: 20.4 us -> none  [widen(): return jnp.repeat(jnp.swapaxes(member, 1, 2), channels, axis=2)]
    unnamed x40 -> x18, local copies, waits for them, and re-layouts: 24.3 us -> 4.25 us
    transpose x74 -> x0, local copies, waits for them, and re-layouts: 19.5 us -> none  [the longest x72 19.5 us: widen(): return jnp.repeat(jnp.swapaxes(member, 1, 2), channels, axis=2)]
    mul x48 -> x0, other arithmetic: 17.5 us -> none  [advance(): drives = (step_blk * value_blk)[:, None, :] * widen(drive_blk)]
    all_to_all x4 -> x2, starting transfers between devices: 17.3 us -> 8.71 us  [local(): got = lax.all_to_all(sent, 'col', 0, 0, tiled=True)]
  transfers between devices with their start and end apart: 6 -> 6, of which waited for: 3 -> 6; matrix products, arithmetic and copies ran while one was open for 34% -> 2% of each run, Pallas kernels for 0% -> 0%
where the time goes in v1:
time: 65.7 us; the launch traced here: 65.3 us
  Pallas kernels  25.2 us (38%)
  starting transfers between devices  18.3 us (28%)
  waiting for transfers between devices  17.5 us (27%)
  local copies, waits for them, and re-layouts  4.25 us (6%)
    pallas_call x5, Pallas kernels, call(): pl.pallas_call(kernel, name=name, out_shape=outs, in_specs=[smem()] * sca...  25.2 us
    all_to_all x2, waiting for transfers between devices, local(): got = lax.all_to_all(sent, 'col', 0, 0, tiled=True)  13.2 us
    all_to_all x2, starting transfers between devices, local(): got = lax.all_to_all(sent, 'col', 0, 0, tiled=True)  8.71 us
    ppermute x3, starting transfers between devices, local(): lax.ppermute(pieces[s], 'row', [(i, (i + s) % n_row) for i in range(n_row)])  6.15 us
    unnamed x18, local copies, waits for them, and re-layouts  4.25 us
    ppermute x1, starting transfers between devices, local(): above = lax.ppermute(tail, 'row', [(i, i + 1) for i in range(n_row - 1)])  3.47 us
    ppermute x3, waiting for transfers between devices, local(): lax.ppermute(pieces[s], 'row', [(i, (i + s) % n_row) for i in range(n_row)])  2.41 us
    ppermute x1, waiting for transfers between devices, local(): above = lax.ppermute(tail, 'row', [(i, i + 1) for i in range(n_row - 1)])  1.89 us
  transfers between devices with their start and end apart: 6, of which 6 were waited for; matrix products, arithmetic and copies ran while one was open for 2% of the time, Pallas kernels for 0%

profile of v1, /device:TPU:0, one launch (start us, length us, event | category | flops | bytes accessed | tf_op | source)
XLA Modules:
  0.0 65.3 jit_solution(1919135127524414874)
XLA Ops:
  0.0 2.2 %pack.1 = bf16[8,64,384]{2,1,0:T(8,128)(2,1)} custom-call(bf16[8,8,1024]{2,1,0:T(8,128)(2,1)} %feat_ref.1, bf16[8,8,1024]{2,1,0:T(8,128)(2,1)} %gate_ref.1, bf16[1024,128]{1,0:T(8,128)(2,1)} %w_ref.2), custom_call_target="tpu_custom_call" | custom-call | tf_op jit(solution)/shard_map/pack/pallas_call | solution.py:204
  2.2 5.3 %all-to-all-start = ((bf16[8,64,384]{2,1,0:T(8,128)(2,1)}), bf16[8,64,384]{2,1,0:T(8,128)(2,1)S(1)}, u32[]{:S(2)}, u32[]{:S(2)}) async-start(bf16[8,64,384]{2,1,0:T(8,128)(2,1)} %pack.1), calls=%async_computation | async-start | bytes 786432 | tf_op jit(solution)/shard_map/all_to_all | solution.py:240
  7.5 0.8 %copy.14.rate_ref = f32[2,128,16]{2,1,0:T(8,128)} copy(f32[2,128,16]{1,2,0:T(8,128)S(1)} %copy-done.7) | data formatting | bytes 32768 | tf_op args[5]
  8.2 7.5 %all-to-all-done = bf16[8,64,384]{2,1,0:T(8,128)(2,1)S(1)} async-done(((bf16[8,64,384]{2,1,0:T(8,128)(2,1)}), bf16[8,64,384]{2,1,0:T(8,128)(2,1)S(1)}, u32[]{:S(2)}, u32[]{:S(2)}) %all-to-all-start) | async-done | bytes 393248 | tf_op jit(solution)/shard_map/all_to_all | solution.py:240
  15.8 0.8 %copy-done = bf16[8,64,384]{2,1,0:T(8,128)(2,1)} copy-done((bf16[8,64,384]{2,1,0:T(8,128)(2,1)}, bf16[8,64,384]{2,1,0:T(8,128)(2,1)S(1)}, u32[]{:S(2)}) %copy-start) | copy-done | bytes 393240
  16.6 11.7 %row_scan.1 = (bf16[64,8,128]{2,1,0:T(8,128)(2,1)}, bf16[2,64,128]{2,1,0:T(8,128)(2,1)}) custom-call(bf16[64,8,384]{2,1,0:T(8,128)(2,1)} %bitcast.4, bf16[2,32,128]{2,1,0:T(8,128)(2,1)} %w_dt_ref.1, f32[2,128]{1,0:T(2,128)} %bias_ref.1, f32[2,128,16]{2,1,0:T(8,128)} %copy.14.rate_ref, f32[1,128]{1,0:T(1,128)} %bitcast.5), custom_call_target="tpu_custom_call" | custom-call | tf_op jit(solution)/shard_map/row_scan/pallas_call | solution.py:204
  28.2 3.5 %collective-permute-start = (bf16[2,64,128]{2,1,0:T(8,128)(2,1)}, bf16[2,64,128]{2,1,0:T(8,128)(2,1)S(1)}, u32[]{:S(2)}, u32[]{:S(2)}) collective-permute-start(bf16[2,64,128]{2,1,0:T(8,128)(2,1)} %get-tuple-element.12), channel_id=1, source_target_pairs={{0,8},{8,16},{16,24},{1,9},{9,17},{17,25},{2,10},{10,18},{18,26},{... | collective-permute-start | bytes 98312 | tf_op jit(solution)/shard_map/ppermute | solution.py:258
  31.7 1.9 %collective-permute-done.above_ref = bf16[2,64,128]{2,1,0:T(8,128)(2,1)S(1)} collective-permute-done((bf16[2,64,128]{2,1,0:T(8,128)(2,1)}, bf16[2,64,128]{2,1,0:T(8,128)(2,1)S(1)}, u32[]{:S(2)}, u32[]{:S(2)}) %collective-permute-start) | collective-permute-done | bytes 32800 | tf_op jit(solution)/shard_map/ppermute | solution.py:258
  33.6 0.6 copy-done.6
  34.2 2.1 %conv.1 = bf16[8,72,128]{2,1,0:T(8,128)(2,1)} custom-call(bf16[64,8,128]{2,1,0:T(8,128)(2,1)} %get-tuple-element.11.mid_ref, bf16[2,64,128]{2,1,0:T(8,128)(2,1)} %copy-done.6, f32[3,3,128]{2,1,0:T(4,128)} %taps_ref.1, f32[1,128]{1,0:T(1,128)} %bitcast.6), custom_call_target="tpu_custom_call" | custom-call | tf_op jit(solution)/shard_map/conv/pallas_call | solution.py:204
  36.3 3.4 %all-to-all-start.1 = ((bf16[8,72,128]{2,1,0:T(8,128)(2,1)}), bf16[8,72,128]{2,1,0:T(8,128)(2,1)S(1)}, u32[]{:S(2)}, u32[]{:S(2)}) async-start(bf16[8,72,128]{2,1,0:T(8,128)(2,1)} %conv.1), calls=%async_computation.1 | async-start | bytes 294912 | tf_op jit(solution)/shard_map/all_to_all | solution.py:269
  39.7 5.6 %all-to-all-done.1.got_ref = bf16[8,72,128]{2,1,0:T(8,128)(2,1)S(1)} async-done(((bf16[8,72,128]{2,1,0:T(8,128)(2,1)}), bf16[8,72,128]{2,1,0:T(8,128)(2,1)S(1)}, u32[]{:S(2)}, u32[]{:S(2)}) %all-to-all-start.1) | async-done | bytes 147488 | tf_op jit(solution)/shard_map/all_to_all | solution.py:269
  45.3 0.7 %copy-done.1 = bf16[8,72,128]{2,1,0:T(8,128)(2,1)} copy-done((bf16[8,72,128]{2,1,0:T(8,128)(2,1)}, bf16[8,72,128]{2,1,0:T(8,128)(2,1)S(1)}, u32[]{:S(2)}) %copy-start.1) | copy-done | bytes 147480
  45.9 2.3 %turn.1 = (bf16[72,384]{1,0:T(8,128)(2,1)}, bf16[72,384]{1,0:T(8,128)(2,1)}, bf16[72,384]{1,0:T(8,128)(2,1)}, bf16[72,384]{1,0:T(8,128)(2,1)}) custom-call(s32[1]{0:T(128)} %bitcast.me_ref, bf16[8,72,128]{2,1,0:T(8,128)(2,1)} %copy-done.1, bf16[1024,128]{1,0:T(8,128)(2,1)} %w_ref.3), custom_call_target="tpu_custom_call" | custom-call | tf_op jit(solution)/shard_map/turn/pallas_call | solution.py:204
  48.2 2.2 %collective-permute-start.1 = (bf16[72,384]{1,0:T(8,128)(2,1)}, bf16[72,384]{1,0:T(8,128)(2,1)S(1)}, u32[]{:S(2)}, u32[]{:S(2)}) collective-permute-start(bf16[72,384]{1,0:T(8,128)(2,1)} %get-tuple-element.14), channel_id=1, source_target_pairs={{0,8},{8,16},{16,24},{24,0},{1,9},{9,17},{17,25},{25,1},{2,10},{10... | collective-permute-start | bytes 165896 | tf_op jit(solution)/shard_map/ppermute | solution.py:282
  50.4 2.6 %collective-permute-start.2 = (bf16[72,384]{1,0:T(8,128)(2,1)}, bf16[72,384]{1,0:T(8,128)(2,1)S(1)}, u32[]{:S(2)}, u32[]{:S(2)}) collective-permute-start(bf16[72,384]{1,0:T(8,128)(2,1)} %get-tuple-element.15), channel_id=1, source_target_pairs={{0,16},{8,24},{16,0},{24,8},{1,17},{9,25},{17,1},{25,9},{2,18},{10... | collective-permute-start | bytes 165896 | tf_op jit(solution)/shard_map/ppermute | solution.py:282
  53.0 1.3 %collective-permute-start.3 = (bf16[72,384]{1,0:T(8,128)(2,1)}, bf16[72,384]{1,0:T(8,128)(2,1)S(1)}, u32[]{:S(2)}, u32[]{:S(2)}) collective-permute-start(bf16[72,384]{1,0:T(8,128)(2,1)} %get-tuple-element.16), channel_id=1, source_target_pairs={{0,24},{8,0},{16,8},{24,16},{1,25},{9,1},{17,9},{25,17},{2,26},{10... | collective-permute-start | bytes 165896 | tf_op jit(solution)/shard_map/ppermute | solution.py:282
  54.4 0.8 %copy.15.refs_6_ = f32[2,256,16]{2,1,0:T(8,128)} copy(f32[2,256,16]{1,2,0:T(8,128)S(1)} %copy-done.5) | data formatting | bytes 65536 | tf_op args[12]
  55.2 0.1 collective-permute-done.1.refs_1_
  55.3 2.0 %collective-permute-done.2.refs_2_ = bf16[72,384]{1,0:T(8,128)(2,1)S(1)} collective-permute-done((bf16[72,384]{1,0:T(8,128)(2,1)}, bf16[72,384]{1,0:T(8,128)(2,1)S(1)}, u32[]{:S(2)}, u32[]{:S(2)}) %collective-permute-start.2) | collective-permute-done | bytes 55328 | tf_op jit(solution)/shard_map/ppermute | solution.py:282
  57.3 0.3 collective-permute-done.3.refs_3_
  57.6 0.3 copy-done.3
  57.9 0.3 copy-done.4
  58.2 7.0 %col_scan.1 = bf16[32,8,256]{2,1,0:T(8,128)(2,1)} custom-call(s32[1]{0:T(128)} %bitcast.me_ref, bf16[72,384]{1,0:T(8,128)(2,1)} %get-tuple-element.13.refs_0_, bf16[72,384]{1,0:T(8,128)(2,1)} %copy-done.2, bf16[72,384]{1,0:T(8,128)(2,1)} %copy-done.3, bf16[72,384]{1,0:T(8,128)(2,1)} %copy-done.4, bf16[2,32,256]{2,1,0:T(8,128)(2,1)} %refs_4_.1, ...), custom_call_target="tpu_custom_call" | custom-call | tf_op jit(solution)/shard_map/col_scan/pallas_call | solution.py:204
  (11 shorter events, 0.0 us)
Async XLA Ops:
  2.2 5.3 %copy-start.7 = (f32[2,128,16]{1,2,0:T(8,128)S(1)}, f32[2,128,16]{1,2,0:T(8,128)}, u32[]{:S(2)}) copy-start(f32[2,128,16]{1,2,0:T(8,128)} %param.18) | copy-start | bytes 49156
  2.2 13.6 %all-to-all-start = ((bf16[8,64,384]{2,1,0:T(8,128)(2,1)}), bf16[8,64,384]{2,1,0:T(8,128)(2,1)S(1)}, u32[]{:S(2)}, u32[]{:S(2)}) async-start(bf16[8,64,384]{2,1,0:T(8,128)(2,1)} %pack.1), calls=%async_computation | async-start | bytes 786432 | tf_op jit(solution)/shard_map/all_to_all | solution.py:240
  15.8 0.8 %copy-start = (bf16[8,64,384]{2,1,0:T(8,128)(2,1)}, bf16[8,64,384]{2,1,0:T(8,128)(2,1)S(1)}, u32[]{:S(2)}) copy-start(bf16[8,64,384]{2,1,0:T(8,128)(2,1)S(1)} %all-to-all-done) | copy-start | bytes 1179652
  28.2 5.4 %collective-permute-start = (bf16[2,64,128]{2,1,0:T(8,128)(2,1)}, bf16[2,64,128]{2,1,0:T(8,128)(2,1)S(1)}, u32[]{:S(2)}, u32[]{:S(2)}) collective-permute-start(bf16[2,64,128]{2,1,0:T(8,128)(2,1)} %get-tuple-element.12), channel_id=1, source_target_pairs={{0,8},{8,16},{16,24},{1,9},{9,17},{17,25},{2,10},{10,18},{18,26},{... | collective-permute-start | bytes 98312 | tf_op jit(solution)/shard_map/ppermute | solution.py:258
  33.6 0.6 copy-start.6
  36.3 9.0 %all-to-all-start.1 = ((bf16[8,72,128]{2,1,0:T(8,128)(2,1)}), bf16[8,72,128]{2,1,0:T(8,128)(2,1)S(1)}, u32[]{:S(2)}, u32[]{:S(2)}) async-start(bf16[8,72,128]{2,1,0:T(8,128)(2,1)} %conv.1), calls=%async_computation.1 | async-start | bytes 294912 | tf_op jit(solution)/shard_map/all_to_all | solution.py:269
  45.3 0.7 %copy-start.1 = (bf16[8,72,128]{2,1,0:T(8,128)(2,1)}, bf16[8,72,128]{2,1,0:T(8,128)(2,1)S(1)}, u32[]{:S(2)}) copy-start(bf16[8,72,128]{2,1,0:T(8,128)(2,1)S(1)} %all-to-all-done.1.got_ref) | copy-start | bytes 442372
  45.9 8.4 %copy-start.5 = (f32[2,256,16]{1,2,0:T(8,128)S(1)}, f32[2,256,16]{1,2,0:T(8,128)}, u32[]{:S(2)}) copy-start(f32[2,256,16]{1,2,0:T(8,128)} %param.25) | copy-start | bytes 98308
  48.2 7.1 %collective-permute-start.1 = (bf16[72,384]{1,0:T(8,128)(2,1)}, bf16[72,384]{1,0:T(8,128)(2,1)S(1)}, u32[]{:S(2)}, u32[]{:S(2)}) collective-permute-start(bf16[72,384]{1,0:T(8,128)(2,1)} %get-tuple-element.14), channel_id=1, source_target_pairs={{0,8},{8,16},{16,24},{24,0},{1,9},{9,17},{17,25},{25,1},{2,10},{10... | collective-permute-start | bytes 165896 | tf_op jit(solution)/shard_map/ppermute | solution.py:282
  50.4 6.9 %collective-permute-start.2 = (bf16[72,384]{1,0:T(8,128)(2,1)}, bf16[72,384]{1,0:T(8,128)(2,1)S(1)}, u32[]{:S(2)}, u32[]{:S(2)}) collective-permute-start(bf16[72,384]{1,0:T(8,128)(2,1)} %get-tuple-element.15), channel_id=1, source_target_pairs={{0,16},{8,24},{16,0},{24,8},{1,17},{9,25},{17,1},{25,9},{2,18},{10... | collective-permute-start | bytes 165896 | tf_op jit(solution)/shard_map/ppermute | solution.py:282
  53.0 4.6 %collective-permute-start.3 = (bf16[72,384]{1,0:T(8,128)(2,1)}, bf16[72,384]{1,0:T(8,128)(2,1)S(1)}, u32[]{:S(2)}, u32[]{:S(2)}) collective-permute-start(bf16[72,384]{1,0:T(8,128)(2,1)} %get-tuple-element.16), channel_id=1, source_target_pairs={{0,24},{8,0},{16,8},{24,16},{1,25},{9,1},{17,9},{25,17},{2,26},{10... | collective-permute-start | bytes 165896 | tf_op jit(solution)/shard_map/ppermute | solution.py:282
  55.3 2.3 %copy-start.2 = (bf16[72,384]{1,0:T(8,128)(2,1)}, bf16[72,384]{1,0:T(8,128)(2,1)S(1)}, u32[]{:S(2)}) copy-start(bf16[72,384]{1,0:T(8,128)(2,1)S(1)} %collective-permute-done.1.refs_1_) | copy-start | bytes 165892
  57.3 0.6 copy-start.3
  57.6 0.6 copy-start.4

commit v2 on v1

--- a/solution.py
+++ b/solution.py
@@ -53,9 +53,15 @@
         out_ref[part, :, 2 * share :] = proj
 
 
-def prepare(proj, w_dt_ref, bias_ref, rate_ref, wide_ref, step_ref, rates_ref):
+def one_hot(height, width, hit):
+    row = lax.broadcasted_iota(jnp.int32, (height, width), 0)
+    column = lax.broadcasted_iota(jnp.int32, (height, width), 1)
+    return jnp.where(hit(row, column), 1.0, 0.0).astype(BF16)
+
+
+def prepare(proj, w_dt_ref, bias_ref, rate_ref, wide_ref, step_ref, rates_ref, pick_ref, ends_ref):
     _, rank, channels = w_dt_ref.shape
-    state = rate_ref.shape[2]
+    state = rate_ref.shape[1]
     segment = rank + 2 * state
     lines = rates_ref.shape[2]
     wide_ref[...] = jnp.zeros_like(wide_ref)
@@ -65,51 +71,64 @@
     for k in range(2):
         part = raw[:, k * channels : (k + 1) * channels] + bias_ref[k : k + 1, :]
         step_ref[k] = softplus(part).reshape(step_ref.shape[1:])
-        turned = jnp.transpose(rate_ref[k] * -LOG2E)
+        turned = rate_ref[k] * -LOG2E
         for n in range(state):
             rates_ref[k, n] = jnp.broadcast_to(turned[n : n + 1, :], (lines, channels))
-
-
-def scan(k, rank, step_ref, value_ref, proj_ref, rates_ref, out_ref, unroll):
+        base = k * segment + rank
+        ends_ref[k] = dot(proj, one_hot(proj.shape[1], 2 * state, lambda r, c: r == c + base)).astype(BF16)
+    for n in range(state):
+        pick_ref[n] = one_hot(2 * state, 2 * LANES, lambda r, c: r == n + jnp.where(c < LANES, 0, state))
+
+
+def scan(k, step_ref, value_ref, rates_ref, pick_ref, ends_ref, state_ref, out_ref):
     positions, lines, channels = out_ref.shape
     state = rates_ref.shape[1]
-    base = k * (rank + 2 * state) + rank
-
-    def advance(at, carried):
-        pos = at if k == 0 else positions - 1 - at
-        step = step_ref[k, pos]
-        drive = step * value_ref[pos]
-        proj = proj_ref[pos]
-        total = out_ref[pos]
-        states = []
+    width = min(channels, LANES)
+    groups = [pl.ds(at, width) for at in range(0, channels, width)]
+    size = math.gcd(positions, max(1, 64 // (lines * len(groups))))
+    state_ref[...] = jnp.zeros_like(state_ref)
+
+    def advance(at, _):
+        first = at * size if k == 0 else positions - (at + 1) * size
+        first = pl.multiple_of(first, size)
+        order = list(range(size)) if k == 0 else list(reversed(range(size)))
+        steps = [[step_ref[k, first + p, :, g] for g in groups] for p in range(size)]
+        drives = [[steps[p][i] * value_ref[first + p, :, g] for i, g in enumerate(groups)] for p in range(size)]
+        totals = [[out_ref[first + p, :, g] for g in groups] for p in range(size)]
+        ends = ends_ref[k, pl.ds(pl.multiple_of(first * lines, size * lines), size * lines), :]
         for n in range(state):
-            b = jnp.broadcast_to(proj[:, base + n : base + n + 1], (lines, channels))
-            c = jnp.broadcast_to(proj[:, base + state + n : base + state + n + 1], (lines, channels))
-            s = jnp.exp2(step * rates_ref[k, n]) * carried[n] + drive * b
-            states.append(s)
-            total = total + c * s
-        out_ref[pos] = total
-        return tuple(states)
-
-    zero = jnp.zeros((lines, channels), F32)
-    lax.fori_loop(0, positions, advance, (zero,) * state, unroll=unroll)
+            rates = [rates_ref[k, n, :, g] for g in groups]
+            held = [state_ref[n, :, g] for g in groups]
+            spread = dot(ends, pick_ref[n])
+            for p in order:
+                b = spread[p * lines : (p + 1) * lines, :width]
+                c = spread[p * lines : (p + 1) * lines, LANES : LANES + width]
+                for i in range(len(groups)):
+                    held[i] = jnp.exp2(steps[p][i] * rates[i]) * held[i] + drives[p][i] * b
+                    totals[p][i] = totals[p][i] + c * held[i]
+            for i, g in enumerate(groups):
+                state_ref[n, :, g] = held[i]
+        for p in range(size):
+            for i, g in enumerate(groups):
+                out_ref[first + p, :, g] = totals[p][i]
+        return 0
+
+    lax.fori_loop(0, positions // size, advance, 0)
 
 
 def row_kernel(
     got_ref, w_dt_ref, bias_ref, rate_ref, skip_ref, out_ref, tail_ref,
-    wide_ref, step_ref, rates_ref, value_ref, proj_ref, sum_ref, flat_ref,
+    wide_ref, step_ref, rates_ref, pick_ref, ends_ref, state_ref, value_ref, sum_ref, flat_ref,
 ):
     positions, lines, share = out_ref.shape
-    rank = w_dt_ref.shape[1]
     width = got_ref.shape[2] - 2 * share
     proj = got_ref[:, :, 2 * share :].reshape(positions * lines, width)
-    prepare(proj, w_dt_ref, bias_ref, rate_ref, wide_ref, step_ref, rates_ref)
-    proj_ref[...] = proj.astype(F32).reshape(proj_ref.shape)
+    prepare(proj, w_dt_ref, bias_ref, rate_ref, wide_ref, step_ref, rates_ref, pick_ref, ends_ref)
     values = got_ref[:, :, :share].astype(F32)
     value_ref[...] = values
     sum_ref[...] = values * skip_ref[...]
     for k in range(2):
-        scan(k, rank, step_ref, value_ref, proj_ref, rates_ref, sum_ref, 4)
+        scan(k, step_ref, value_ref, rates_ref, pick_ref, ends_ref, state_ref, sum_ref)
     gated = sum_ref[...] * silu(got_ref[:, :, share : 2 * share].astype(F32))
     out_ref[...] = gated.astype(BF16)
     flat_ref[...] = gated.reshape(flat_ref.shape)
@@ -167,9 +186,8 @@
 
 def col_kernel(me_ref, *refs, count, rows):
     got_refs = refs[:count]
-    (w_dt_ref, bias_ref, rate_ref, out_ref, wide_ref, step_ref, rates_ref, all_ref, value_ref, proj_ref, sum_ref) = refs[count:]
+    (w_dt_ref, bias_ref, rate_ref, out_ref, wide_ref, step_ref, rates_ref, pick_ref, ends_ref, state_ref, all_ref, value_ref, sum_ref) = refs[count:]
     positions, lines, share = out_ref.shape
-    rank = w_dt_ref.shape[1]
     block = rows * lines
     me = me_ref[0]
     for shift in range(count):
@@ -182,12 +200,11 @@
 
     everything = all_ref[lines:, :]
     proj = everything[:, share:]
-    prepare(proj, w_dt_ref, bias_ref, rate_ref, wide_ref, step_ref, rates_ref)
-    proj_ref[...] = proj.astype(F32).reshape(proj_ref.shape)
+    prepare(proj, w_dt_ref, bias_ref, rate_ref, wide_ref, step_ref, rates_ref, pick_ref, ends_ref)
     value_ref[...] = everything[:, :share].astype(F32).reshape(value_ref.shape)
     sum_ref[...] = jnp.zeros_like(sum_ref)
     for k in range(2):
-        scan(k, rank, step_ref, value_ref, proj_ref, rates_ref, sum_ref, 4)
+        scan(k, step_ref, value_ref, rates_ref, pick_ref, ends_ref, state_ref, sum_ref)
     out_ref[...] = sum_ref[...].astype(BF16)
 
 
@@ -213,7 +230,11 @@
 
 
 def array(shape, dtype=BF16):
-    return jax.ShapeDtypeStruct(shape, dtype)
+    return pltpu.VMEM(shape, dtype)
+
+
+def near(x):
+    return pltpu.with_memory_space_constraint(x, pltpu.VMEM)
 
 
 def scan_scratch(positions, lines, channels, width, state):
@@ -221,6 +242,9 @@
         pltpu.VMEM((width, 2 * channels), BF16),
         pltpu.VMEM((2, positions, lines, channels), F32),
         pltpu.VMEM((2, state, lines, channels), F32),
+        pltpu.VMEM((state, 2 * state, 2 * LANES), BF16),
+        pltpu.VMEM((2, positions * lines, 2 * state), BF16),
+        pltpu.VMEM((state, lines, channels), F32),
     ]
 
 
@@ -245,14 +269,13 @@
         scan_scratch(line, rows, share, width, state)
         + [
             pltpu.VMEM((line, rows, share), F32),
-            pltpu.VMEM((line, rows, width), F32),
             pltpu.VMEM((line, rows, share), F32),
             pltpu.VMEM((line * rows, share), F32),
         ],
-        got.reshape(line, rows, 2 * share + width),
+        near(got.reshape(line, rows, 2 * share + width)),
         w_dt_row,
         dt_bias_row,
-        rate_row,
+        jnp.swapaxes(rate_row, 1, 2),
         skip_row.reshape(1, share),
     )
     above = lax.ppermute(tail, "row", [(i, i + 1) for i in range(n_row - 1)])
@@ -261,8 +284,8 @@
         "conv",
         array((n_col, more, share)),
         [pltpu.VMEM((line + 2, rows + 8, share), F32), pltpu.VMEM((2, line + 16, share), F32)],
-        gated,
-        above,
+        near(gated),
+        near(above),
         conv_taps,
         conv_bias.reshape(1, share),
     )
@@ -274,7 +297,7 @@
         [array((more, col_share + width))] * n_row,
         [],
         me,
-        got,
+        near(got),
         w_col_proj,
         scalars=1,
     )
@@ -284,19 +307,18 @@
     return call(
         functools.partial(col_kernel, count=n_row, rows=rows),
         "col_scan",
-        array((column, cols, col_share)),
+        jax.ShapeDtypeStruct((column, cols, col_share), BF16),
         scan_scratch(column, cols, col_share, width, state)
         + [
             pltpu.VMEM(((column + 1) * cols, col_share + width), BF16),
             pltpu.VMEM((column, cols, col_share), F32),
-            pltpu.VMEM((column, cols, width), F32),
             pltpu.VMEM((column, cols, col_share), F32),
         ],
         me,
-        *pieces,
+        *[near(piece) for piece in pieces],
         w_dt_col,
         dt_bias_col,
-        rate_col,
+        jnp.swapaxes(rate_col, 1, 2),
         scalars=1,
     )
 

time: 65.7 us -> 53.6 us (0.82)
  blocking collectives: 0 us -> 13.3 us
  Pallas kernels: 25.2 us -> 16.4 us
  waiting for transfers between devices: 17.5 us -> 10.2 us
  starting transfers between devices: 18.3 us -> 13.2 us
  local copies, waits for them, and re-layouts: 4.25 us -> 0 us
    all_to_all x0 -> x1, blocking collectives: none -> 13.3 us  [local(): got = lax.all_to_all(sent, 'col', 0, 0, tiled=True)]
    pallas_call x5, Pallas kernels: 25.2 us -> 16.4 us  [call(): pl.pallas_call(kernel, name=name, out_shape=outs, in_specs=[smem()] * sca...]
    all_to_all x2 -> x1, waiting for transfers between devices: 13.2 us -> 5.61 us  [local(): got = lax.all_to_all(sent, 'col', 0, 0, tiled=True)]
    all_to_all x2 -> x1, starting transfers between devices: 8.71 us -> 3.38 us  [local(): got = lax.all_to_all(sent, 'col', 0, 0, tiled=True)]
    unnamed x18 -> x0, local copies, waits for them, and re-layouts: 4.25 us -> none
  transfers between devices with their start and end apart: 6 -> 5, of which waited for: 6 -> 5; matrix products, arithmetic and copies ran while one was open for 2% -> 0% of each run, Pallas kernels for 0% -> 0%
where the time goes in v2:
time: 53.6 us; the launch traced here: 53.1 us
  Pallas kernels  16.4 us (31%)
  blocking collectives  13.3 us (25%)
  starting transfers between devices  13.2 us (25%)
  waiting for transfers between devices  10.2 us (19%)
    pallas_call x5, Pallas kernels, call(): pl.pallas_call(kernel, name=name, out_shape=outs, in_specs=[smem()] * sca...  16.4 us
    all_to_all x1, blocking collectives, local(): got = lax.all_to_all(sent, 'col', 0, 0, tiled=True)  13.3 us
    ppermute x3, starting transfers between devices, local(): lax.ppermute(pieces[s], 'row', [(i, (i + s) % n_row) for i in range(n_row)])  6.31 us
    all_to_all x1, waiting for transfers between devices, local(): got = lax.all_to_all(sent, 'col', 0, 0, tiled=True)  5.61 us
    ppermute x1, starting transfers between devices, local(): above = lax.ppermute(tail, 'row', [(i, i + 1) for i in range(n_row - 1)])  3.48 us
    all_to_all x1, starting transfers between devices, local(): got = lax.all_to_all(sent, 'col', 0, 0, tiled=True)  3.38 us
    ppermute x3, waiting for transfers between devices, local(): lax.ppermute(pieces[s], 'row', [(i, (i + s) % n_row) for i in range(n_row)])  3.03 us
    ppermute x1, waiting for transfers between devices, local(): above = lax.ppermute(tail, 'row', [(i, i + 1) for i in range(n_row - 1)])  1.58 us
  transfers between devices with their start and end apart: 5, of which 5 were waited for; matrix products, arithmetic and copies ran while one was open for 0% of the time, Pallas kernels for 0%

profile of v2, /device:TPU:0, one launch (start us, length us, event | category | flops | bytes accessed | tf_op | source)
XLA Modules:
  0.0 53.1 jit_solution(9868434976318182508)
XLA Ops:
  0.0 1.4 %pack.1 = bf16[8,64,384]{2,1,0:T(8,128)(2,1)S(1)} custom-call(bf16[8,8,1024]{2,1,0:T(8,128)(2,1)} %feat_ref.1, bf16[8,8,1024]{2,1,0:T(8,128)(2,1)} %gate_ref.1, bf16[1024,128]{1,0:T(8,128)(2,1)} %w_ref.2), custom_call_target="tpu_custom_call" | custom-call | tf_op jit(solution)/shard_map/pack/pallas_call | solution.py:221
  1.4 13.3 %all_to_all.10 = bf16[8,64,384]{2,1,0:T(8,128)(2,1)S(1)} all-to-all(bf16[8,64,384]{2,1,0:T(8,128)(2,1)S(1)} %pack.1), channel_id=1, replica_groups=mesh['row'=4,'col'=8] {'col'}, dimensions={0} | all-to-all | bytes 786432 | tf_op jit(solution)/shard_map/all_to_all | solution.py:264
  14.7 5.9 %row_scan.1 = (bf16[64,8,128]{2,1,0:T(8,128)(2,1)S(1)}, bf16[2,64,128]{2,1,0:T(8,128)(2,1)S(1)}) custom-call(bf16[64,8,384]{2,1,0:T(8,128)(2,1)S(1)} %bitcast.6, bf16[2,32,128]{2,1,0:T(8,128)(2,1)} %w_dt_ref.1, f32[2,128]{1,0:T(2,128)} %bias_ref.1, f32[2,16,128]{2,1,0:T(8,128)} %bitcast.8, f32[1,128]{1,0:T(1,128)} %bitcast.9), custom_call_target="tpu_custom_call" | custom-call | tf_op jit(solution)/shard_map/row_scan/pallas_call | solution.py:221
  20.6 3.5 %collective-permute-start = (bf16[2,64,128]{2,1,0:T(8,128)(2,1)S(1)}, bf16[2,64,128]{2,1,0:T(8,128)(2,1)S(1)}, u32[]{:S(2)}, u32[]{:S(2)}) collective-permute-start(bf16[2,64,128]{2,1,0:T(8,128)(2,1)S(1)} %get-tuple-element.12), channel_id=1, source_target_pairs={{0,8},{8,16},{16,24},{1,9},{9,17},{17,25},{2,10},{10,18},{18,26},{... | collective-permute-start | bytes 98312 | tf_op jit(solution)/shard_map/ppermute | solution.py:281
  24.1 1.6 %collective-permute-done.above_ref = bf16[2,64,128]{2,1,0:T(8,128)(2,1)S(1)} collective-permute-done((bf16[2,64,128]{2,1,0:T(8,128)(2,1)S(1)}, bf16[2,64,128]{2,1,0:T(8,128)(2,1)S(1)}, u32[]{:S(2)}, u32[]{:S(2)}) %collective-permute-start) | collective-permute-done | bytes 32800 | tf_op jit(solution)/shard_map/ppermute | solution.py:281
  25.7 1.8 %conv.1 = bf16[8,72,128]{2,1,0:T(8,128)(2,1)} custom-call(bf16[64,8,128]{2,1,0:T(8,128)(2,1)S(1)} %get-tuple-element.11.mid_ref, bf16[2,64,128]{2,1,0:T(8,128)(2,1)S(1)} %collective-permute-done.above_ref, f32[3,3,128]{2,1,0:T(4,128)} %taps_ref.1, f32[1,128]{1,0:T(1,128)} %bitcast.10), custom_call_target="tpu_custom_call" | custom-call | tf_op jit(solution)/shard_map/conv/pallas_call | solution.py:221
  27.5 3.4 %all-to-all-start.1 = ((bf16[8,72,128]{2,1,0:T(8,128)(2,1)}), bf16[8,72,128]{2,1,0:T(8,128)(2,1)S(1)}, u32[]{:S(2)}, u32[]{:S(2)}) async-start(bf16[8,72,128]{2,1,0:T(8,128)(2,1)} %conv.1), calls=%async_computation.1 | async-start | bytes 294912 | tf_op jit(solution)/shard_map/all_to_all | solution.py:292
  30.9 5.6 %all-to-all-done.1.got_ref = bf16[8,72,128]{2,1,0:T(8,128)(2,1)S(1)} async-done(((bf16[8,72,128]{2,1,0:T(8,128)(2,1)}), bf16[8,72,128]{2,1,0:T(8,128)(2,1)S(1)}, u32[]{:S(2)}, u32[]{:S(2)}) %all-to-all-start.1) | async-done | bytes 147488 | tf_op jit(solution)/shard_map/all_to_all | solution.py:292
  36.5 1.5 %turn.1 = (bf16[72,384]{1,0:T(8,128)(2,1)S(1)}, bf16[72,384]{1,0:T(8,128)(2,1)S(1)}, bf16[72,384]{1,0:T(8,128)(2,1)S(1)}, bf16[72,384]{1,0:T(8,128)(2,1)S(1)}) custom-call(s32[1]{0:T(128)} %bitcast.me_ref, bf16[8,72,128]{2,1,0:T(8,128)(2,1)S(1)} %all-to-all-done.1.got_ref, bf16[1024,128]{1,0:T(8,128)(2,1)} %w_ref.3), custom_call_target="tpu_custom_call" | custom-call | tf_op jit(solution)/shard_map/turn/pallas_call | solution.py:221
  38.0 2.4 %collective-permute-start.1 = (bf16[72,384]{1,0:T(8,128)(2,1)S(1)}, bf16[72,384]{1,0:T(8,128)(2,1)S(1)}, u32[]{:S(2)}, u32[]{:S(2)}) collective-permute-start(bf16[72,384]{1,0:T(8,128)(2,1)S(1)} %get-tuple-element.14), channel_id=1, source_target_pairs={{0,8},{8,16},{16,24},{24,0},{1,9},{9,17},{17,25},{25,1},{2,10},{10... | collective-permute-start | bytes 165896 | tf_op jit(solution)/shard_map/ppermute | solution.py:305
  40.4 2.6 %collective-permute-start.2 = (bf16[72,384]{1,0:T(8,128)(2,1)S(1)}, bf16[72,384]{1,0:T(8,128)(2,1)S(1)}, u32[]{:S(2)}, u32[]{:S(2)}) collective-permute-start(bf16[72,384]{1,0:T(8,128)(2,1)S(1)} %get-tuple-element.15), channel_id=1, source_target_pairs={{0,16},{8,24},{16,0},{24,8},{1,17},{9,25},{17,1},{25,9},{2,18},{10... | collective-permute-start | bytes 165896 | tf_op jit(solution)/shard_map/ppermute | solution.py:305
  43.0 1.3 %collective-permute-start.3 = (bf16[72,384]{1,0:T(8,128)(2,1)S(1)}, bf16[72,384]{1,0:T(8,128)(2,1)S(1)}, u32[]{:S(2)}, u32[]{:S(2)}) collective-permute-start(bf16[72,384]{1,0:T(8,128)(2,1)S(1)} %get-tuple-element.16), channel_id=1, source_target_pairs={{0,24},{8,0},{16,8},{24,16},{1,25},{9,1},{17,9},{25,17},{2,26},{10... | collective-permute-start | bytes 165896 | tf_op jit(solution)/shard_map/ppermute | solution.py:305
  44.3 0.7 %collective-permute-done.1.refs_1_ = bf16[72,384]{1,0:T(8,128)(2,1)S(1)} collective-permute-done((bf16[72,384]{1,0:T(8,128)(2,1)S(1)}, bf16[72,384]{1,0:T(8,128)(2,1)S(1)}, u32[]{:S(2)}, u32[]{:S(2)}) %collective-permute-start.1) | collective-permute-done | bytes 55328 | tf_op jit(solution)/shard_map/ppermute | solution.py:305
  45.1 2.0 %collective-permute-done.2.refs_2_ = bf16[72,384]{1,0:T(8,128)(2,1)S(1)} collective-permute-done((bf16[72,384]{1,0:T(8,128)(2,1)S(1)}, bf16[72,384]{1,0:T(8,128)(2,1)S(1)}, u32[]{:S(2)}, u32[]{:S(2)}) %collective-permute-start.2) | collective-permute-done | bytes 55328 | tf_op jit(solution)/shard_map/ppermute | solution.py:305
  47.1 0.3 collective-permute-done.3.refs_3_
  47.4 5.8 %col_scan.1 = bf16[32,8,256]{2,1,0:T(8,128)(2,1)} custom-call(s32[1]{0:T(128)} %bitcast.me_ref, bf16[72,384]{1,0:T(8,128)(2,1)S(1)} %get-tuple-element.13.refs_0_, bf16[72,384]{1,0:T(8,128)(2,1)S(1)} %collective-permute-done.1.refs_1_, bf16[72,384]{1,0:T(8,128)(2,1)S(1)} %collective-permute-done.2.refs_2_, ...), custom_call_target="tpu_custom_call" | custom-call | tf_op jit(solution)/shard_map/col_scan/pallas_call | solution.py:221
Async XLA Ops:
  20.6 5.1 %collective-permute-start = (bf16[2,64,128]{2,1,0:T(8,128)(2,1)S(1)}, bf16[2,64,128]{2,1,0:T(8,128)(2,1)S(1)}, u32[]{:S(2)}, u32[]{:S(2)}) collective-permute-start(bf16[2,64,128]{2,1,0:T(8,128)(2,1)S(1)} %get-tuple-element.12), channel_id=1, source_target_pairs={{0,8},{8,16},{16,24},{1,9},{9,17},{17,25},{2,10},{10,18},{18,26},{... | collective-permute-start | bytes 98312 | tf_op jit(solution)/shard_map/ppermute | solution.py:281
  27.5 9.0 %all-to-all-start.1 = ((bf16[8,72,128]{2,1,0:T(8,128)(2,1)}), bf16[8,72,128]{2,1,0:T(8,128)(2,1)S(1)}, u32[]{:S(2)}, u32[]{:S(2)}) async-start(bf16[8,72,128]{2,1,0:T(8,128)(2,1)} %conv.1), calls=%async_computation.1 | async-start | bytes 294912 | tf_op jit(solution)/shard_map/all_to_all | solution.py:292
  38.0 7.0 %collective-permute-start.1 = (bf16[72,384]{1,0:T(8,128)(2,1)S(1)}, bf16[72,384]{1,0:T(8,128)(2,1)S(1)}, u32[]{:S(2)}, u32[]{:S(2)}) collective-permute-start(bf16[72,384]{1,0:T(8,128)(2,1)S(1)} %get-tuple-element.14), channel_id=1, source_target_pairs={{0,8},{8,16},{16,24},{24,0},{1,9},{9,17},{17,25},{25,1},{2,10},{10... | collective-permute-start | bytes 165896 | tf_op jit(solution)/shard_map/ppermute | solution.py:305
  40.4 6.7 %collective-permute-start.2 = (bf16[72,384]{1,0:T(8,128)(2,1)S(1)}, bf16[72,384]{1,0:T(8,128)(2,1)S(1)}, u32[]{:S(2)}, u32[]{:S(2)}) collective-permute-start(bf16[72,384]{1,0:T(8,128)(2,1)S(1)} %get-tuple-element.15), channel_id=1, source_target_pairs={{0,16},{8,24},{16,0},{24,8},{1,17},{9,25},{17,1},{25,9},{2,18},{10... | collective-permute-start | bytes 165896 | tf_op jit(solution)/shard_map/ppermute | solution.py:305
  43.0 4.4 %collective-permute-start.3 = (bf16[72,384]{1,0:T(8,128)(2,1)S(1)}, bf16[72,384]{1,0:T(8,128)(2,1)S(1)}, u32[]{:S(2)}, u32[]{:S(2)}) collective-permute-start(bf16[72,384]{1,0:T(8,128)(2,1)S(1)} %get-tuple-element.16), channel_id=1, source_target_pairs={{0,24},{8,0},{16,8},{24,16},{1,25},{9,1},{17,9},{25,17},{2,26},{10... | collective-permute-start | bytes 165896 | tf_op jit(solution)/shard_map/ppermute | solution.py:305

commit v3 on v2

--- a/solution.py
+++ b/solution.py
@@ -80,88 +80,102 @@
         pick_ref[n] = one_hot(2 * state, 2 * LANES, lambda r, c: r == n + jnp.where(c < LANES, 0, state))
 
 
-def scan(k, step_ref, value_ref, rates_ref, pick_ref, ends_ref, state_ref, out_ref):
+def scan(step_ref, value_ref, rates_ref, pick_ref, ends_ref, state_ref, out_ref, back_ref):
     positions, lines, channels = out_ref.shape
     state = rates_ref.shape[1]
     width = min(channels, LANES)
     groups = [pl.ds(at, width) for at in range(0, channels, width)]
-    size = math.gcd(positions, max(1, 64 // (lines * len(groups))))
+    size = math.gcd(positions, max(1, 32 // (lines * len(groups))))
+    blocks = positions // size
     state_ref[...] = jnp.zeros_like(state_ref)
 
     def advance(at, _):
-        first = at * size if k == 0 else positions - (at + 1) * size
-        first = pl.multiple_of(first, size)
-        order = list(range(size)) if k == 0 else list(reversed(range(size)))
-        steps = [[step_ref[k, first + p, :, g] for g in groups] for p in range(size)]
-        drives = [[steps[p][i] * value_ref[first + p, :, g] for i, g in enumerate(groups)] for p in range(size)]
-        totals = [[out_ref[first + p, :, g] for g in groups] for p in range(size)]
-        ends = ends_ref[k, pl.ds(pl.multiple_of(first * lines, size * lines), size * lines), :]
+        firsts = (pl.multiple_of(at * size, size), pl.multiple_of((blocks - 1 - at) * size, size))
+        orders = (list(range(size)), list(reversed(range(size))))
+        steps, drives, ends = [], [], []
+        for k, first in enumerate(firsts):
+            steps.append([[step_ref[k, first + p, :, g] for g in groups] for p in range(size)])
+            drives.append([[steps[k][p][i] * value_ref[first + p, :, g] for i, g in enumerate(groups)] for p in range(size)])
+            ends.append(ends_ref[k, pl.ds(pl.multiple_of(first * lines, size * lines), size * lines), :])
+        totals = [[[None] * len(groups) for _ in range(size)] for _ in firsts]
+        both = jnp.concatenate(ends, axis=0)
         for n in range(state):
-            rates = [rates_ref[k, n, :, g] for g in groups]
-            held = [state_ref[n, :, g] for g in groups]
-            spread = dot(ends, pick_ref[n])
-            for p in order:
-                b = spread[p * lines : (p + 1) * lines, :width]
-                c = spread[p * lines : (p + 1) * lines, LANES : LANES + width]
-                for i in range(len(groups)):
-                    held[i] = jnp.exp2(steps[p][i] * rates[i]) * held[i] + drives[p][i] * b
-                    totals[p][i] = totals[p][i] + c * held[i]
-            for i, g in enumerate(groups):
-                state_ref[n, :, g] = held[i]
+            spread = dot(both, pick_ref[n])
+            held = [[state_ref[k, n, :, g] for g in groups] for k in range(2)]
+            rates = [[rates_ref[k, n, :, g] for g in groups] for k in range(2)]
+            for at_p in range(size):
+                for k in range(2):
+                    p = orders[k][at_p]
+                    row = (k * size + p) * lines
+                    b = spread[row : row + lines, :width]
+                    c = spread[row : row + lines, LANES : LANES + width]
+                    for i in range(len(groups)):
+                        held[k][i] = jnp.exp2(steps[k][p][i] * rates[k][i]) * held[k][i] + drives[k][p][i] * b
+                        read = c * held[k][i]
+                        totals[k][p][i] = read if n == 0 else totals[k][p][i] + read
+            for k in range(2):
+                for i, g in enumerate(groups):
+                    state_ref[k, n, :, g] = held[k][i]
         for p in range(size):
             for i, g in enumerate(groups):
-                out_ref[first + p, :, g] = totals[p][i]
+                out_ref[firsts[0] + p, :, g] = totals[0][p][i]
+                back_ref[firsts[1] + p, :, g] = totals[1][p][i]
         return 0
 
-    lax.fori_loop(0, positions // size, advance, 0)
+    lax.fori_loop(0, blocks, advance, 0, unroll=math.gcd(blocks, 4))
 
 
 def row_kernel(
     got_ref, w_dt_ref, bias_ref, rate_ref, skip_ref, out_ref, tail_ref,
-    wide_ref, step_ref, rates_ref, pick_ref, ends_ref, state_ref, value_ref, sum_ref, flat_ref,
+    wide_ref, step_ref, rates_ref, pick_ref, ends_ref, state_ref, value_ref, sum_ref, back_ref, flat_ref,
 ):
     positions, lines, share = out_ref.shape
     width = got_ref.shape[2] - 2 * share
     proj = got_ref[:, :, 2 * share :].reshape(positions * lines, width)
     prepare(proj, w_dt_ref, bias_ref, rate_ref, wide_ref, step_ref, rates_ref, pick_ref, ends_ref)
-    values = got_ref[:, :, :share].astype(F32)
-    value_ref[...] = values
-    sum_ref[...] = values * skip_ref[...]
-    for k in range(2):
-        scan(k, step_ref, value_ref, rates_ref, pick_ref, ends_ref, state_ref, sum_ref)
-    gated = sum_ref[...] * silu(got_ref[:, :, share : 2 * share].astype(F32))
+    value_ref[...] = got_ref[:, :, :share].astype(F32)
+    scan(step_ref, value_ref, rates_ref, pick_ref, ends_ref, state_ref, sum_ref, back_ref)
+    mix = sum_ref[...] + back_ref[...] + skip_ref[...] * value_ref[...]
+    gated = mix * silu(got_ref[:, :, share : 2 * share].astype(F32))
     out_ref[...] = gated.astype(BF16)
     flat_ref[...] = gated.reshape(flat_ref.shape)
     for j in range(2):
         tail_ref[j] = flat_ref[pl.ds(lines - 2 + j, positions, stride=lines), :].astype(BF16)
 
 
-def conv_kernel(mid_ref, above_ref, taps_ref, bias_ref, out_ref, pad_ref, low_ref):
+def conv_kernel(me_ref, mid_ref, above_ref, taps_ref, bias_ref, out_ref, pad_ref):
     positions, lines, share = mid_ref.shape
     parts = out_ref.shape[0]
     cols = positions // parts
-    mid = mid_ref[...].astype(F32)
-    zero_edge = jnp.zeros((1, lines + 8, share), F32)
+    height = pad_ref.shape[1]
+    top = height - lines
+    zero_edge = jnp.zeros((1, height, share), F32)
     pad_ref[0:1] = zero_edge
     pad_ref[positions + 1 : positions + 2] = zero_edge
-    pad_ref[1 : positions + 1, 8 : 8 + lines, :] = mid
-    above = above_ref[...].astype(F32)
-    pad_ref[1 : positions + 1, 6:7, :] = above[0][:, None, :]
-    pad_ref[1 : positions + 1, 7:8, :] = above[1][:, None, :]
-    total = jnp.zeros((positions, lines, share), F32) + bias_ref[...]
+    pad_ref[1 : positions + 1, top:, :] = mid_ref[...].astype(F32)
+    flat_ref = pad_ref.reshape((positions + 2) * height, share)
+    for j in range(2):
+        flat_ref[pl.ds(height + top - 2 + j, positions, stride=height), :] = above_ref[j].astype(F32)
+    slot = lax.broadcasted_iota(jnp.int32, (lines, share), 0)
+    first = me_ref[0] == 0
+    beyond = (jnp.logical_and(first, slot == 1), None, jnp.logical_and(first, slot == 0))
+    taps = []
     for i in range(3):
-        for j in range(3):
-            total = total + taps_ref[i, j : j + 1, :] * pad_ref[j : j + positions, 6 + i : 6 + i + lines, :]
-    main = silu(total).astype(BF16)
-    out_ref[:, : cols * lines, :] = main.reshape(parts, cols * lines, share)
-    low_ref[...] = jnp.zeros_like(low_ref)
-    for j in range(2):
-        low_ref[j, 8 : 8 + positions, :] = mid[:, lines - 2 + j, :]
-    last = jnp.zeros((positions, share), F32) + bias_ref[...]
-    for i in range(2):
-        for j in range(3):
-            last = last + taps_ref[i, j : j + 1, :] * low_ref[i, 7 + j : 7 + j + positions, :]
-    out_ref[:, cols * lines :, :] = silu(last).astype(BF16).reshape(parts, cols, share)
+        wide = [jnp.broadcast_to(taps_ref[i, j : j + 1, :], (lines, share)) for j in range(3)]
+        taps.append(wide if beyond[i] is None else [jnp.where(beyond[i], 0.0, tap) for tap in wide])
+    bias = jnp.broadcast_to(bias_ref[...], (lines, share))
+
+    def block(part, _):
+        start = part * cols
+        for w in range(cols):
+            total = bias
+            for i in range(3):
+                for j in range(3):
+                    total = total + taps[i][j] * pad_ref[start + w + j, top - 2 + i : top - 2 + i + lines, :]
+            out_ref[part, w * lines : (w + 1) * lines, :] = silu(total).astype(BF16)
+        return 0
+
+    lax.fori_loop(0, parts, block, 0, unroll=2)
 
 
 def turn_kernel(me_ref, got_ref, w_ref, *out_refs, rows):
@@ -169,8 +183,7 @@
     width = w_ref.shape[1]
     count = len(out_refs)
     each = parts // count
-    cols = tokens // (rows + 1)
-    order = shuffle(tokens, rows, cols)
+    order = shuffle(tokens, rows, tokens // rows)
     total = jnp.zeros((tokens, width), F32)
     for part in range(parts):
         total = total + dot(got_ref[part], w_ref[pl.ds(part * share, share), :])
@@ -184,28 +197,31 @@
         out_refs[shift][:, each * share :] = proj
 
 
-def col_kernel(me_ref, *refs, count, rows):
+def col_kernel(
+    me_ref, *refs, count, rows,
+):
     got_refs = refs[:count]
-    (w_dt_ref, bias_ref, rate_ref, out_ref, wide_ref, step_ref, rates_ref, pick_ref, ends_ref, state_ref, all_ref, value_ref, sum_ref) = refs[count:]
+    (w_dt_ref, bias_ref, rate_ref, out_ref, wide_ref, step_ref, rates_ref, pick_ref, ends_ref,
+     state_ref, proj_ref, value_ref, sum_ref, back_ref) = refs[count:]
     positions, lines, share = out_ref.shape
     block = rows * lines
     me = me_ref[0]
     for shift in range(count):
         frm = lax.rem(me + count - shift, count)
-        all_ref[pl.ds(pl.multiple_of(frm * block, block), block), :] = got_refs[shift][:block, :]
-
-        @pl.when(frm == count - 1)
+        piece = got_refs[shift][:, :share].astype(F32).reshape(rows, lines, share)
+        value_ref[pl.ds(frm * rows, rows)] = piece
+        proj_ref[pl.ds(pl.multiple_of(frm * block, block), block), :] = got_refs[shift][:, share:]
+
+        @pl.when(frm == 0)
         def _():
-            all_ref[pl.ds(count * block, lines), :] = got_refs[shift][block:, :]
-
-    everything = all_ref[lines:, :]
-    proj = everything[:, share:]
+            value_ref[positions] = piece[0]
+            proj_ref[pl.ds(positions * lines, lines), :] = got_refs[shift][:lines, share:]
+
+    proj = proj_ref[lines:, :]
     prepare(proj, w_dt_ref, bias_ref, rate_ref, wide_ref, step_ref, rates_ref, pick_ref, ends_ref)
-    value_ref[...] = everything[:, :share].astype(F32).reshape(value_ref.shape)
-    sum_ref[...] = jnp.zeros_like(sum_ref)
-    for k in range(2):
-        scan(k, step_ref, value_ref, rates_ref, pick_ref, ends_ref, state_ref, sum_ref)
-    out_ref[...] = sum_ref[...].astype(BF16)
+    values = value_ref.at[pl.ds(1, positions)]
+    scan(step_ref, values, rates_ref, pick_ref, ends_ref, state_ref, sum_ref, back_ref)
+    out_ref[...] = (sum_ref[...] + back_ref[...]).astype(BF16)
 
 
 def vmem():
@@ -244,7 +260,7 @@
         pltpu.VMEM((2, state, lines, channels), F32),
         pltpu.VMEM((state, 2 * state, 2 * LANES), BF16),
         pltpu.VMEM((2, positions * lines, 2 * state), BF16),
-        pltpu.VMEM((state, lines, channels), F32),
+        pltpu.VMEM((2, state, lines, channels), F32),
     ]
 
 
@@ -258,7 +274,8 @@
     n_col, n_row = lax.axis_size("col"), lax.axis_size("row")
     share, col_share = channels // n_col, channels // n_row
     line, column = cols * n_col, rows * n_row
-    tokens, more = rows * cols, (rows + 1) * cols
+    tokens = rows * cols
+    me = lax.axis_index("row").astype(jnp.int32).reshape(1)
 
     sent = call(pack_kernel, "pack", array((n_col, tokens, 2 * share + width)), [], features, gate_branch, w_row_proj)
     got = lax.all_to_all(sent, "col", 0, 0, tiled=True)
@@ -270,35 +287,37 @@
         + [
             pltpu.VMEM((line, rows, share), F32),
             pltpu.VMEM((line, rows, share), F32),
+            pltpu.VMEM((line, rows, share), F32),
             pltpu.VMEM((line * rows, share), F32),
         ],
         near(got.reshape(line, rows, 2 * share + width)),
-        w_dt_row,
-        dt_bias_row,
-        jnp.swapaxes(rate_row, 1, 2),
-        skip_row.reshape(1, share),
-    )
-    above = lax.ppermute(tail, "row", [(i, i + 1) for i in range(n_row - 1)])
+        near(w_dt_row),
+        near(dt_bias_row),
+        near(jnp.swapaxes(rate_row, 1, 2)),
+        near(skip_row.reshape(1, share)),
+    )
+    above = lax.ppermute(tail, "row", [(i, (i + 1) % n_row) for i in range(n_row)])
     sent = call(
         conv_kernel,
         "conv",
-        array((n_col, more, share)),
-        [pltpu.VMEM((line + 2, rows + 8, share), F32), pltpu.VMEM((2, line + 16, share), F32)],
+        array((n_col, tokens, share)),
+        [pltpu.VMEM((line + 2, rows + 8, share), F32)],
+        me,
         near(gated),
         near(above),
-        conv_taps,
-        conv_bias.reshape(1, share),
+        near(conv_taps),
+        near(conv_bias.reshape(1, share)),
+        scalars=1,
     )
     got = lax.all_to_all(sent, "col", 0, 0, tiled=True)
-    me = lax.axis_index("row").astype(jnp.int32).reshape(1)
     pieces = call(
         functools.partial(turn_kernel, rows=rows),
         "turn",
-        [array((more, col_share + width))] * n_row,
+        [array((tokens, col_share + width))] * n_row,
         [],
         me,
         near(got),
-        w_col_proj,
+        near(w_col_proj),
         scalars=1,
     )
     pieces = [pieces[0]] + [
@@ -310,15 +329,16 @@
         jax.ShapeDtypeStruct((column, cols, col_share), BF16),
         scan_scratch(column, cols, col_share, width, state)
         + [
-            pltpu.VMEM(((column + 1) * cols, col_share + width), BF16),
+            pltpu.VMEM(((column + 1) * cols, width), BF16),
+            pltpu.VMEM((column + 1, cols, col_share), F32),
             pltpu.VMEM((column, cols, col_share), F32),
             pltpu.VMEM((column, cols, col_share), F32),
         ],
         me,
         *[near(piece) for piece in pieces],
-        w_dt_col,
-        dt_bias_col,
-        jnp.swapaxes(rate_col, 1, 2),
+        near(w_dt_col),
+        near(dt_bias_col),
+        near(jnp.swapaxes(rate_col, 1, 2)),
         scalars=1,
     )
 

time: 53.6 us -> 44.6 us (0.83)
  blocking collectives: 13.3 us -> 21.2 us
  starting transfers between devices: 13.2 us -> 5.5 us
  Pallas kernels: 16.4 us -> 9.2 us
  waiting for transfers between devices: 10.2 us -> 7.01 us
  local copies, waits for them, and re-layouts: 0 us -> 1.36 us
    all_to_all x1 -> x2, blocking collectives: 13.3 us -> 21.2 us  [local(): got = lax.all_to_all(sent, 'col', 0, 0, tiled=True)]
    pallas_call x5, Pallas kernels: 16.4 us -> 9.2 us  [call(): pl.pallas_call(kernel, name=name, out_shape=outs, in_specs=[smem()] * sca...]
    all_to_all x1 -> x0, waiting for transfers between devices: 5.61 us -> none  [local(): got = lax.all_to_all(sent, 'col', 0, 0, tiled=True)]
    all_to_all x1 -> x0, starting transfers between devices: 3.38 us -> none  [local(): got = lax.all_to_all(sent, 'col', 0, 0, tiled=True)]
    ppermute x1, waiting for transfers between devices: 1.58 us -> 4.14 us  [local(): lax.ppermute(tail, 'row', [(i, (i + 1) % n_row) for i in range(n_row)])]
    ppermute x3, starting transfers between devices: 6.31 us -> 3.87 us  [local(): lax.ppermute(pieces[s], 'row', [(i, (i + s) % n_row) for i in range(n_row)])]
    ppermute x1, starting transfers between devices: 3.48 us -> 1.63 us  [local(): lax.ppermute(tail, 'row', [(i, (i + 1) % n_row) for i in range(n_row)])]
    unnamed x0 -> x20, local copies, waits for them, and re-layouts: none -> 1.36 us
  transfers between devices with their start and end apart: 5 -> 4, of which waited for: 5 -> 3; matrix products, arithmetic and copies ran while one was open for 0% -> 0% of each run, Pallas kernels for 0% -> 0%
where the time goes in v3:
time: 44.6 us; the launch traced here: 44.3 us
  blocking collectives  21.2 us (48%)
  Pallas kernels  9.2 us (21%)
  waiting for transfers between devices  7.01 us (16%)
  starting transfers between devices  5.5 us (12%)
  local copies, waits for them, and re-layouts  1.36 us (3%)
    all_to_all x2, blocking collectives, local(): got = lax.all_to_all(sent, 'col', 0, 0, tiled=True)  21.2 us
    pallas_call x5, Pallas kernels, call(): pl.pallas_call(kernel, name=name, out_shape=outs, in_specs=[smem()] * sca...  9.2 us
    ppermute x1, waiting for transfers between devices, local(): lax.ppermute(tail, 'row', [(i, (i + 1) % n_row) for i in range(n_row)])  4.14 us
    ppermute x3, starting transfers between devices, local(): lax.ppermute(pieces[s], 'row', [(i, (i + s) % n_row) for i in range(n_row)])  3.87 us
    ppermute x3, waiting for transfers between devices, local(): lax.ppermute(pieces[s], 'row', [(i, (i + s) % n_row) for i in range(n_row)])  2.87 us
    ppermute x1, starting transfers between devices, local(): lax.ppermute(tail, 'row', [(i, (i + 1) % n_row) for i in range(n_row)])  1.63 us
    unnamed x20, local copies, waits for them, and re-layouts  1.36 us
  transfers between devices with their start and end apart: 4, of which 3 were waited for; matrix products, arithmetic and copies ran while one was open for 0% of the time, Pallas kernels for 0%

profile of v3, /device:TPU:0, one launch (start us, length us, event | category | flops | bytes accessed | tf_op | source)
XLA Modules:
  0.0 44.3 jit_solution(6291198266254593524)
XLA Ops:
  0.0 1.4 %pack.1 = bf16[8,64,384]{2,1,0:T(8,128)(2,1)S(1)} custom-call(bf16[8,8,1024]{2,1,0:T(8,128)(2,1)} %feat_ref.1, bf16[8,8,1024]{2,1,0:T(8,128)(2,1)} %gate_ref.1, bf16[1024,128]{1,0:T(8,128)(2,1)} %w_ref.2), custom_call_target="tpu_custom_call" | custom-call | tf_op jit(solution)/shard_map/pack/pallas_call | solution.py:237
  1.4 0.0 copy-start.3
  1.4 0.0 copy-start.4
  1.4 13.3 %all_to_all.10 = bf16[8,64,384]{2,1,0:T(8,128)(2,1)S(1)} all-to-all(bf16[8,64,384]{2,1,0:T(8,128)(2,1)S(1)} %pack.1), channel_id=1, replica_groups=mesh['row'=4,'col'=8] {'col'}, dimensions={0} | all-to-all | bytes 786432 | tf_op jit(solution)/shard_map/all_to_all | solution.py:281
  14.7 0.0 copy-done.3
  14.7 0.0 copy-done.4
  14.7 0.7 %copy-done.7 = f32[2,128]{1,0:T(2,128)S(1)} copy-done((f32[2,128]{1,0:T(2,128)S(1)}, f32[2,128]{1,0:T(2,128)}, u32[]{:S(2)}) %copy-start.7) | copy-done | bytes 1048
  15.4 0.0 copy-done.8
  15.4 3.4 %row_scan.1 = (bf16[64,8,128]{2,1,0:T(8,128)(2,1)S(1)}, bf16[2,64,128]{2,1,0:T(8,128)(2,1)S(1)}) custom-call(bf16[64,8,384]{2,1,0:T(8,128)(2,1)S(1)} %bitcast.6, bf16[2,32,128]{2,1,0:T(8,128)(2,1)S(1)} %copy-done.3, f32[2,128]{1,0:T(2,128)S(1)} %copy-done.7, f32[2,16,128]{2,1,0:T(8,128)S(1)} %bitcast.8, f32[1,128]{1,0:T(1,128)S(1)} %bitcast.9), custom_call_target="tpu_custom_call" | custom-call | tf_op jit(solution)/shard_map/row_scan/pallas_call | solution.py:237
  18.8 1.6 %collective-permute-start = (bf16[2,64,128]{2,1,0:T(8,128)(2,1)S(1)}, bf16[2,64,128]{2,1,0:T(8,128)(2,1)S(1)}, u32[]{:S(2)}, u32[]{:S(2)}) collective-permute-start(bf16[2,64,128]{2,1,0:T(8,128)(2,1)S(1)} %get-tuple-element.12), channel_id=1, source_target_pairs={{0,8},{8,16},{16,24},{24,0},{1,9},{9,17},{17,25},{25,1},{2,10},{10... | collective-permute-start | bytes 98312 | tf_op jit(solution)/shard_map/ppermute | solution.py:299
  20.4 4.1 %collective-permute-done.above_ref = bf16[2,64,128]{2,1,0:T(8,128)(2,1)S(1)} collective-permute-done((bf16[2,64,128]{2,1,0:T(8,128)(2,1)S(1)}, bf16[2,64,128]{2,1,0:T(8,128)(2,1)S(1)}, u32[]{:S(2)}, u32[]{:S(2)}) %collective-permute-start) | collective-permute-done | bytes 32800 | tf_op jit(solution)/shard_map/ppermute | solution.py:299
  24.6 0.0 copy-done.5
  24.6 0.7 %copy-done.9 = f32[128]{0:T(128)S(1)} copy-done((f32[128]{0:T(128)S(1)}, f32[128]{0:T(128)}, u32[]{:S(2)}) %copy-start.9) | copy-done | bytes 536
  25.2 0.3 conv.1
  25.6 7.9 %all_to_all.11.got_ref = bf16[8,64,128]{2,1,0:T(8,128)(2,1)S(1)} all-to-all(bf16[8,64,128]{2,1,0:T(8,128)(2,1)S(1)} %conv.1), channel_id=1, replica_groups=mesh['row'=4,'col'=8] {'col'}, dimensions={0} | all-to-all | bytes 262144 | tf_op jit(solution)/shard_map/all_to_all | solution.py:312
  33.4 0.0 copy-done
  33.5 0.4 turn.1
  33.9 0.1 collective-permute-start.1
  33.9 2.4 %collective-permute-start.2 = (bf16[64,384]{1,0:T(8,128)(2,1)S(1)}, bf16[64,384]{1,0:T(8,128)(2,1)S(1)}, u32[]{:S(2)}, u32[]{:S(2)}) collective-permute-start(bf16[64,384]{1,0:T(8,128)(2,1)S(1)} %get-tuple-element.15), channel_id=1, source_target_pairs={{0,16},{8,24},{16,0},{24,8},{1,17},{9,25},{17,1},{25,9},{2,18},{10... | collective-permute-start | bytes 147464 | tf_op jit(solution)/shard_map/ppermute | solution.py:324
  36.3 1.5 %collective-permute-start.3 = (bf16[64,384]{1,0:T(8,128)(2,1)S(1)}, bf16[64,384]{1,0:T(8,128)(2,1)S(1)}, u32[]{:S(2)}, u32[]{:S(2)}) collective-permute-start(bf16[64,384]{1,0:T(8,128)(2,1)S(1)} %get-tuple-element.16), channel_id=1, source_target_pairs={{0,24},{8,0},{16,8},{24,16},{1,25},{9,1},{17,9},{25,17},{2,26},{10... | collective-permute-start | bytes 147464 | tf_op jit(solution)/shard_map/ppermute | solution.py:324
  37.8 2.2 %collective-permute-done.1.refs_1_ = bf16[64,384]{1,0:T(8,128)(2,1)S(1)} collective-permute-done((bf16[64,384]{1,0:T(8,128)(2,1)S(1)}, bf16[64,384]{1,0:T(8,128)(2,1)S(1)}, u32[]{:S(2)}, u32[]{:S(2)}) %collective-permute-start.1) | collective-permute-done | bytes 49184 | tf_op jit(solution)/shard_map/ppermute | solution.py:324
  40.0 0.7 %collective-permute-done.2.refs_2_ = bf16[64,384]{1,0:T(8,128)(2,1)S(1)} collective-permute-done((bf16[64,384]{1,0:T(8,128)(2,1)S(1)}, bf16[64,384]{1,0:T(8,128)(2,1)S(1)}, u32[]{:S(2)}, u32[]{:S(2)}) %collective-permute-start.2) | collective-permute-done | bytes 49184 | tf_op jit(solution)/shard_map/ppermute | solution.py:324
  40.6 0.0 collective-permute-done.3.refs_3_
  40.7 3.7 %col_scan.1 = bf16[32,8,256]{2,1,0:T(8,128)(2,1)} custom-call(s32[1]{0:T(128)} %bitcast.me_ref, bf16[64,384]{1,0:T(8,128)(2,1)S(1)} %get-tuple-element.13.refs_0_, bf16[64,384]{1,0:T(8,128)(2,1)S(1)} %collective-permute-done.1.refs_1_, bf16[64,384]{1,0:T(8,128)(2,1)S(1)} %collective-permute-done.2.refs_2_, ...), custom_call_target="tpu_custom_call" | custom-call | tf_op jit(solution)/shard_map/col_scan/pallas_call | solution.py:237
  (11 shorter events, 0.0 us)
Async XLA Ops:
  1.4 13.3 %copy-start.3 = (bf16[2,32,128]{2,1,0:T(8,128)(2,1)S(1)}, bf16[2,32,128]{2,1,0:T(8,128)(2,1)}, u32[]{:S(2)}) copy-start(bf16[2,32,128]{2,1,0:T(8,128)(2,1)} %w_dt_ref.1) | copy-start | bytes 49156
  1.4 13.3 %copy-start.4 = (f32[2,128,16]{1,2,0:T(8,128)S(1)}, f32[2,128,16]{1,2,0:T(8,128)}, u32[]{:S(2)}) copy-start(f32[2,128,16]{1,2,0:T(8,128)} %param.18) | copy-start | bytes 49156
  14.7 0.7 %copy-start.7 = (f32[2,128]{1,0:T(2,128)S(1)}, f32[2,128]{1,0:T(2,128)}, u32[]{:S(2)}) copy-start(f32[2,128]{1,0:T(2,128)} %bias_ref.1) | copy-start | bytes 3076
  14.7 0.7 %copy-start.8 = (f32[128]{0:T(128)S(1)}, f32[128]{0:T(128)}, u32[]{:S(2)}) copy-start(f32[128]{0:T(128)} %param.19) | copy-start | bytes 1540
  18.8 5.8 %collective-permute-start = (bf16[2,64,128]{2,1,0:T(8,128)(2,1)S(1)}, bf16[2,64,128]{2,1,0:T(8,128)(2,1)S(1)}, u32[]{:S(2)}, u32[]{:S(2)}) collective-permute-start(bf16[2,64,128]{2,1,0:T(8,128)(2,1)S(1)} %get-tuple-element.12), channel_id=1, source_target_pairs={{0,8},{8,16},{16,24},{24,0},{1,9},{9,17},{17,25},{25,1},{2,10},{10... | collective-permute-start | bytes 98312 | tf_op jit(solution)/shard_map/ppermute | solution.py:299
  20.4 4.1 %copy-start.5 = (f32[3,3,128]{2,1,0:T(4,128)S(1)}, f32[3,3,128]{2,1,0:T(4,128)}, u32[]{:S(2)}) copy-start(f32[3,3,128]{2,1,0:T(4,128)} %taps_ref.1) | copy-start | bytes 13828
  24.6 0.7 %copy-start.9 = (f32[128]{0:T(128)S(1)}, f32[128]{0:T(128)}, u32[]{:S(2)}) copy-start(f32[128]{0:T(128)} %param.21) | copy-start | bytes 1540
  25.2 8.2 %copy-start = (bf16[1024,128]{1,0:T(8,128)(2,1)S(1)}, bf16[1024,128]{1,0:T(8,128)(2,1)}, u32[]{:S(2)}) copy-start(bf16[1024,128]{1,0:T(8,128)(2,1)} %w_ref.3) | copy-start | bytes 786436
  33.5 7.2 %copy-start.1 = (bf16[2,32,256]{2,1,0:T(8,128)(2,1)S(1)}, bf16[2,32,256]{2,1,0:T(8,128)(2,1)}, u32[]{:S(2)}) copy-start(bf16[2,32,256]{2,1,0:T(8,128)(2,1)} %refs_4_.1) | copy-start | bytes 98308
  33.5 7.2 %copy-start.2 = (f32[2,256,16]{1,2,0:T(8,128)S(1)}, f32[2,256,16]{1,2,0:T(8,128)}, u32[]{:S(2)}) copy-start(f32[2,256,16]{1,2,0:T(8,128)} %param.25) | copy-start | bytes 98308
  33.9 6.1 %collective-permute-start.1 = (bf16[64,384]{1,0:T(8,128)(2,1)S(1)}, bf16[64,384]{1,0:T(8,128)(2,1)S(1)}, u32[]{:S(2)}, u32[]{:S(2)}) collective-permute-start(bf16[64,384]{1,0:T(8,128)(2,1)S(1)} %get-tuple-element.14), channel_id=1, source_target_pairs={{0,8},{8,16},{16,24},{24,0},{1,9},{9,17},{17,25},{25,1},{2,10},{10... | collective-permute-start | bytes 147464 | tf_op jit(solution)/shard_map/ppermute | solution.py:324
  33.9 6.7 %collective-permute-start.2 = (bf16[64,384]{1,0:T(8,128)(2,1)S(1)}, bf16[64,384]{1,0:T(8,128)(2,1)S(1)}, u32[]{:S(2)}, u32[]{:S(2)}) collective-permute-start(bf16[64,384]{1,0:T(8,128)(2,1)S(1)} %get-tuple-element.15), channel_id=1, source_target_pairs={{0,16},{8,24},{16,0},{24,8},{1,17},{9,25},{17,1},{25,9},{2,18},{10... | collective-permute-start | bytes 147464 | tf_op jit(solution)/shard_map/ppermute | solution.py:324
  36.3 4.3 %copy-start.6 = (f32[2,256]{1,0:T(2,128)S(1)}, f32[2,256]{1,0:T(2,128)}, u32[]{:S(2)}) copy-start(f32[2,256]{1,0:T(2,128)} %refs_5_.1) | copy-start | bytes 6148
  36.3 4.3 %collective-permute-start.3 = (bf16[64,384]{1,0:T(8,128)(2,1)S(1)}, bf16[64,384]{1,0:T(8,128)(2,1)S(1)}, u32[]{:S(2)}, u32[]{:S(2)}) collective-permute-start(bf16[64,384]{1,0:T(8,128)(2,1)S(1)} %get-tuple-element.16), channel_id=1, source_target_pairs={{0,24},{8,0},{16,8},{24,16},{1,25},{9,1},{17,9},{25,17},{2,26},{10... | collective-permute-start | bytes 147464 | tf_op jit(solution)/shard_map/ppermute | solution.py:324

commit v4 on v3

--- a/solution.py
+++ b/solution.py
@@ -35,22 +35,38 @@
     return jnp.where(frm == wanted, 1.0, 0.0).astype(BF16)
 
 
-def pack_kernel(feat_ref, gate_ref, w_ref, out_ref):
+def fetches(sources, targets, sems):
+    copies = [pltpu.make_async_copy(s, t, sems.at[i]) for i, (s, t) in enumerate(zip(sources, targets))]
+    for copy in copies:
+        copy.start()
+    return copies
+
+
+def pack_kernel(feat_hbm, gate_hbm, w_hbm, *refs):
+    count = (len(refs) - 5) // 2
+    param_refs, (out_ref, *held_refs) = refs[:count], refs[count : 2 * count + 1]
+    feat_ref, gate_ref, w_ref, sems = refs[2 * count + 1 :]
+    copies = fetches((feat_hbm, w_hbm, gate_hbm, *param_refs), (feat_ref, w_ref, gate_ref, *held_refs), sems)
     rows, cols, channels = feat_ref.shape
     tokens = rows * cols
     parts = out_ref.shape[0]
     share = channels // parts
+    order = shuffle(tokens, cols, rows)
+    copies[0].wait()
     feats = feat_ref[...].reshape(tokens, channels)
-    gates = gate_ref[...].reshape(tokens, channels)
-    proj = dot(feats, w_ref[...]).astype(BF16)
-    order = shuffle(tokens, cols, rows)
-    feats = dot(order, feats).astype(BF16)
-    gates = dot(order, gates).astype(BF16)
-    proj = dot(order, proj).astype(BF16)
+    moved = dot(order, feats).astype(BF16)
     for part in range(parts):
-        out_ref[part, :, :share] = feats[:, part * share : (part + 1) * share]
-        out_ref[part, :, share : 2 * share] = gates[:, part * share : (part + 1) * share]
+        out_ref[part, :, :share] = moved[:, part * share : (part + 1) * share]
+    copies[1].wait()
+    proj = dot(order, dot(feats, w_ref[...]).astype(BF16)).astype(BF16)
+    for part in range(parts):
         out_ref[part, :, 2 * share :] = proj
+    copies[2].wait()
+    moved = dot(order, gate_ref[...].reshape(tokens, channels)).astype(BF16)
+    for part in range(parts):
+        out_ref[part, :, share : 2 * share] = moved[:, part * share : (part + 1) * share]
+    for copy in copies[3:]:
+        copy.wait()
 
 
 def one_hot(height, width, hit):
@@ -122,29 +138,110 @@
                 back_ref[firsts[1] + p, :, g] = totals[1][p][i]
         return 0
 
-    lax.fori_loop(0, blocks, advance, 0, unroll=math.gcd(blocks, 4))
-
-
-def row_kernel(
-    got_ref, w_dt_ref, bias_ref, rate_ref, skip_ref, out_ref, tail_ref,
-    wide_ref, step_ref, rates_ref, pick_ref, ends_ref, state_ref, value_ref, sum_ref, back_ref, flat_ref,
-):
+    lax.fori_loop(0, blocks, advance, 0, unroll=True)
+
+
+def joint_scan(step_ref, value_ref, rates_ref, pick_ref, ends_ref, out_ref):
+    positions, lines, channels = out_ref.shape
+    state = rates_ref.shape[0]
+    size = math.gcd(positions, 8)
+    held = [jnp.zeros((lines, channels), F32)] * state
+    for first in range(0, positions, size):
+        steps = [step_ref[first + p] for p in range(size)]
+        drives = [steps[p] * value_ref[first + p] for p in range(size)]
+        totals = [None] * size
+        ends = ends_ref[first * lines : (first + size) * lines, :]
+        for n in range(state):
+            spread = dot(ends, pick_ref[n])
+            rates = rates_ref[n]
+            for p in range(size):
+                b = spread[p * lines : (p + 1) * lines, :channels]
+                c = spread[p * lines : (p + 1) * lines, LANES : LANES + channels]
+                held[n] = jnp.exp2(steps[p] * rates) * held[n] + drives[p] * b
+                read = c * held[n]
+                totals[p] = read if n == 0 else totals[p] + read
+        for p in range(size):
+            out_ref[first + p] = totals[p]
+
+
+def row_tables(w_dt_ref, rate_ref, wide_ref, rates_ref, pick_ref):
+    _, rank, channels = w_dt_ref.shape
+    state = rate_ref.shape[1]
+    segment = rank + 2 * state
+    lines = rates_ref.shape[1]
+    low = lax.broadcasted_iota(jnp.int32, (lines, channels), 0) < lines // 2
+    wide_ref[...] = jnp.zeros_like(wide_ref)
+    for k in range(2):
+        wide_ref[pl.ds(k * segment, rank), pl.ds(k * channels, channels)] = w_dt_ref[k]
+    turned = [rate_ref[k] * -LOG2E for k in range(2)]
+    for n in range(state):
+        rates_ref[n] = jnp.where(low, *[jnp.broadcast_to(t[n : n + 1, :], (lines, channels)) for t in turned])
+        pick_ref[n] = one_hot(2 * state, 2 * LANES, lambda r, c: r == n + jnp.where(c < LANES, 0, state))
+
+
+def half_rows(upper, rank, got_ref, bias_ref, skip_ref, wide_ref, rates_ref, pick_ref, out_ref, scratch):
+    step_ref, value_ref, proj_ref, ends_ref, sum_ref = scratch
     positions, lines, share = out_ref.shape
-    width = got_ref.shape[2] - 2 * share
-    proj = got_ref[:, :, 2 * share :].reshape(positions * lines, width)
-    prepare(proj, w_dt_ref, bias_ref, rate_ref, wide_ref, step_ref, rates_ref, pick_ref, ends_ref)
-    value_ref[...] = got_ref[:, :, :share].astype(F32)
-    scan(step_ref, value_ref, rates_ref, pick_ref, ends_ref, state_ref, sum_ref, back_ref)
-    mix = sum_ref[...] + back_ref[...] + skip_ref[...] * value_ref[...]
-    gated = mix * silu(got_ref[:, :, share : 2 * share].astype(F32))
-    out_ref[...] = gated.astype(BF16)
-    flat_ref[...] = gated.reshape(flat_ref.shape)
+    state = rates_ref.shape[0]
+    segment = rank + 2 * state
+    width = proj_ref.shape[2]
+    half = lines // 2
+
+    def low(columns):
+        return lax.broadcasted_iota(jnp.int32, (lines, columns), 0) < half
+
+    def swap(v):
+        return pltpu.roll(v, half, 0)
+
+    def packed(p, at):
+        there = got_ref[p, :, at].astype(F32)
+        back = got_ref[positions - 1 - p, :, at].astype(F32)
+        there, back = (swap(there), back) if upper else (there, swap(back))
+        return jnp.where(low(there.shape[1]), there, back)
+
+    for p in range(positions):
+        value_ref[p] = packed(p, pl.ds(0, share))
+        proj_ref[p] = packed(p, pl.ds(2 * share, width))
+    proj = proj_ref[...].reshape(positions * lines, width).astype(BF16)
+    raw = dot(proj, wide_ref[...])
+    parts = [(raw[:, k * share : (k + 1) * share] + bias_ref[k : k + 1, :]).reshape(positions, lines, share) for k in range(2)]
+    step_ref[...] = softplus(jnp.where(low(share), *parts))
+    ends = [
+        dot(proj, one_hot(width, 2 * state, lambda r, c: r == c + k * segment + rank)).reshape(positions, lines, 2 * state)
+        for k in range(2)
+    ]
+    ends_ref[...] = jnp.where(low(2 * state), *ends).reshape(ends_ref.shape).astype(BF16)
+    joint_scan(step_ref, value_ref, rates_ref, pick_ref, ends_ref, sum_ref)
+    for p in range(positions):
+        there, back = sum_ref[p], sum_ref[positions - 1 - p]
+        mix = swap(there) + back if upper else there + swap(back)
+        mix = mix + skip_ref[...] * got_ref[p, :, :share].astype(F32)
+        gated = mix * silu(got_ref[p, :, share : 2 * share].astype(F32))
+        value_ref[p] = gated
+        out_ref[p] = gated.astype(BF16)
+
+
+def upper_kernel(got_ref, w_dt_ref, bias_ref, rate_ref, skip_ref, *refs):
+    *scratch, sems = refs[-6:]
+    count = (len(refs) - 11) // 2
+    out_ref, tail_ref, wide_ref, rates_ref, pick_ref, *held_refs = refs[count:-6]
+    copies = fetches(refs[:count], held_refs, sems)
+    positions, lines, share = out_ref.shape
+    row_tables(w_dt_ref, rate_ref, wide_ref, rates_ref, pick_ref)
+    half_rows(True, w_dt_ref.shape[1], got_ref, bias_ref, skip_ref, wide_ref, rates_ref, pick_ref, out_ref, scratch)
+    flat_ref = scratch[1].reshape(positions * lines, share)
     for j in range(2):
         tail_ref[j] = flat_ref[pl.ds(lines - 2 + j, positions, stride=lines), :].astype(BF16)
-
-
-def conv_kernel(me_ref, mid_ref, above_ref, taps_ref, bias_ref, out_ref, pad_ref):
-    positions, lines, share = mid_ref.shape
+    for copy in copies:
+        copy.wait()
+
+
+def lower_kernel(got_ref, bias_ref, skip_ref, wide_ref, rates_ref, pick_ref, out_ref, *scratch, rank):
+    half_rows(False, rank, got_ref, bias_ref, skip_ref, wide_ref, rates_ref, pick_ref, out_ref, scratch)
+
+
+def conv_kernel(me_ref, lower_ref, upper_ref, above_ref, taps_ref, bias_ref, out_ref, pad_ref):
+    positions, lines, share = lower_ref.shape
     parts = out_ref.shape[0]
     cols = positions // parts
     height = pad_ref.shape[1]
@@ -152,11 +249,12 @@
     zero_edge = jnp.zeros((1, height, share), F32)
     pad_ref[0:1] = zero_edge
     pad_ref[positions + 1 : positions + 2] = zero_edge
-    pad_ref[1 : positions + 1, top:, :] = mid_ref[...].astype(F32)
+    slot = lax.broadcasted_iota(jnp.int32, (lines, share), 0)
+    mid = jnp.where(slot < lines // 2, lower_ref[...].astype(F32), upper_ref[...].astype(F32))
+    pad_ref[1 : positions + 1, top:, :] = mid
     flat_ref = pad_ref.reshape((positions + 2) * height, share)
     for j in range(2):
         flat_ref[pl.ds(height + top - 2 + j, positions, stride=height), :] = above_ref[j].astype(F32)
-    slot = lax.broadcasted_iota(jnp.int32, (lines, share), 0)
     first = me_ref[0] == 0
     beyond = (jnp.logical_and(first, slot == 1), None, jnp.logical_and(first, slot == 0))
     taps = []
@@ -232,17 +330,18 @@
     return pl.BlockSpec(memory_space=pltpu.SMEM)
 
 
-def call(kernel, name, outs, scratch, *args, scalars=0):
+def call(kernel, name, outs, scratch, *args, scalars=0, far=()):
     many = isinstance(outs, (list, tuple))
+    hbm = pl.BlockSpec(memory_space=pltpu.HBM)
     return pl.pallas_call(
         kernel,
         name=name,
         out_shape=outs,
-        in_specs=[smem()] * scalars + [vmem()] * (len(args) - scalars),
+        in_specs=[smem()] * scalars + [vmem()] * (len(args) - scalars) + [hbm] * len(far),
         out_specs=[vmem()] * len(outs) if many else vmem(),
         scratch_shapes=scratch,
-        compiler_params=pltpu.CompilerParams(vmem_limit_bytes=56 << 20),
-    )(*args)
+        compiler_params=pltpu.CompilerParams(vmem_limit_bytes=24 << 20),
+    )(*args, *[pltpu.with_memory_space_constraint(x, pltpu.HBM) for x in far])
 
 
 def array(shape, dtype=BF16):
@@ -251,6 +350,10 @@
 
 def near(x):
     return pltpu.with_memory_space_constraint(x, pltpu.VMEM)
+
+
+def like(x):
+    return array(x.shape, x.dtype)
 
 
 def scan_scratch(positions, lines, channels, width, state):
@@ -277,36 +380,75 @@
     tokens = rows * cols
     me = lax.axis_index("row").astype(jnp.int32).reshape(1)
 
-    sent = call(pack_kernel, "pack", array((n_col, tokens, 2 * share + width)), [], features, gate_branch, w_row_proj)
+    row_params = (w_dt_row, dt_bias_row, jnp.swapaxes(rate_row, 1, 2), skip_row.reshape(1, share))
+    params = (
+        conv_taps,
+        conv_bias.reshape(1, share),
+        w_col_proj,
+        w_dt_col,
+        dt_bias_col,
+        jnp.swapaxes(rate_col, 1, 2),
+    )
+    sent, *row_params = call(
+        pack_kernel,
+        "pack",
+        [array((n_col, tokens, 2 * share + width))] + [like(p) for p in row_params],
+        [
+            pltpu.VMEM(features.shape, BF16),
+            pltpu.VMEM(gate_branch.shape, BF16),
+            pltpu.VMEM(w_row_proj.shape, BF16),
+            pltpu.SemaphoreType.DMA((3 + len(row_params),)),
+        ],
+        far=(features, gate_branch, w_row_proj, *row_params),
+    )
     got = lax.all_to_all(sent, "col", 0, 0, tiled=True)
-    gated, tail = call(
-        row_kernel,
-        "row_scan",
-        [array((line, rows, share)), array((2, line, share))],
-        scan_scratch(line, rows, share, width, state)
-        + [
-            pltpu.VMEM((line, rows, share), F32),
-            pltpu.VMEM((line, rows, share), F32),
-            pltpu.VMEM((line, rows, share), F32),
-            pltpu.VMEM((line * rows, share), F32),
-        ],
-        near(got.reshape(line, rows, 2 * share + width)),
-        near(w_dt_row),
-        near(dt_bias_row),
-        near(jnp.swapaxes(rate_row, 1, 2)),
-        near(skip_row.reshape(1, share)),
+    got = near(got.reshape(line, rows, 2 * share + width))
+    scratch = [
+        pltpu.VMEM((line, rows, share), F32),
+        pltpu.VMEM((line, rows, share), F32),
+        pltpu.VMEM((line, rows, width), F32),
+        pltpu.VMEM((line * rows, 2 * state), BF16),
+        pltpu.VMEM((line, rows, share), F32),
+    ]
+    upper, tail, wide, rates, pick, *params = call(
+        upper_kernel,
+        "upper_rows",
+        [
+            array((line, rows, share)),
+            array((2, line, share)),
+            array((width, 2 * share)),
+            array((state, rows, share), F32),
+            array((state, 2 * state, 2 * LANES)),
+        ]
+        + [like(p) for p in params],
+        scratch + [pltpu.SemaphoreType.DMA((len(params),))],
+        got,
+        *row_params,
+        far=params,
     )
     above = lax.ppermute(tail, "row", [(i, (i + 1) % n_row) for i in range(n_row)])
+    lower = call(
+        functools.partial(lower_kernel, rank=w_dt_row.shape[1]),
+        "lower_rows",
+        array((line, rows, share)),
+        scratch,
+        got,
+        row_params[1],
+        row_params[3],
+        near(wide),
+        near(rates),
+        near(pick),
+    )
     sent = call(
         conv_kernel,
         "conv",
         array((n_col, tokens, share)),
         [pltpu.VMEM((line + 2, rows + 8, share), F32)],
         me,
-        near(gated),
+        near(lower),
+        near(upper),
         near(above),
-        near(conv_taps),
-        near(conv_bias.reshape(1, share)),
+        *params[:2],
         scalars=1,
     )
     got = lax.all_to_all(sent, "col", 0, 0, tiled=True)
@@ -317,7 +459,7 @@
         [],
         me,
         near(got),
-        near(w_col_proj),
+        params[2],
         scalars=1,
     )
     pieces = [pieces[0]] + [
@@ -336,9 +478,7 @@
         ],
         me,
         *[near(piece) for piece in pieces],
-        near(w_dt_col),
-        near(dt_bias_col),
-        near(jnp.swapaxes(rate_col, 1, 2)),
+        *params[3:],
         scalars=1,
     )
 

time: 44.6 us -> 41.3 us (0.926)
  waiting for transfers between devices: 7.01 us -> 5.49 us
  local copies, waits for them, and re-layouts: 1.36 us -> 0 us
    ppermute x1, waiting for transfers between devices: 4.14 us -> 2.62 us  [local(): lax.ppermute(tail, 'row', [(i, (i + 1) % n_row) for i in range(n_row)])]
    unnamed x20 -> x0, local copies, waits for them, and re-layouts: 1.36 us -> none
    pallas_call x5 -> x6, Pallas kernels: 9.2 us -> 8.83 us  [call(): pl.pallas_call(kernel, name=name, out_shape=outs, in_specs=[smem()] * sca...]
  transfers between devices with their start and end apart: 4 -> 4, of which waited for: 3 -> 3; matrix products, arithmetic and copies ran while one was open for 0% -> 0% of each run, Pallas kernels for 0% -> 4%
where the time goes in v4:
time: 41.3 us; the launch traced here: 41.1 us
  blocking collectives  21.2 us (51%)
  Pallas kernels  8.83 us (21%)
  starting transfers between devices  5.51 us (13%)
  waiting for transfers between devices  5.49 us (13%)
    all_to_all x2, blocking collectives, local(): got = lax.all_to_all(sent, 'col', 0, 0, tiled=True)  21.2 us
    pallas_call x6, Pallas kernels, call(): pl.pallas_call(kernel, name=name, out_shape=outs, in_specs=[smem()] * sca...  8.83 us
    ppermute x3, starting transfers between devices, local(): lax.ppermute(pieces[s], 'row', [(i, (i + s) % n_row) for i in range(n_row)])  3.87 us
    ppermute x3, waiting for transfers between devices, local(): lax.ppermute(pieces[s], 'row', [(i, (i + s) % n_row) for i in range(n_row)])  2.87 us
    ppermute x1, waiting for transfers between devices, local(): lax.ppermute(tail, 'row', [(i, (i + 1) % n_row) for i in range(n_row)])  2.62 us
    ppermute x1, starting transfers between devices, local(): lax.ppermute(tail, 'row', [(i, (i + 1) % n_row) for i in range(n_row)])  1.63 us
  transfers between devices with their start and end apart: 4, of which 3 were waited for; matrix products, arithmetic and copies ran while one was open for 0% of the time, Pallas kernels for 4%

profile of v4, /device:TPU:0, one launch (start us, length us, event | category | flops | bytes accessed | tf_op | source)
XLA Modules:
  0.0 41.1 jit_solution(17269679278951670846)
XLA Ops:
  0.0 1.6 %pack.1 = (bf16[8,64,384]{2,1,0:T(8,128)(2,1)S(1)}, bf16[2,32,128]{2,1,0:T(8,128)(2,1)S(1)}, f32[2,128]{1,0:T(2,128)S(1)}, f32[2,16,128]{2,1,0:T(8,128)S(1)}, f32[1,128]{1,0:T(1,128)S(1)}) custom-call(bf16[8,8,1024]{2,1,0:T(8,128)(2,1)} %feat_hbm.1, bf16[8,8,1024]{2,1,0:T(8,128)(2,1)} %gate_hbm.1, bf16[1024,128]{1,0:T(8,128)(2,1)} %w_hbm.1, ...), custom_call_target="tpu_custom_call" | custom-call | tf_op jit(solution)/shard_map/pack/pallas_call | solution.py:336
  1.6 13.3 %all_to_all.10 = bf16[8,64,384]{2,1,0:T(8,128)(2,1)S(1)} all-to-all(bf16[8,64,384]{2,1,0:T(8,128)(2,1)S(1)} %get-tuple-element.25), channel_id=1, replica_groups=mesh['row'=4,'col'=8] {'col'}, dimensions={0} | all-to-all | bytes 786432 | tf_op jit(solution)/shard_map/all_to_all | solution.py:404
  14.9 1.6 %upper_rows.1 = (bf16[64,8,128]{2,1,0:T(8,128)(2,1)S(1)}, bf16[2,64,128]{2,1,0:T(8,128)(2,1)S(1)}, bf16[128,256]{1,0:T(8,128)(2,1)S(1)}, f32[16,8,128]{2,1,0:T(8...) custom-call(bf16[64,8,384]{2,1,0:T(8,128)(2,1)S(1)} %bitcast.6, ...), custom_call_target="tpu_custom_call" | custom-call | tf_op jit(solution)/shard_map/upper_rows/pallas_call | solution.py:336
  16.6 1.6 %collective-permute-start = (bf16[2,64,128]{2,1,0:T(8,128)(2,1)S(1)}, bf16[2,64,128]{2,1,0:T(8,128)(2,1)S(1)}, u32[]{:S(2)}, u32[]{:S(2)}) collective-permute-start(bf16[2,64,128]{2,1,0:T(8,128)(2,1)S(1)} %get-tuple-element.34), channel_id=1, source_target_pairs={{0,8},{8,16},{16,24},{24,0},{1,9},{9,17},{17,25},{25,1},{2,10},{10... | collective-permute-start | bytes 98312 | tf_op jit(solution)/shard_map/ppermute | solution.py:429
  18.2 1.5 %lower_rows.1.lower_ref = bf16[64,8,128]{2,1,0:T(8,128)(2,1)S(1)} custom-call(bf16[64,8,384]{2,1,0:T(8,128)(2,1)S(1)} %bitcast.7, f32[2,128]{1,0:T(2,128)S(1)} %get-tuple-element.26.bias_ref, f32[1,128]{1,0:T(1,128)S(1)} %get-tuple-element.27.skip_ref, bf16[128,256]{1,0:T(8,128)(2,1)S(1)} %get-tuple-element.30.wide_ref, ...), custom_call_target="tpu_custom_call" | custom-call | tf_op jit(solution)/shard_map/lower_rows/pallas_call | solution.py:336
  19.7 2.6 %collective-permute-done.above_ref = bf16[2,64,128]{2,1,0:T(8,128)(2,1)S(1)} collective-permute-done((bf16[2,64,128]{2,1,0:T(8,128)(2,1)S(1)}, bf16[2,64,128]{2,1,0:T(8,128)(2,1)S(1)}, u32[]{:S(2)}, u32[]{:S(2)}) %collective-permute-start) | collective-permute-done | bytes 32800 | tf_op jit(solution)/shard_map/ppermute | solution.py:429
  22.3 0.3 conv.1
  22.7 7.9 %all_to_all.11.got_ref = bf16[8,64,128]{2,1,0:T(8,128)(2,1)S(1)} all-to-all(bf16[8,64,128]{2,1,0:T(8,128)(2,1)S(1)} %conv.1), channel_id=1, replica_groups=mesh['row'=4,'col'=8] {'col'}, dimensions={0} | all-to-all | bytes 262144 | tf_op jit(solution)/shard_map/all_to_all | solution.py:454
  30.6 0.4 %turn.1 = (bf16[64,384]{1,0:T(8,128)(2,1)S(1)}, bf16[64,384]{1,0:T(8,128)(2,1)S(1)}, bf16[64,384]{1,0:T(8,128)(2,1)S(1)}, bf16[64,384]{1,0:T(8,128)(2,1)S(1)}) custom-call(s32[1]{0:T(128)} %bitcast.me_ref, bf16[8,64,128]{2,1,0:T(8,128)(2,1)S(1)} %all_to_all.11.got_ref, bf16[1024,128]{1,0:T(8,128)(2,1)S(1)} %get-tuple-element.37.w_ref), custom_call_target="tpu_custom_call" | custom-call | tf_op jit(solution)/shard_map/turn/pallas_call | solution.py:336
  31.0 0.1 collective-permute-start.1
  31.1 2.3 %collective-permute-start.2 = (bf16[64,384]{1,0:T(8,128)(2,1)S(1)}, bf16[64,384]{1,0:T(8,128)(2,1)S(1)}, u32[]{:S(2)}, u32[]{:S(2)}) collective-permute-start(bf16[64,384]{1,0:T(8,128)(2,1)S(1)} %get-tuple-element.40), channel_id=1, source_target_pairs={{0,16},{8,24},{16,0},{24,8},{1,17},{9,25},{17,1},{25,9},{2,18},{10... | collective-permute-start | bytes 147464 | tf_op jit(solution)/shard_map/ppermute | solution.py:466
  33.4 1.5 %collective-permute-start.3 = (bf16[64,384]{1,0:T(8,128)(2,1)S(1)}, bf16[64,384]{1,0:T(8,128)(2,1)S(1)}, u32[]{:S(2)}, u32[]{:S(2)}) collective-permute-start(bf16[64,384]{1,0:T(8,128)(2,1)S(1)} %get-tuple-element.41), channel_id=1, source_target_pairs={{0,24},{8,0},{16,8},{24,16},{1,25},{9,1},{17,9},{25,17},{2,26},{10... | collective-permute-start | bytes 147464 | tf_op jit(solution)/shard_map/ppermute | solution.py:466
  34.9 2.2 %collective-permute-done.1.refs_1_ = bf16[64,384]{1,0:T(8,128)(2,1)S(1)} collective-permute-done((bf16[64,384]{1,0:T(8,128)(2,1)S(1)}, bf16[64,384]{1,0:T(8,128)(2,1)S(1)}, u32[]{:S(2)}, u32[]{:S(2)}) %collective-permute-start.1) | collective-permute-done | bytes 49184 | tf_op jit(solution)/shard_map/ppermute | solution.py:466
  37.1 0.7 %collective-permute-done.2.refs_2_ = bf16[64,384]{1,0:T(8,128)(2,1)S(1)} collective-permute-done((bf16[64,384]{1,0:T(8,128)(2,1)S(1)}, bf16[64,384]{1,0:T(8,128)(2,1)S(1)}, u32[]{:S(2)}, u32[]{:S(2)}) %collective-permute-start.2) | collective-permute-done | bytes 49184 | tf_op jit(solution)/shard_map/ppermute | solution.py:466
  37.8 0.0 collective-permute-done.3.refs_3_
  37.8 3.3 %col_scan.1 = bf16[32,8,256]{2,1,0:T(8,128)(2,1)} custom-call(s32[1]{0:T(128)} %bitcast.me_ref, bf16[64,384]{1,0:T(8,128)(2,1)S(1)} %get-tuple-element.38.refs_0_, bf16[64,384]{1,0:T(8,128)(2,1)S(1)} %collective-permute-done.1.refs_1_, bf16[64,384]{1,0:T(8,128)(2,1)S(1)} %collective-permute-done.2.refs_2_, ...), custom_call_target="tpu_custom_call" | custom-call | tf_op jit(solution)/shard_map/col_scan/pallas_call | solution.py:336
Async XLA Ops:
  16.6 5.8 %collective-permute-start = (bf16[2,64,128]{2,1,0:T(8,128)(2,1)S(1)}, bf16[2,64,128]{2,1,0:T(8,128)(2,1)S(1)}, u32[]{:S(2)}, u32[]{:S(2)}) collective-permute-start(bf16[2,64,128]{2,1,0:T(8,128)(2,1)S(1)} %get-tuple-element.34), channel_id=1, source_target_pairs={{0,8},{8,16},{16,24},{24,0},{1,9},{9,17},{17,25},{25,1},{2,10},{10... | collective-permute-start | bytes 98312 | tf_op jit(solution)/shard_map/ppermute | solution.py:429
  31.0 6.1 %collective-permute-start.1 = (bf16[64,384]{1,0:T(8,128)(2,1)S(1)}, bf16[64,384]{1,0:T(8,128)(2,1)S(1)}, u32[]{:S(2)}, u32[]{:S(2)}) collective-permute-start(bf16[64,384]{1,0:T(8,128)(2,1)S(1)} %get-tuple-element.39), channel_id=1, source_target_pairs={{0,8},{8,16},{16,24},{24,0},{1,9},{9,17},{17,25},{25,1},{2,10},{10... | collective-permute-start | bytes 147464 | tf_op jit(solution)/shard_map/ppermute | solution.py:466
  31.1 6.7 %collective-permute-start.2 = (bf16[64,384]{1,0:T(8,128)(2,1)S(1)}, bf16[64,384]{1,0:T(8,128)(2,1)S(1)}, u32[]{:S(2)}, u32[]{:S(2)}) collective-permute-start(bf16[64,384]{1,0:T(8,128)(2,1)S(1)} %get-tuple-element.40), channel_id=1, source_target_pairs={{0,16},{8,24},{16,0},{24,8},{1,17},{9,25},{17,1},{25,9},{2,18},{10... | collective-permute-start | bytes 147464 | tf_op jit(solution)/shard_map/ppermute | solution.py:466
  33.4 4.3 %collective-permute-start.3 = (bf16[64,384]{1,0:T(8,128)(2,1)S(1)}, bf16[64,384]{1,0:T(8,128)(2,1)S(1)}, u32[]{:S(2)}, u32[]{:S(2)}) collective-permute-start(bf16[64,384]{1,0:T(8,128)(2,1)S(1)} %get-tuple-element.41), channel_id=1, source_target_pairs={{0,24},{8,0},{16,8},{24,16},{1,25},{9,1},{17,9},{25,17},{2,26},{10... | collective-permute-start | bytes 147464 | tf_op jit(solution)/shard_map/ppermute | solution.py:466

commit v5 on v4

--- a/solution.py
+++ b/solution.py
@@ -42,10 +42,15 @@
     return copies
 
 
-def pack_kernel(feat_hbm, gate_hbm, w_hbm, *refs):
-    count = (len(refs) - 5) // 2
-    param_refs, (out_ref, *held_refs) = refs[:count], refs[count : 2 * count + 1]
-    feat_ref, gate_ref, w_ref, sems = refs[2 * count + 1 :]
+def there(spot, shift):
+    return spot // 2 ^ shift
+
+
+def pack_kernel(spot_ref, feat_hbm, gate_hbm, w_hbm, *refs, chips):
+    count = (len(refs) - 5 - chips) // 2
+    param_refs, held_refs = refs[:count], refs[count + chips : 2 * count + chips]
+    send_refs = refs[count : count + chips]
+    feat_ref, gate_ref, w_ref, out_ref, sems = refs[2 * count + chips :]
     copies = fetches((feat_hbm, w_hbm, gate_hbm, *param_refs), (feat_ref, w_ref, gate_ref, *held_refs), sems)
     rows, cols, channels = feat_ref.shape
     tokens = rows * cols
@@ -65,8 +70,19 @@
     moved = dot(order, gate_ref[...].reshape(tokens, channels)).astype(BF16)
     for part in range(parts):
         out_ref[part, :, share : 2 * share] = moved[:, part * share : (part + 1) * share]
+    spot = spot_ref[0]
+    for shift in range(chips):
+        for other in range(2):
+            send_refs[shift][other] = out_ref[there(spot, shift) * 2 + (spot % 2 ^ other)]
     for copy in copies[3:]:
         copy.wait()
+
+
+def gathered(spot, refs, put):
+    chips = len(refs) // 2
+    for shift in range(chips):
+        for other in range(2):
+            put(there(spot, shift) * 2 + (spot % 2 ^ other), refs[other * chips + shift][other])
 
 
 def one_hot(height, width, hit):
@@ -221,29 +237,37 @@
         out_ref[p] = gated.astype(BF16)
 
 
-def upper_kernel(got_ref, w_dt_ref, bias_ref, rate_ref, skip_ref, *refs):
-    *scratch, sems = refs[-6:]
-    count = (len(refs) - 11) // 2
-    out_ref, tail_ref, wide_ref, rates_ref, pick_ref, *held_refs = refs[count:-6]
-    copies = fetches(refs[:count], held_refs, sems)
+def upper_kernel(spot_ref, *refs, sources):
+    block_refs, (w_dt_ref, bias_ref, rate_ref, skip_ref), refs = refs[:sources], refs[sources : sources + 4], refs[sources + 4 :]
+    out_ref, tail_ref, wide_ref, rates_ref, pick_ref, got_ref, *scratch = refs
     positions, lines, share = out_ref.shape
+    cols = positions // sources
+
+    def put(place, block):
+        got_ref[pl.ds(place * cols, cols)] = block.reshape(cols, lines, block.shape[1])
+
+    gathered(spot_ref[0], block_refs, put)
     row_tables(w_dt_ref, rate_ref, wide_ref, rates_ref, pick_ref)
     half_rows(True, w_dt_ref.shape[1], got_ref, bias_ref, skip_ref, wide_ref, rates_ref, pick_ref, out_ref, scratch)
     flat_ref = scratch[1].reshape(positions * lines, share)
     for j in range(2):
         tail_ref[j] = flat_ref[pl.ds(lines - 2 + j, positions, stride=lines), :].astype(BF16)
+
+
+def lower_kernel(got_ref, bias_ref, skip_ref, wide_ref, rates_ref, pick_ref, *refs, rank):
+    *scratch, sems = refs[-6:]
+    count = (len(refs) - 7) // 2
+    out_ref, *held_refs = refs[count:-6]
+    copies = fetches(refs[:count], held_refs, sems)
+    half_rows(False, rank, got_ref, bias_ref, skip_ref, wide_ref, rates_ref, pick_ref, out_ref, scratch)
     for copy in copies:
         copy.wait()
 
 
-def lower_kernel(got_ref, bias_ref, skip_ref, wide_ref, rates_ref, pick_ref, out_ref, *scratch, rank):
-    half_rows(False, rank, got_ref, bias_ref, skip_ref, wide_ref, rates_ref, pick_ref, out_ref, scratch)
-
-
-def conv_kernel(me_ref, lower_ref, upper_ref, above_ref, taps_ref, bias_ref, out_ref, pad_ref):
+def conv_kernel(me_ref, spot_ref, lower_ref, upper_ref, above_ref, taps_ref, bias_ref, *refs):
+    *send_refs, pad_ref = refs
     positions, lines, share = lower_ref.shape
-    parts = out_ref.shape[0]
-    cols = positions // parts
+    cols = positions // (2 * len(send_refs))
     height = pad_ref.shape[1]
     top = height - lines
     zero_edge = jnp.zeros((1, height, share), F32)
@@ -263,29 +287,33 @@
         taps.append(wide if beyond[i] is None else [jnp.where(beyond[i], 0.0, tap) for tap in wide])
     bias = jnp.broadcast_to(bias_ref[...], (lines, share))
 
-    def block(part, _):
-        start = part * cols
-        for w in range(cols):
-            total = bias
-            for i in range(3):
-                for j in range(3):
-                    total = total + taps[i][j] * pad_ref[start + w + j, top - 2 + i : top - 2 + i + lines, :]
-            out_ref[part, w * lines : (w + 1) * lines, :] = silu(total).astype(BF16)
-        return 0
-
-    lax.fori_loop(0, parts, block, 0, unroll=2)
-
-
-def turn_kernel(me_ref, got_ref, w_ref, *out_refs, rows):
+    spot = spot_ref[0]
+    for shift, send_ref in enumerate(send_refs):
+        for other in range(2):
+            start = (there(spot, shift) * 2 + (spot % 2 ^ other)) * cols
+            for w in range(cols):
+                total = bias
+                for i in range(3):
+                    for j in range(3):
+                        total = total + taps[i][j] * pad_ref[start + w + j, top - 2 + i : top - 2 + i + lines, :]
+                send_ref[other, w * lines : (w + 1) * lines, :] = silu(total).astype(BF16)
+
+
+def turn_kernel(me_ref, spot_ref, *refs, sources, rows):
+    block_refs, w_ref, out_refs, got_ref = refs[:sources], refs[sources], refs[sources + 1 : -1], refs[-1]
     parts, tokens, share = got_ref.shape
     width = w_ref.shape[1]
     count = len(out_refs)
     each = parts // count
     order = shuffle(tokens, rows, tokens // rows)
-    total = jnp.zeros((tokens, width), F32)
-    for part in range(parts):
-        total = total + dot(got_ref[part], w_ref[pl.ds(part * share, share), :])
-    proj = dot(order, total.astype(BF16)).astype(BF16)
+    sums = []
+
+    def put(place, block):
+        got_ref[place] = block
+        sums.append(dot(block, w_ref[pl.ds(pl.multiple_of(place * share, share), share), :]))
+
+    gathered(spot_ref[0], block_refs, put)
+    proj = dot(order, sum(sums).astype(BF16)).astype(BF16)
     me = me_ref[0]
     for shift in range(count):
         to = lax.rem(me + shift, count)
@@ -379,6 +407,16 @@
     line, column = cols * n_col, rows * n_row
     tokens = rows * cols
     me = lax.axis_index("row").astype(jnp.int32).reshape(1)
+    spot = lax.axis_index("col").astype(jnp.int32).reshape(1)
+    chips = n_col // 2
+
+    def exchange(pieces):
+        pieces = [pieces[0]] + [
+            lax.ppermute(pieces[s], "col", [(i, (i // 2 ^ s) * 2 + i % 2) for i in range(n_col)]) for s in range(1, chips)
+        ]
+        passed = [lax.ppermute(piece, "col", [(i, i ^ 1) for i in range(n_col)]) for piece in pieces]
+        return [near(piece) for piece in pieces + passed]
+
 
     row_params = (w_dt_row, dt_bias_row, jnp.swapaxes(rate_row, 1, 2), skip_row.reshape(1, share))
     params = (
@@ -389,20 +427,23 @@
         dt_bias_col,
         jnp.swapaxes(rate_col, 1, 2),
     )
-    sent, *row_params = call(
-        pack_kernel,
+    sent = call(
+        functools.partial(pack_kernel, chips=chips),
         "pack",
-        [array((n_col, tokens, 2 * share + width))] + [like(p) for p in row_params],
+        [array((2, tokens, 2 * share + width))] * chips + [like(p) for p in row_params],
         [
             pltpu.VMEM(features.shape, BF16),
             pltpu.VMEM(gate_branch.shape, BF16),
             pltpu.VMEM(w_row_proj.shape, BF16),
+            pltpu.VMEM((n_col, tokens, 2 * share + width), BF16),
             pltpu.SemaphoreType.DMA((3 + len(row_params),)),
         ],
+        spot,
+        scalars=1,
         far=(features, gate_branch, w_row_proj, *row_params),
     )
-    got = lax.all_to_all(sent, "col", 0, 0, tiled=True)
-    got = near(got.reshape(line, rows, 2 * share + width))
+    sent, row_params = sent[:chips], sent[chips:]
+    blocks = exchange(sent)
     scratch = [
         pltpu.VMEM((line, rows, share), F32),
         pltpu.VMEM((line, rows, share), F32),
@@ -410,8 +451,8 @@
         pltpu.VMEM((line * rows, 2 * state), BF16),
         pltpu.VMEM((line, rows, share), F32),
     ]
-    upper, tail, wide, rates, pick, *params = call(
-        upper_kernel,
+    upper, tail, wide, rates, pick, got = call(
+        functools.partial(upper_kernel, sources=n_col),
         "upper_rows",
         [
             array((line, rows, share)),
@@ -419,48 +460,52 @@
             array((width, 2 * share)),
             array((state, rows, share), F32),
             array((state, 2 * state, 2 * LANES)),
-        ]
-        + [like(p) for p in params],
-        scratch + [pltpu.SemaphoreType.DMA((len(params),))],
-        got,
+            array((line, rows, 2 * share + width)),
+        ],
+        scratch,
+        spot,
+        *blocks,
         *row_params,
-        far=params,
+        scalars=1,
     )
     above = lax.ppermute(tail, "row", [(i, (i + 1) % n_row) for i in range(n_row)])
-    lower = call(
+    lower, *params = call(
         functools.partial(lower_kernel, rank=w_dt_row.shape[1]),
         "lower_rows",
-        array((line, rows, share)),
-        scratch,
-        got,
+        [array((line, rows, share))] + [like(p) for p in params],
+        scratch + [pltpu.SemaphoreType.DMA((len(params),))],
+        near(got),
         row_params[1],
         row_params[3],
         near(wide),
         near(rates),
         near(pick),
+        far=params,
     )
     sent = call(
         conv_kernel,
         "conv",
-        array((n_col, tokens, share)),
+        [array((2, tokens, share))] * chips,
         [pltpu.VMEM((line + 2, rows + 8, share), F32)],
         me,
+        spot,
         near(lower),
         near(upper),
         near(above),
         *params[:2],
-        scalars=1,
-    )
-    got = lax.all_to_all(sent, "col", 0, 0, tiled=True)
+        scalars=2,
+    )
+    blocks = exchange(sent)
     pieces = call(
-        functools.partial(turn_kernel, rows=rows),
+        functools.partial(turn_kernel, sources=n_col, rows=rows),
         "turn",
         [array((tokens, col_share + width))] * n_row,
-        [],
+        [pltpu.VMEM((n_col, tokens, share), BF16)],
         me,
-        near(got),
+        spot,
+        *blocks,
         params[2],
-        scalars=1,
+        scalars=2,
     )
     pieces = [pieces[0]] + [
         lax.ppermute(pieces[s], "row", [(i, (i + s) % n_row) for i in range(n_row)]) for s in range(1, n_row)

time: 41.3 us -> 40 us (0.969)
  blocking collectives: 21.2 us -> 0 us
  waiting for transfers between devices: 5.49 us -> 17.2 us
  starting transfers between devices: 5.51 us -> 13.7 us
    all_to_all x2 -> x0, blocking collectives: 21.2 us -> none  [local(): got = lax.all_to_all(sent, 'col', 0, 0, tiled=True)]
    ppermute x0 -> x14, waiting for transfers between devices: none -> 10.9 us  [the longest x6 8.38 us: exchange(): lax.ppermute(pieces[s], 'col', [(i, (i // 2 ^ s) * 2 + i % 2) for i in ra...]
    ppermute x0 -> x14, starting transfers between devices: none -> 8.24 us  [the longest x6 8.13 us: exchange(): lax.ppermute(pieces[s], 'col', [(i, (i // 2 ^ s) * 2 + i % 2) for i in ra...]
    ppermute x3, waiting for transfers between devices: 2.87 us -> 3.75 us  [local(): lax.ppermute(pieces[s], 'row', [(i, (i + s) % n_row) for i in range(n_row)])]
  transfers between devices with their start and end apart: 4 -> 18, of which waited for: 3 -> 11; matrix products, arithmetic and copies ran while one was open for 0% -> 0% of each run, Pallas kernels for 4% -> 4%
where the time goes in v5:
time: 40 us; the launch traced here: 39.8 us
  waiting for transfers between devices  17.2 us (43%)
  starting transfers between devices  13.7 us (34%)
  Pallas kernels  8.85 us (22%)
    pallas_call x6, Pallas kernels, call(): pl.pallas_call(kernel, name=name, out_shape=outs, in_specs=[smem()] * sca...  8.85 us
    ppermute x6, waiting for transfers between devices, exchange(): lax.ppermute(pieces[s], 'col', [(i, (i // 2 ^ s) * 2 + i % 2) for i in ra...  8.38 us
    ppermute x6, starting transfers between devices, exchange(): lax.ppermute(pieces[s], 'col', [(i, (i // 2 ^ s) * 2 + i % 2) for i in ra...  8.13 us
    ppermute x3, starting transfers between devices, local(): lax.ppermute(pieces[s], 'row', [(i, (i + s) % n_row) for i in range(n_row)])  3.87 us
    ppermute x3, waiting for transfers between devices, local(): lax.ppermute(pieces[s], 'row', [(i, (i + s) % n_row) for i in range(n_row)])  3.75 us
    ppermute x1, waiting for transfers between devices, local(): lax.ppermute(tail, 'row', [(i, (i + 1) % n_row) for i in range(n_row)])  2.56 us
    ppermute x8, waiting for transfers between devices, exchange(): lax.ppermute(piece, 'col', [(i, i ^ 1) for i in range(n_col)])  2.48 us
    ppermute x1, starting transfers between devices, local(): lax.ppermute(tail, 'row', [(i, (i + 1) % n_row) for i in range(n_row)])  1.63 us
  transfers between devices with their start and end apart: 18, of which 11 were waited for; matrix products, arithmetic and copies ran while one was open for 0% of the time, Pallas kernels for 4%

profile of v5, /device:TPU:0, one launch (start us, length us, event | category | flops | bytes accessed | tf_op | source)
XLA Modules:
  0.0 39.8 jit_solution(2409465616297902818)
XLA Ops:
  0.0 1.7 %pack.1 = (bf16[2,64,384]{2,1,0:T(8,128)(2,1)S(1)}, bf16[2,64,384]{2,1,0:T(8,128)(2,1)S(1)}, bf16[2,64,384]{2,1,0:T(8,128)(2,1)S(1)}, bf16[2,64,384]{2,1,0:T(8,1...) custom-call(s32[1]{0:T(128)} %bitcast.1.spot_ref, ...), custom_call_target="tpu_custom_call" | custom-call | tf_op jit(solution)/shard_map/pack/pallas_call | solution.py:364
  1.7 3.0 %collective-permute-start = (bf16[2,64,384]{2,1,0:T(8,128)(2,1)S(1)}, bf16[2,64,384]{2,1,0:T(8,128)(2,1)S(1)}, u32[]{:S(2)}, u32[]{:S(2)}) collective-permute-start(bf16[2,64,384]{2,1,0:T(8,128)(2,1)S(1)} %get-tuple-element.35), channel_id=1, source_target_pairs={{0,2},{1,3},{2,0},{3,1},{4,6},{5,7},{6,4},{7,5},{8,10},{9,11},{10,... | collective-permute-start | bytes 294920 | tf_op jit(solution)/shard_map/ppermute | solution.py:415
  4.7 1.5 %collective-permute-start.1 = (bf16[2,64,384]{2,1,0:T(8,128)(2,1)S(1)}, bf16[2,64,384]{2,1,0:T(8,128)(2,1)S(1)}, u32[]{:S(2)}, u32[]{:S(2)}) collective-permute-start(bf16[2,64,384]{2,1,0:T(8,128)(2,1)S(1)} %get-tuple-element.36), channel_id=1, source_target_pairs={{0,4},{1,5},{2,6},{3,7},{4,0},{5,1},{6,2},{7,3},{8,12},{9,13},{10,... | collective-permute-start | bytes 294920 | tf_op jit(solution)/shard_map/ppermute | solution.py:415
  6.2 1.5 %collective-permute-done.refs_1_ = bf16[2,64,384]{2,1,0:T(8,128)(2,1)S(1)} collective-permute-done((bf16[2,64,384]{2,1,0:T(8,128)(2,1)S(1)}, bf16[2,64,384]{2,1,0:T(8,128)(2,1)S(1)}, u32[]{:S(2)}, u32[]{:S(2)}) %collective-permute-start) | collective-permute-done | bytes 98336 | tf_op jit(solution)/shard_map/ppermute | solution.py:415
  7.8 2.6 %collective-permute-done.1.refs_2_ = bf16[2,64,384]{2,1,0:T(8,128)(2,1)S(1)} collective-permute-done((bf16[2,64,384]{2,1,0:T(8,128)(2,1)S(1)}, bf16[2,64,384]{2,1,0:T(8,128)(2,1)S(1)}, u32[]{:S(2)}, u32[]{:S(2)}) %collective-permute-start.1) | collective-permute-done | bytes 98336 | tf_op jit(solution)/shard_map/ppermute | solution.py:415
  10.4 1.4 %collective-permute-done.2.refs_3_ = bf16[2,64,384]{2,1,0:T(8,128)(2,1)S(1)} collective-permute-done((bf16[2,64,384]{2,1,0:T(8,128)(2,1)S(1)}, bf16[2,64,384]{2,1,0:T(8,128)(2,1)S(1)}, u32[]{:S(2)}, u32[]{:S(2)}) %collective-permute-start.2) | collective-permute-done | bytes 98336 | tf_op jit(solution)/shard_map/ppermute | solution.py:415
  11.8 1.3 %collective-permute-done.6.refs_7_ = bf16[2,64,384]{2,1,0:T(8,128)(2,1)S(1)} collective-permute-done((bf16[2,64,384]{2,1,0:T(8,128)(2,1)S(1)}, bf16[2,64,384]{2,1,0:T(8,128)(2,1)S(1)}, u32[]{:S(2)}, u32[]{:S(2)}) %collective-permute-start.6) | collective-permute-done | bytes 98336 | tf_op jit(solution)/shard_map/ppermute | solution.py:417
  13.0 1.6 %upper_rows.1 = (bf16[64,8,128]{2,1,0:T(8,128)(2,1)S(1)}, bf16[2,64,128]{2,1,0:T(8,128)(2,1)S(1)}, bf16[128,256]{1,0:T(8,128)(2,1)S(1)}, f32[16,8,128]{2,1,0:T(8...) custom-call(s32[1]{0:T(128)} %bitcast.1.spot_ref, ...), custom_call_target="tpu_custom_call" | custom-call | tf_op jit(solution)/shard_map/upper_rows/pallas_call | solution.py:364
  14.7 1.6 %collective-permute-start.7 = (bf16[2,64,128]{2,1,0:T(8,128)(2,1)S(1)}, bf16[2,64,128]{2,1,0:T(8,128)(2,1)S(1)}, u32[]{:S(2)}, u32[]{:S(2)}) collective-permute-start(bf16[2,64,128]{2,1,0:T(8,128)(2,1)S(1)} %get-tuple-element.48), channel_id=1, source_target_pairs={{0,8},{8,16},{16,24},{24,0},{1,9},{9,17},{17,25},{25,1},{2,10},{10... | collective-permute-start | bytes 98312 | tf_op jit(solution)/shard_map/ppermute | solution.py:471
  16.3 1.6 %lower_rows.1 = (bf16[64,8,128]{2,1,0:T(8,128)(2,1)S(1)}, f32[3,3,128]{2,1,0:T(4,128)S(1)}, f32[1,128]{1,0:T(1,128)S(1)}, bf16[1024,128]{1,0:T(8,128)(2,1)S(1)},...) custom-call(bf16[64,8,384]{2,1,0:T(8,128)(2,1)S(1)} %get-tuple-element.42.got_ref, ...), custom_call_target="tpu_custom_call" | custom-call | tf_op jit(solution)/shard_map/lower_rows/pallas_call | solution.py:364
  17.9 2.6 %collective-permute-done.7.above_ref = bf16[2,64,128]{2,1,0:T(8,128)(2,1)S(1)} collective-permute-done((bf16[2,64,128]{2,1,0:T(8,128)(2,1)S(1)}, bf16[2,64,128]{2,1,0:T(8,128)(2,1)S(1)}, u32[]{:S(2)}, u32[]{:S(2)}) %collective-permute-start.7) | collective-permute-done | bytes 32800 | tf_op jit(solution)/shard_map/ppermute | solution.py:471
  20.7 0.7 %collective-permute-start.8 = (bf16[2,64,128]{2,1,0:T(8,128)(2,1)S(1)}, bf16[2,64,128]{2,1,0:T(8,128)(2,1)S(1)}, u32[]{:S(2)}, u32[]{:S(2)}) collective-permute-start(bf16[2,64,128]{2,1,0:T(8,128)(2,1)S(1)} %get-tuple-element.52), channel_id=1, source_target_pairs={{0,2},{1,3},{2,0},{3,1},{4,6},{5,7},{6,4},{7,5},{8,10},{9,11},{10,... | collective-permute-start | bytes 98312 | tf_op jit(solution)/shard_map/ppermute | solution.py:415
  21.4 1.0 %collective-permute-start.9 = (bf16[2,64,128]{2,1,0:T(8,128)(2,1)S(1)}, bf16[2,64,128]{2,1,0:T(8,128)(2,1)S(1)}, u32[]{:S(2)}, u32[]{:S(2)}) collective-permute-start(bf16[2,64,128]{2,1,0:T(8,128)(2,1)S(1)} %get-tuple-element.53), channel_id=1, source_target_pairs={{0,4},{1,5},{2,6},{3,7},{4,0},{5,1},{6,2},{7,3},{8,12},{9,13},{10,... | collective-permute-start | bytes 98312 | tf_op jit(solution)/shard_map/ppermute | solution.py:415
  22.5 1.8 %collective-permute-start.10 = (bf16[2,64,128]{2,1,0:T(8,128)(2,1)S(1)}, bf16[2,64,128]{2,1,0:T(8,128)(2,1)S(1)}, u32[]{:S(2)}, u32[]{:S(2)}) collective-permute-start(bf16[2,64,128]{2,1,0:T(8,128)(2,1)S(1)} %get-tuple-element.54), channel_id=1, source_target_pairs={{0,6},{1,7},{2,4},{3,5},{4,2},{5,3},{6,0},{7,1},{8,14},{9,15},{10,... | collective-permute-start | bytes 98312 | tf_op jit(solution)/shard_map/ppermute | solution.py:415
  24.3 0.4 %collective-permute-done.8.refs_1_ = bf16[2,64,128]{2,1,0:T(8,128)(2,1)S(1)} collective-permute-done((bf16[2,64,128]{2,1,0:T(8,128)(2,1)S(1)}, bf16[2,64,128]{2,1,0:T(8,128)(2,1)S(1)}, u32[]{:S(2)}, u32[]{:S(2)}) %collective-permute-start.8) | collective-permute-done | bytes 32800 | tf_op jit(solution)/shard_map/ppermute | solution.py:415
  24.8 0.7 %collective-permute-done.9.refs_2_ = bf16[2,64,128]{2,1,0:T(8,128)(2,1)S(1)} collective-permute-done((bf16[2,64,128]{2,1,0:T(8,128)(2,1)S(1)}, bf16[2,64,128]{2,1,0:T(8,128)(2,1)S(1)}, u32[]{:S(2)}, u32[]{:S(2)}) %collective-permute-start.9) | collective-permute-done | bytes 32800 | tf_op jit(solution)/shard_map/ppermute | solution.py:415
  25.5 1.8 %collective-permute-done.10.refs_3_ = bf16[2,64,128]{2,1,0:T(8,128)(2,1)S(1)} collective-permute-done((bf16[2,64,128]{2,1,0:T(8,128)(2,1)S(1)}, bf16[2,64,128]{2,1,0:T(8,128)(2,1)S(1)}, u32[]{:S(2)}, u32[]{:S(2)}) %collective-permute-start.10) | collective-permute-done | bytes 32800 | tf_op jit(solution)/shard_map/ppermute | solution.py:415
  27.3 1.2 %collective-permute-done.14.refs_7_ = bf16[2,64,128]{2,1,0:T(8,128)(2,1)S(1)} collective-permute-done((bf16[2,64,128]{2,1,0:T(8,128)(2,1)S(1)}, bf16[2,64,128]{2,1,0:T(8,128)(2,1)S(1)}, u32[]{:S(2)}, u32[]{:S(2)}) %collective-permute-start.14) | collective-permute-done | bytes 32800 | tf_op jit(solution)/shard_map/ppermute | solution.py:417
  28.5 0.4 %turn.1 = (bf16[64,384]{1,0:T(8,128)(2,1)S(1)}, bf16[64,384]{1,0:T(8,128)(2,1)S(1)}, bf16[64,384]{1,0:T(8,128)(2,1)S(1)}, bf16[64,384]{1,0:T(8,128)(2,1)S(1)}) custom-call(s32[1]{0:T(128)} %bitcast.me_ref, s32[1]{0:T(128)} %bitcast.1.spot_ref, bf16[2,64,128]{2,1,0:T(8,128)(2,1)S(1)} %get-tuple-element.51.refs_0_, ...), custom_call_target="tpu_custom_call" | custom-call | tf_op jit(solution)/shard_map/turn/pallas_call | solution.py:364
  29.0 2.4 %collective-permute-start.16 = (bf16[64,384]{1,0:T(8,128)(2,1)S(1)}, bf16[64,384]{1,0:T(8,128)(2,1)S(1)}, u32[]{:S(2)}, u32[]{:S(2)}) collective-permute-start(bf16[64,384]{1,0:T(8,128)(2,1)S(1)} %get-tuple-element.58), channel_id=1, source_target_pairs={{0,16},{8,24},{16,0},{24,8},{1,17},{9,25},{17,1},{25,9},{2,18},{10... | collective-permute-start | bytes 147464 | tf_op jit(solution)/shard_map/ppermute | solution.py:511
  31.4 1.4 %collective-permute-start.17 = (bf16[64,384]{1,0:T(8,128)(2,1)S(1)}, bf16[64,384]{1,0:T(8,128)(2,1)S(1)}, u32[]{:S(2)}, u32[]{:S(2)}) collective-permute-start(bf16[64,384]{1,0:T(8,128)(2,1)S(1)} %get-tuple-element.59), channel_id=1, source_target_pairs={{0,24},{8,0},{16,8},{24,16},{1,25},{9,1},{17,9},{25,17},{2,26},{10... | collective-permute-start | bytes 147464 | tf_op jit(solution)/shard_map/ppermute | solution.py:511
  32.8 2.6 %collective-permute-done.15.refs_1_ = bf16[64,384]{1,0:T(8,128)(2,1)S(1)} collective-permute-done((bf16[64,384]{1,0:T(8,128)(2,1)S(1)}, bf16[64,384]{1,0:T(8,128)(2,1)S(1)}, u32[]{:S(2)}, u32[]{:S(2)}) %collective-permute-start.15) | collective-permute-done | bytes 49184 | tf_op jit(solution)/shard_map/ppermute | solution.py:511
  35.4 1.1 %collective-permute-done.16.refs_2_ = bf16[64,384]{1,0:T(8,128)(2,1)S(1)} collective-permute-done((bf16[64,384]{1,0:T(8,128)(2,1)S(1)}, bf16[64,384]{1,0:T(8,128)(2,1)S(1)}, u32[]{:S(2)}, u32[]{:S(2)}) %collective-permute-start.16) | collective-permute-done | bytes 49184 | tf_op jit(solution)/shard_map/ppermute | solution.py:511
  36.5 3.3 %col_scan.1 = bf16[32,8,256]{2,1,0:T(8,128)(2,1)} custom-call(s32[1]{0:T(128)} %bitcast.me_ref, bf16[64,384]{1,0:T(8,128)(2,1)S(1)} %get-tuple-element.56.refs_0_, bf16[64,384]{1,0:T(8,128)(2,1)S(1)} %collective-permute-done.15.refs_1_, bf16[64,384]{1,0:T(8,128)(2,1)S(1)} %collective-permute-done.16.refs_2_, ...), custom_call_target="tpu_custom_call" | custom-call | tf_op jit(solution)/shard_map/col_scan/pallas_call | solution.py:364
  (18 shorter events, 0.5 us)
Async XLA Ops:
  1.7 6.1 %collective-permute-start = (bf16[2,64,384]{2,1,0:T(8,128)(2,1)S(1)}, bf16[2,64,384]{2,1,0:T(8,128)(2,1)S(1)}, u32[]{:S(2)}, u32[]{:S(2)}) collective-permute-start(bf16[2,64,384]{2,1,0:T(8,128)(2,1)S(1)} %get-tuple-element.35), channel_id=1, source_target_pairs={{0,2},{1,3},{2,0},{3,1},{4,6},{5,7},{6,4},{7,5},{8,10},{9,11},{10,... | collective-permute-start | bytes 294920 | tf_op jit(solution)/shard_map/ppermute | solution.py:415
  4.7 5.7 %collective-permute-start.1 = (bf16[2,64,384]{2,1,0:T(8,128)(2,1)S(1)}, bf16[2,64,384]{2,1,0:T(8,128)(2,1)S(1)}, u32[]{:S(2)}, u32[]{:S(2)}) collective-permute-start(bf16[2,64,384]{2,1,0:T(8,128)(2,1)S(1)} %get-tuple-element.36), channel_id=1, source_target_pairs={{0,4},{1,5},{2,6},{3,7},{4,0},{5,1},{6,2},{7,3},{8,12},{9,13},{10,... | collective-permute-start | bytes 294920 | tf_op jit(solution)/shard_map/ppermute | solution.py:415
  6.2 5.5 %collective-permute-start.2 = (bf16[2,64,384]{2,1,0:T(8,128)(2,1)S(1)}, bf16[2,64,384]{2,1,0:T(8,128)(2,1)S(1)}, u32[]{:S(2)}, u32[]{:S(2)}) collective-permute-start(bf16[2,64,384]{2,1,0:T(8,128)(2,1)S(1)} %get-tuple-element.37), channel_id=1, source_target_pairs={{0,6},{1,7},{2,4},{3,5},{4,2},{5,3},{6,0},{7,1},{8,14},{9,15},{10,... | collective-permute-start | bytes 294920 | tf_op jit(solution)/shard_map/ppermute | solution.py:415
  6.2 5.5 %collective-permute-start.3 = (bf16[2,64,384]{2,1,0:T(8,128)(2,1)S(1)}, bf16[2,64,384]{2,1,0:T(8,128)(2,1)S(1)}, u32[]{:S(2)}, u32[]{:S(2)}) collective-permute-start(bf16[2,64,384]{2,1,0:T(8,128)(2,1)S(1)} %get-tuple-element.34.refs_0_), channel_id=1, source_target_pairs={{0,1},{1,0},{2,3},{3,2},{4,5},{5,4},{6,7},{7,6},{8,9},{9,8},{10,11... | collective-permute-start | bytes 294920 | tf_op jit(solution)/shard_map/ppermute | solution.py:417
  7.8 4.0 %collective-permute-start.4 = (bf16[2,64,384]{2,1,0:T(8,128)(2,1)S(1)}, bf16[2,64,384]{2,1,0:T(8,128)(2,1)S(1)}, u32[]{:S(2)}, u32[]{:S(2)}) collective-permute-start(bf16[2,64,384]{2,1,0:T(8,128)(2,1)S(1)} %collective-permute-done.refs_1_), channel_id=1, source_target_pairs={{0,1},{1,0},{2,3},{3,2},{4,5},{5,4},{6,7},{7,6},{8,9},{9,8},{10,11... | collective-permute-start | bytes 294920 | tf_op jit(solution)/shard_map/ppermute | solution.py:417
  10.4 1.4 %collective-permute-start.5 = (bf16[2,64,384]{2,1,0:T(8,128)(2,1)S(1)}, bf16[2,64,384]{2,1,0:T(8,128)(2,1)S(1)}, u32[]{:S(2)}, u32[]{:S(2)}) collective-permute-start(bf16[2,64,384]{2,1,0:T(8,128)(2,1)S(1)} %collective-permute-done.1.refs_2_), channel_id=1, source_target_pairs={{0,1},{1,0},{2,3},{3,2},{4,5},{5,4},{6,7},{7,6},{8,9},{9,8},{10,11... | collective-permute-start | bytes 294920 | tf_op jit(solution)/shard_map/ppermute | solution.py:417
  11.7 1.3 %collective-permute-start.6 = (bf16[2,64,384]{2,1,0:T(8,128)(2,1)S(1)}, bf16[2,64,384]{2,1,0:T(8,128)(2,1)S(1)}, u32[]{:S(2)}, u32[]{:S(2)}) collective-permute-start(bf16[2,64,384]{2,1,0:T(8,128)(2,1)S(1)} %collective-permute-done.2.refs_3_), channel_id=1, source_target_pairs={{0,1},{1,0},{2,3},{3,2},{4,5},{5,4},{6,7},{7,6},{8,9},{9,8},{10,11... | collective-permute-start | bytes 294920 | tf_op jit(solution)/shard_map/ppermute | solution.py:417
  14.7 5.8 %collective-permute-start.7 = (bf16[2,64,128]{2,1,0:T(8,128)(2,1)S(1)}, bf16[2,64,128]{2,1,0:T(8,128)(2,1)S(1)}, u32[]{:S(2)}, u32[]{:S(2)}) collective-permute-start(bf16[2,64,128]{2,1,0:T(8,128)(2,1)S(1)} %get-tuple-element.48), channel_id=1, source_target_pairs={{0,8},{8,16},{16,24},{24,0},{1,9},{9,17},{17,25},{25,1},{2,10},{10... | collective-permute-start | bytes 98312 | tf_op jit(solution)/shard_map/ppermute | solution.py:471
  20.7 4.0 %collective-permute-start.8 = (bf16[2,64,128]{2,1,0:T(8,128)(2,1)S(1)}, bf16[2,64,128]{2,1,0:T(8,128)(2,1)S(1)}, u32[]{:S(2)}, u32[]{:S(2)}) collective-permute-start(bf16[2,64,128]{2,1,0:T(8,128)(2,1)S(1)} %get-tuple-element.52), channel_id=1, source_target_pairs={{0,2},{1,3},{2,0},{3,1},{4,6},{5,7},{6,4},{7,5},{8,10},{9,11},{10,... | collective-permute-start | bytes 98312 | tf_op jit(solution)/shard_map/ppermute | solution.py:415
  21.4 4.1 %collective-permute-start.9 = (bf16[2,64,128]{2,1,0:T(8,128)(2,1)S(1)}, bf16[2,64,128]{2,1,0:T(8,128)(2,1)S(1)}, u32[]{:S(2)}, u32[]{:S(2)}) collective-permute-start(bf16[2,64,128]{2,1,0:T(8,128)(2,1)S(1)} %get-tuple-element.53), channel_id=1, source_target_pairs={{0,4},{1,5},{2,6},{3,7},{4,0},{5,1},{6,2},{7,3},{8,12},{9,13},{10,... | collective-permute-start | bytes 98312 | tf_op jit(solution)/shard_map/ppermute | solution.py:415
  22.5 4.8 %collective-permute-start.10 = (bf16[2,64,128]{2,1,0:T(8,128)(2,1)S(1)}, bf16[2,64,128]{2,1,0:T(8,128)(2,1)S(1)}, u32[]{:S(2)}, u32[]{:S(2)}) collective-permute-start(bf16[2,64,128]{2,1,0:T(8,128)(2,1)S(1)} %get-tuple-element.54), channel_id=1, source_target_pairs={{0,6},{1,7},{2,4},{3,5},{4,2},{5,3},{6,0},{7,1},{8,14},{9,15},{10,... | collective-permute-start | bytes 98312 | tf_op jit(solution)/shard_map/ppermute | solution.py:415
  24.3 3.0 %collective-permute-start.11 = (bf16[2,64,128]{2,1,0:T(8,128)(2,1)S(1)}, bf16[2,64,128]{2,1,0:T(8,128)(2,1)S(1)}, u32[]{:S(2)}, u32[]{:S(2)}) collective-permute-start(bf16[2,64,128]{2,1,0:T(8,128)(2,1)S(1)} %get-tuple-element.51.refs_0_), channel_id=1, source_target_pairs={{0,1},{1,0},{2,3},{3,2},{4,5},{5,4},{6,7},{7,6},{8,9},{9,8},{10,11... | collective-permute-start | bytes 98312 | tf_op jit(solution)/shard_map/ppermute | solution.py:417
  24.7 2.6 %collective-permute-start.12 = (bf16[2,64,128]{2,1,0:T(8,128)(2,1)S(1)}, bf16[2,64,128]{2,1,0:T(8,128)(2,1)S(1)}, u32[]{:S(2)}, u32[]{:S(2)}) collective-permute-start(bf16[2,64,128]{2,1,0:T(8,128)(2,1)S(1)} %collective-permute-done.8.refs_1_), channel_id=1, source_target_pairs={{0,1},{1,0},{2,3},{3,2},{4,5},{5,4},{6,7},{7,6},{8,9},{9,8},{10,11... | collective-permute-start | bytes 98312 | tf_op jit(solution)/shard_map/ppermute | solution.py:417
  25.5 1.8 %collective-permute-start.13 = (bf16[2,64,128]{2,1,0:T(8,128)(2,1)S(1)}, bf16[2,64,128]{2,1,0:T(8,128)(2,1)S(1)}, u32[]{:S(2)}, u32[]{:S(2)}) collective-permute-start(bf16[2,64,128]{2,1,0:T(8,128)(2,1)S(1)} %collective-permute-done.9.refs_2_), channel_id=1, source_target_pairs={{0,1},{1,0},{2,3},{3,2},{4,5},{5,4},{6,7},{7,6},{8,9},{9,8},{10,11... | collective-permute-start | bytes 98312 | tf_op jit(solution)/shard_map/ppermute | solution.py:417
  27.3 1.2 %collective-permute-start.14 = (bf16[2,64,128]{2,1,0:T(8,128)(2,1)S(1)}, bf16[2,64,128]{2,1,0:T(8,128)(2,1)S(1)}, u32[]{:S(2)}, u32[]{:S(2)}) collective-permute-start(bf16[2,64,128]{2,1,0:T(8,128)(2,1)S(1)} %collective-permute-done.10.refs_3_), channel_id=1, source_target_pairs={{0,1},{1,0},{2,3},{3,2},{4,5},{5,4},{6,7},{7,6},{8,9},{9,8},{10,11... | collective-permute-start | bytes 98312 | tf_op jit(solution)/shard_map/ppermute | solution.py:417
  28.9 6.5 %collective-permute-start.15 = (bf16[64,384]{1,0:T(8,128)(2,1)S(1)}, bf16[64,384]{1,0:T(8,128)(2,1)S(1)}, u32[]{:S(2)}, u32[]{:S(2)}) collective-permute-start(bf16[64,384]{1,0:T(8,128)(2,1)S(1)} %get-tuple-element.57), channel_id=1, source_target_pairs={{0,8},{8,16},{16,24},{24,0},{1,9},{9,17},{17,25},{25,1},{2,10},{10... | collective-permute-start | bytes 147464 | tf_op jit(solution)/shard_map/ppermute | solution.py:511
  29.0 7.6 %collective-permute-start.16 = (bf16[64,384]{1,0:T(8,128)(2,1)S(1)}, bf16[64,384]{1,0:T(8,128)(2,1)S(1)}, u32[]{:S(2)}, u32[]{:S(2)}) collective-permute-start(bf16[64,384]{1,0:T(8,128)(2,1)S(1)} %get-tuple-element.58), channel_id=1, source_target_pairs={{0,16},{8,24},{16,0},{24,8},{1,17},{9,25},{17,1},{25,9},{2,18},{10... | collective-permute-start | bytes 147464 | tf_op jit(solution)/shard_map/ppermute | solution.py:511
  31.4 5.1 %collective-permute-start.17 = (bf16[64,384]{1,0:T(8,128)(2,1)S(1)}, bf16[64,384]{1,0:T(8,128)(2,1)S(1)}, u32[]{:S(2)}, u32[]{:S(2)}) collective-permute-start(bf16[64,384]{1,0:T(8,128)(2,1)S(1)} %get-tuple-element.59), channel_id=1, source_target_pairs={{0,24},{8,0},{16,8},{24,16},{1,25},{9,1},{17,9},{25,17},{2,26},{10... | collective-permute-start | bytes 147464 | tf_op jit(solution)/shard_map/ppermute | solution.py:511

commit v6 on v5

--- a/solution.py
+++ b/solution.py
@@ -42,8 +42,16 @@
     return copies
 
 
+def shifts(chips):
+    return [0, *([chips - 1] if chips > 1 else []), *range(1, chips - 1)]
+
+
 def there(spot, shift):
     return spot // 2 ^ shift
+
+
+def place(spot, shift, other):
+    return there(spot, shift) * 2 + (spot % 2 ^ other)
 
 
 def pack_kernel(spot_ref, feat_hbm, gate_hbm, w_hbm, *refs, chips):
@@ -70,19 +78,18 @@
     moved = dot(order, gate_ref[...].reshape(tokens, channels)).astype(BF16)
     for part in range(parts):
         out_ref[part, :, share : 2 * share] = moved[:, part * share : (part + 1) * share]
-    spot = spot_ref[0]
-    for shift in range(chips):
+    for shift, send_ref in zip(shifts(chips), send_refs):
         for other in range(2):
-            send_refs[shift][other] = out_ref[there(spot, shift) * 2 + (spot % 2 ^ other)]
+            send_ref[other] = out_ref[place(spot_ref[0], shift, other)]
     for copy in copies[3:]:
         copy.wait()
 
 
 def gathered(spot, refs, put):
     chips = len(refs) // 2
-    for shift in range(chips):
+    for at, shift in enumerate(shifts(chips)):
         for other in range(2):
-            put(there(spot, shift) * 2 + (spot % 2 ^ other), refs[other * chips + shift][other])
+            put(place(spot, shift, other), refs[other * chips + at][other])
 
 
 def one_hot(height, width, hit):
@@ -243,8 +250,8 @@
     positions, lines, share = out_ref.shape
     cols = positions // sources
 
-    def put(place, block):
-        got_ref[pl.ds(place * cols, cols)] = block.reshape(cols, lines, block.shape[1])
+    def put(source, block):
+        got_ref[pl.ds(source * cols, cols)] = block.reshape(cols, lines, block.shape[1])
 
     gathered(spot_ref[0], block_refs, put)
     row_tables(w_dt_ref, rate_ref, wide_ref, rates_ref, pick_ref)
@@ -288,9 +295,9 @@
     bias = jnp.broadcast_to(bias_ref[...], (lines, share))
 
     spot = spot_ref[0]
-    for shift, send_ref in enumerate(send_refs):
+    for shift, send_ref in zip(shifts(len(send_refs)), send_refs):
         for other in range(2):
-            start = (there(spot, shift) * 2 + (spot % 2 ^ other)) * cols
+            start = place(spot, shift, other) * cols
             for w in range(cols):
                 total = bias
                 for i in range(3):
@@ -308,9 +315,9 @@
     order = shuffle(tokens, rows, tokens // rows)
     sums = []
 
-    def put(place, block):
-        got_ref[place] = block
-        sums.append(dot(block, w_ref[pl.ds(pl.multiple_of(place * share, share), share), :]))
+    def put(source, block):
+        got_ref[source] = block
+        sums.append(dot(block, w_ref[pl.ds(pl.multiple_of(source * share, share), share), :]))
 
     gathered(spot_ref[0], block_refs, put)
     proj = dot(order, sum(sums).astype(BF16)).astype(BF16)
@@ -412,7 +419,8 @@
 
     def exchange(pieces):
         pieces = [pieces[0]] + [
-            lax.ppermute(pieces[s], "col", [(i, (i // 2 ^ s) * 2 + i % 2) for i in range(n_col)]) for s in range(1, chips)
+            lax.ppermute(piece, "col", [(i, place(i, s, 0)) for i in range(n_col)])
+            for s, piece in list(zip(shifts(chips), pieces))[1:]
         ]
         passed = [lax.ppermute(piece, "col", [(i, i ^ 1) for i in range(n_col)]) for piece in pieces]
         return [near(piece) for piece in pieces + passed]

time: 40 us -> 39.4 us (0.985)
  waiting for transfers between devices: 17.2 us -> 16.1 us
  starting transfers between devices: 13.7 us -> 14.2 us
    ppermute x6, waiting for transfers between devices: 8.38 us -> 7.68 us  [exchange(): lax.ppermute(piece, 'col', [(i, place(i, s, 0)) for i in range(n_col)])]
    ppermute x8, starting transfers between devices: 0.11 us -> 0.53 us  [exchange(): lax.ppermute(piece, 'col', [(i, i ^ 1) for i in range(n_col)])]
  transfers between devices with their start and end apart: 18 -> 18, of which waited for: 11 -> 12; matrix products, arithmetic and copies ran while one was open for 0% -> 0% of each run, Pallas kernels for 4% -> 4%
where the time goes in v6:
time: 39.4 us; the launch traced here: 39.3 us
  waiting for transfers between devices  16.1 us (41%)
  starting transfers between devices  14.2 us (36%)
  Pallas kernels  8.85 us (22%)
    pallas_call x6, Pallas kernels, call(): pl.pallas_call(kernel, name=name, out_shape=outs, in_specs=[smem()] * sca...  8.85 us
    ppermute x6, starting transfers between devices, exchange(): lax.ppermute(piece, 'col', [(i, place(i, s, 0)) for i in range(n_col)])  8.19 us
    ppermute x6, waiting for transfers between devices, exchange(): lax.ppermute(piece, 'col', [(i, place(i, s, 0)) for i in range(n_col)])  7.68 us
    ppermute x3, starting transfers between devices, local(): lax.ppermute(pieces[s], 'row', [(i, (i + s) % n_row) for i in range(n_row)])  3.87 us
    ppermute x3, waiting for transfers between devices, local(): lax.ppermute(pieces[s], 'row', [(i, (i + s) % n_row) for i in range(n_row)])  3.75 us
    ppermute x1, waiting for transfers between devices, local(): lax.ppermute(tail, 'row', [(i, (i + 1) % n_row) for i in range(n_row)])  2.57 us
    ppermute x8, waiting for transfers between devices, exchange(): lax.ppermute(piece, 'col', [(i, i ^ 1) for i in range(n_col)])  2.14 us
    ppermute x1, starting transfers between devices, local(): lax.ppermute(tail, 'row', [(i, (i + 1) % n_row) for i in range(n_row)])  1.62 us
  transfers between devices with their start and end apart: 18, of which 12 were waited for; matrix products, arithmetic and copies ran while one was open for 0% of the time, Pallas kernels for 4%

profile of v6, /device:TPU:0, one launch (start us, length us, event | category | flops | bytes accessed | tf_op | source)
XLA Modules:
  0.0 39.3 jit_solution(16504617194976121780)
XLA Ops:
  0.0 1.7 %pack.1 = (bf16[2,64,384]{2,1,0:T(8,128)(2,1)S(1)}, bf16[2,64,384]{2,1,0:T(8,128)(2,1)S(1)}, bf16[2,64,384]{2,1,0:T(8,128)(2,1)S(1)}, bf16[2,64,384]{2,1,0:T(8,1...) custom-call(s32[1]{0:T(128)} %bitcast.1.spot_ref, ...), custom_call_target="tpu_custom_call" | custom-call | tf_op jit(solution)/shard_map/pack/pallas_call | solution.py:371
  1.7 4.0 %collective-permute-start = (bf16[2,64,384]{2,1,0:T(8,128)(2,1)S(1)}, bf16[2,64,384]{2,1,0:T(8,128)(2,1)S(1)}, u32[]{:S(2)}, u32[]{:S(2)}) collective-permute-start(bf16[2,64,384]{2,1,0:T(8,128)(2,1)S(1)} %get-tuple-element.35), channel_id=1, source_target_pairs={{0,6},{1,7},{2,4},{3,5},{4,2},{5,3},{6,0},{7,1},{8,14},{9,15},{10,... | collective-permute-start | bytes 294920 | tf_op jit(solution)/shard_map/ppermute | solution.py:422
  5.7 0.5 %collective-permute-start.1 = (bf16[2,64,384]{2,1,0:T(8,128)(2,1)S(1)}, bf16[2,64,384]{2,1,0:T(8,128)(2,1)S(1)}, u32[]{:S(2)}, u32[]{:S(2)}) collective-permute-start(bf16[2,64,384]{2,1,0:T(8,128)(2,1)S(1)} %get-tuple-element.36), channel_id=1, source_target_pairs={{0,2},{1,3},{2,0},{3,1},{4,6},{5,7},{6,4},{7,5},{8,10},{9,11},{10,... | collective-permute-start | bytes 294920 | tf_op jit(solution)/shard_map/ppermute | solution.py:422
  6.3 2.9 %collective-permute-done.refs_1_ = bf16[2,64,384]{2,1,0:T(8,128)(2,1)S(1)} collective-permute-done((bf16[2,64,384]{2,1,0:T(8,128)(2,1)S(1)}, bf16[2,64,384]{2,1,0:T(8,128)(2,1)S(1)}, u32[]{:S(2)}, u32[]{:S(2)}) %collective-permute-start) | collective-permute-done | bytes 98336 | tf_op jit(solution)/shard_map/ppermute | solution.py:422
  9.2 1.7 %collective-permute-done.1.refs_2_ = bf16[2,64,384]{2,1,0:T(8,128)(2,1)S(1)} collective-permute-done((bf16[2,64,384]{2,1,0:T(8,128)(2,1)S(1)}, bf16[2,64,384]{2,1,0:T(8,128)(2,1)S(1)}, u32[]{:S(2)}, u32[]{:S(2)}) %collective-permute-start.1) | collective-permute-done | bytes 98336 | tf_op jit(solution)/shard_map/ppermute | solution.py:422
  10.9 0.5 %collective-permute-start.6 = (bf16[2,64,384]{2,1,0:T(8,128)(2,1)S(1)}, bf16[2,64,384]{2,1,0:T(8,128)(2,1)S(1)}, u32[]{:S(2)}, u32[]{:S(2)}) collective-permute-start(bf16[2,64,384]{2,1,0:T(8,128)(2,1)S(1)} %collective-permute-done.2.refs_3_), channel_id=1, source_target_pairs={{0,1},{1,0},{2,3},{3,2},{4,5},{5,4},{6,7},{7,6},{8,9},{9,8},{10,11... | collective-permute-start | bytes 294920 | tf_op jit(solution)/shard_map/ppermute | solution.py:425
  11.4 0.8 %collective-permute-done.5.refs_6_ = bf16[2,64,384]{2,1,0:T(8,128)(2,1)S(1)} collective-permute-done((bf16[2,64,384]{2,1,0:T(8,128)(2,1)S(1)}, bf16[2,64,384]{2,1,0:T(8,128)(2,1)S(1)}, u32[]{:S(2)}, u32[]{:S(2)}) %collective-permute-start.5) | collective-permute-done | bytes 98336 | tf_op jit(solution)/shard_map/ppermute | solution.py:425
  12.3 1.6 %upper_rows.1 = (bf16[64,8,128]{2,1,0:T(8,128)(2,1)S(1)}, bf16[2,64,128]{2,1,0:T(8,128)(2,1)S(1)}, bf16[128,256]{1,0:T(8,128)(2,1)S(1)}, f32[16,8,128]{2,1,0:T(8...) custom-call(s32[1]{0:T(128)} %bitcast.1.spot_ref, ...), custom_call_target="tpu_custom_call" | custom-call | tf_op jit(solution)/shard_map/upper_rows/pallas_call | solution.py:371
  14.0 1.6 %collective-permute-start.7 = (bf16[2,64,128]{2,1,0:T(8,128)(2,1)S(1)}, bf16[2,64,128]{2,1,0:T(8,128)(2,1)S(1)}, u32[]{:S(2)}, u32[]{:S(2)}) collective-permute-start(bf16[2,64,128]{2,1,0:T(8,128)(2,1)S(1)} %get-tuple-element.48), channel_id=1, source_target_pairs={{0,8},{8,16},{16,24},{24,0},{1,9},{9,17},{17,25},{25,1},{2,10},{10... | collective-permute-start | bytes 98312 | tf_op jit(solution)/shard_map/ppermute | solution.py:479
  15.6 1.6 %lower_rows.1 = (bf16[64,8,128]{2,1,0:T(8,128)(2,1)S(1)}, f32[3,3,128]{2,1,0:T(4,128)S(1)}, f32[1,128]{1,0:T(1,128)S(1)}, bf16[1024,128]{1,0:T(8,128)(2,1)S(1)},...) custom-call(bf16[64,8,384]{2,1,0:T(8,128)(2,1)S(1)} %get-tuple-element.42.got_ref, ...), custom_call_target="tpu_custom_call" | custom-call | tf_op jit(solution)/shard_map/lower_rows/pallas_call | solution.py:371
  17.2 2.6 %collective-permute-done.7.above_ref = bf16[2,64,128]{2,1,0:T(8,128)(2,1)S(1)} collective-permute-done((bf16[2,64,128]{2,1,0:T(8,128)(2,1)S(1)}, bf16[2,64,128]{2,1,0:T(8,128)(2,1)S(1)}, u32[]{:S(2)}, u32[]{:S(2)}) %collective-permute-start.7) | collective-permute-done | bytes 32800 | tf_op jit(solution)/shard_map/ppermute | solution.py:479
  20.0 2.2 %collective-permute-start.8 = (bf16[2,64,128]{2,1,0:T(8,128)(2,1)S(1)}, bf16[2,64,128]{2,1,0:T(8,128)(2,1)S(1)}, u32[]{:S(2)}, u32[]{:S(2)}) collective-permute-start(bf16[2,64,128]{2,1,0:T(8,128)(2,1)S(1)} %get-tuple-element.52), channel_id=1, source_target_pairs={{0,6},{1,7},{2,4},{3,5},{4,2},{5,3},{6,0},{7,1},{8,14},{9,15},{10,... | collective-permute-start | bytes 98312 | tf_op jit(solution)/shard_map/ppermute | solution.py:422
  22.2 0.5 %collective-permute-start.9 = (bf16[2,64,128]{2,1,0:T(8,128)(2,1)S(1)}, bf16[2,64,128]{2,1,0:T(8,128)(2,1)S(1)}, u32[]{:S(2)}, u32[]{:S(2)}) collective-permute-start(bf16[2,64,128]{2,1,0:T(8,128)(2,1)S(1)} %get-tuple-element.53), channel_id=1, source_target_pairs={{0,2},{1,3},{2,0},{3,1},{4,6},{5,7},{6,4},{7,5},{8,10},{9,11},{10,... | collective-permute-start | bytes 98312 | tf_op jit(solution)/shard_map/ppermute | solution.py:422
  22.8 0.8 %collective-permute-start.10 = (bf16[2,64,128]{2,1,0:T(8,128)(2,1)S(1)}, bf16[2,64,128]{2,1,0:T(8,128)(2,1)S(1)}, u32[]{:S(2)}, u32[]{:S(2)}) collective-permute-start(bf16[2,64,128]{2,1,0:T(8,128)(2,1)S(1)} %get-tuple-element.54), channel_id=1, source_target_pairs={{0,4},{1,5},{2,6},{3,7},{4,0},{5,1},{6,2},{7,3},{8,12},{9,13},{10,... | collective-permute-start | bytes 98312 | tf_op jit(solution)/shard_map/ppermute | solution.py:422
  23.6 1.3 %collective-permute-done.8.refs_1_ = bf16[2,64,128]{2,1,0:T(8,128)(2,1)S(1)} collective-permute-done((bf16[2,64,128]{2,1,0:T(8,128)(2,1)S(1)}, bf16[2,64,128]{2,1,0:T(8,128)(2,1)S(1)}, u32[]{:S(2)}, u32[]{:S(2)}) %collective-permute-start.8) | collective-permute-done | bytes 32800 | tf_op jit(solution)/shard_map/ppermute | solution.py:422
  24.9 1.2 %collective-permute-done.9.refs_2_ = bf16[2,64,128]{2,1,0:T(8,128)(2,1)S(1)} collective-permute-done((bf16[2,64,128]{2,1,0:T(8,128)(2,1)S(1)}, bf16[2,64,128]{2,1,0:T(8,128)(2,1)S(1)}, u32[]{:S(2)}, u32[]{:S(2)}) %collective-permute-start.9) | collective-permute-done | bytes 32800 | tf_op jit(solution)/shard_map/ppermute | solution.py:422
  26.2 0.5 %collective-permute-done.10.refs_3_ = bf16[2,64,128]{2,1,0:T(8,128)(2,1)S(1)} collective-permute-done((bf16[2,64,128]{2,1,0:T(8,128)(2,1)S(1)}, bf16[2,64,128]{2,1,0:T(8,128)(2,1)S(1)}, u32[]{:S(2)}, u32[]{:S(2)}) %collective-permute-start.10) | collective-permute-done | bytes 32800 | tf_op jit(solution)/shard_map/ppermute | solution.py:422
  26.7 0.7 %collective-permute-done.13.refs_6_ = bf16[2,64,128]{2,1,0:T(8,128)(2,1)S(1)} collective-permute-done((bf16[2,64,128]{2,1,0:T(8,128)(2,1)S(1)}, bf16[2,64,128]{2,1,0:T(8,128)(2,1)S(1)}, u32[]{:S(2)}, u32[]{:S(2)}) %collective-permute-start.13) | collective-permute-done | bytes 32800 | tf_op jit(solution)/shard_map/ppermute | solution.py:425
  27.4 0.5 %collective-permute-done.14.refs_7_ = bf16[2,64,128]{2,1,0:T(8,128)(2,1)S(1)} collective-permute-done((bf16[2,64,128]{2,1,0:T(8,128)(2,1)S(1)}, bf16[2,64,128]{2,1,0:T(8,128)(2,1)S(1)}, u32[]{:S(2)}, u32[]{:S(2)}) %collective-permute-start.14) | collective-permute-done | bytes 32800 | tf_op jit(solution)/shard_map/ppermute | solution.py:425
  28.4 2.4 %collective-permute-start.16 = (bf16[64,384]{1,0:T(8,128)(2,1)S(1)}, bf16[64,384]{1,0:T(8,128)(2,1)S(1)}, u32[]{:S(2)}, u32[]{:S(2)}) collective-permute-start(bf16[64,384]{1,0:T(8,128)(2,1)S(1)} %get-tuple-element.58), channel_id=1, source_target_pairs={{0,16},{8,24},{16,0},{24,8},{1,17},{9,25},{17,1},{25,9},{2,18},{10... | collective-permute-start | bytes 147464 | tf_op jit(solution)/shard_map/ppermute | solution.py:519
  30.8 1.5 %collective-permute-start.17 = (bf16[64,384]{1,0:T(8,128)(2,1)S(1)}, bf16[64,384]{1,0:T(8,128)(2,1)S(1)}, u32[]{:S(2)}, u32[]{:S(2)}) collective-permute-start(bf16[64,384]{1,0:T(8,128)(2,1)S(1)} %get-tuple-element.59), channel_id=1, source_target_pairs={{0,24},{8,0},{16,8},{24,16},{1,25},{9,1},{17,9},{25,17},{2,26},{10... | collective-permute-start | bytes 147464 | tf_op jit(solution)/shard_map/ppermute | solution.py:519
  32.2 2.6 %collective-permute-done.15.refs_1_ = bf16[64,384]{1,0:T(8,128)(2,1)S(1)} collective-permute-done((bf16[64,384]{1,0:T(8,128)(2,1)S(1)}, bf16[64,384]{1,0:T(8,128)(2,1)S(1)}, u32[]{:S(2)}, u32[]{:S(2)}) %collective-permute-start.15) | collective-permute-done | bytes 49184 | tf_op jit(solution)/shard_map/ppermute | solution.py:519
  34.8 1.1 %collective-permute-done.16.refs_2_ = bf16[64,384]{1,0:T(8,128)(2,1)S(1)} collective-permute-done((bf16[64,384]{1,0:T(8,128)(2,1)S(1)}, bf16[64,384]{1,0:T(8,128)(2,1)S(1)}, u32[]{:S(2)}, u32[]{:S(2)}) %collective-permute-start.16) | collective-permute-done | bytes 49184 | tf_op jit(solution)/shard_map/ppermute | solution.py:519
  36.0 3.3 %col_scan.1 = bf16[32,8,256]{2,1,0:T(8,128)(2,1)} custom-call(s32[1]{0:T(128)} %bitcast.me_ref, bf16[64,384]{1,0:T(8,128)(2,1)S(1)} %get-tuple-element.56.refs_0_, bf16[64,384]{1,0:T(8,128)(2,1)S(1)} %collective-permute-done.15.refs_1_, bf16[64,384]{1,0:T(8,128)(2,1)S(1)} %collective-permute-done.16.refs_2_, ...), custom_call_target="tpu_custom_call" | custom-call | tf_op jit(solution)/shard_map/col_scan/pallas_call | solution.py:371
  (18 shorter events, 1.1 us)
Async XLA Ops:
  1.7 7.5 %collective-permute-start = (bf16[2,64,384]{2,1,0:T(8,128)(2,1)S(1)}, bf16[2,64,384]{2,1,0:T(8,128)(2,1)S(1)}, u32[]{:S(2)}, u32[]{:S(2)}) collective-permute-start(bf16[2,64,384]{2,1,0:T(8,128)(2,1)S(1)} %get-tuple-element.35), channel_id=1, source_target_pairs={{0,6},{1,7},{2,4},{3,5},{4,2},{5,3},{6,0},{7,1},{8,14},{9,15},{10,... | collective-permute-start | bytes 294920 | tf_op jit(solution)/shard_map/ppermute | solution.py:422
  5.7 5.2 %collective-permute-start.1 = (bf16[2,64,384]{2,1,0:T(8,128)(2,1)S(1)}, bf16[2,64,384]{2,1,0:T(8,128)(2,1)S(1)}, u32[]{:S(2)}, u32[]{:S(2)}) collective-permute-start(bf16[2,64,384]{2,1,0:T(8,128)(2,1)S(1)} %get-tuple-element.36), channel_id=1, source_target_pairs={{0,2},{1,3},{2,0},{3,1},{4,6},{5,7},{6,4},{7,5},{8,10},{9,11},{10,... | collective-permute-start | bytes 294920 | tf_op jit(solution)/shard_map/ppermute | solution.py:422
  6.2 4.7 %collective-permute-start.2 = (bf16[2,64,384]{2,1,0:T(8,128)(2,1)S(1)}, bf16[2,64,384]{2,1,0:T(8,128)(2,1)S(1)}, u32[]{:S(2)}, u32[]{:S(2)}) collective-permute-start(bf16[2,64,384]{2,1,0:T(8,128)(2,1)S(1)} %get-tuple-element.37), channel_id=1, source_target_pairs={{0,4},{1,5},{2,6},{3,7},{4,0},{5,1},{6,2},{7,3},{8,12},{9,13},{10,... | collective-permute-start | bytes 294920 | tf_op jit(solution)/shard_map/ppermute | solution.py:422
  6.3 5.1 %collective-permute-start.3 = (bf16[2,64,384]{2,1,0:T(8,128)(2,1)S(1)}, bf16[2,64,384]{2,1,0:T(8,128)(2,1)S(1)}, u32[]{:S(2)}, u32[]{:S(2)}) collective-permute-start(bf16[2,64,384]{2,1,0:T(8,128)(2,1)S(1)} %get-tuple-element.34.refs_0_), channel_id=1, source_target_pairs={{0,1},{1,0},{2,3},{3,2},{4,5},{5,4},{6,7},{7,6},{8,9},{9,8},{10,11... | collective-permute-start | bytes 294920 | tf_op jit(solution)/shard_map/ppermute | solution.py:425
  9.2 2.3 %collective-permute-start.4 = (bf16[2,64,384]{2,1,0:T(8,128)(2,1)S(1)}, bf16[2,64,384]{2,1,0:T(8,128)(2,1)S(1)}, u32[]{:S(2)}, u32[]{:S(2)}) collective-permute-start(bf16[2,64,384]{2,1,0:T(8,128)(2,1)S(1)} %collective-permute-done.refs_1_), channel_id=1, source_target_pairs={{0,1},{1,0},{2,3},{3,2},{4,5},{5,4},{6,7},{7,6},{8,9},{9,8},{10,11... | collective-permute-start | bytes 294920 | tf_op jit(solution)/shard_map/ppermute | solution.py:425
  10.9 1.3 %collective-permute-start.5 = (bf16[2,64,384]{2,1,0:T(8,128)(2,1)S(1)}, bf16[2,64,384]{2,1,0:T(8,128)(2,1)S(1)}, u32[]{:S(2)}, u32[]{:S(2)}) collective-permute-start(bf16[2,64,384]{2,1,0:T(8,128)(2,1)S(1)} %collective-permute-done.1.refs_2_), channel_id=1, source_target_pairs={{0,1},{1,0},{2,3},{3,2},{4,5},{5,4},{6,7},{7,6},{8,9},{9,8},{10,11... | collective-permute-start | bytes 294920 | tf_op jit(solution)/shard_map/ppermute | solution.py:425
  10.9 1.5 %collective-permute-start.6 = (bf16[2,64,384]{2,1,0:T(8,128)(2,1)S(1)}, bf16[2,64,384]{2,1,0:T(8,128)(2,1)S(1)}, u32[]{:S(2)}, u32[]{:S(2)}) collective-permute-start(bf16[2,64,384]{2,1,0:T(8,128)(2,1)S(1)} %collective-permute-done.2.refs_3_), channel_id=1, source_target_pairs={{0,1},{1,0},{2,3},{3,2},{4,5},{5,4},{6,7},{7,6},{8,9},{9,8},{10,11... | collective-permute-start | bytes 294920 | tf_op jit(solution)/shard_map/ppermute | solution.py:425
  14.0 5.8 %collective-permute-start.7 = (bf16[2,64,128]{2,1,0:T(8,128)(2,1)S(1)}, bf16[2,64,128]{2,1,0:T(8,128)(2,1)S(1)}, u32[]{:S(2)}, u32[]{:S(2)}) collective-permute-start(bf16[2,64,128]{2,1,0:T(8,128)(2,1)S(1)} %get-tuple-element.48), channel_id=1, source_target_pairs={{0,8},{8,16},{16,24},{24,0},{1,9},{9,17},{17,25},{25,1},{2,10},{10... | collective-permute-start | bytes 98312 | tf_op jit(solution)/shard_map/ppermute | solution.py:479
  20.0 4.9 %collective-permute-start.8 = (bf16[2,64,128]{2,1,0:T(8,128)(2,1)S(1)}, bf16[2,64,128]{2,1,0:T(8,128)(2,1)S(1)}, u32[]{:S(2)}, u32[]{:S(2)}) collective-permute-start(bf16[2,64,128]{2,1,0:T(8,128)(2,1)S(1)} %get-tuple-element.52), channel_id=1, source_target_pairs={{0,6},{1,7},{2,4},{3,5},{4,2},{5,3},{6,0},{7,1},{8,14},{9,15},{10,... | collective-permute-start | bytes 98312 | tf_op jit(solution)/shard_map/ppermute | solution.py:422
  22.2 3.9 %collective-permute-start.9 = (bf16[2,64,128]{2,1,0:T(8,128)(2,1)S(1)}, bf16[2,64,128]{2,1,0:T(8,128)(2,1)S(1)}, u32[]{:S(2)}, u32[]{:S(2)}) collective-permute-start(bf16[2,64,128]{2,1,0:T(8,128)(2,1)S(1)} %get-tuple-element.53), channel_id=1, source_target_pairs={{0,2},{1,3},{2,0},{3,1},{4,6},{5,7},{6,4},{7,5},{8,10},{9,11},{10,... | collective-permute-start | bytes 98312 | tf_op jit(solution)/shard_map/ppermute | solution.py:422
  22.8 3.9 %collective-permute-start.10 = (bf16[2,64,128]{2,1,0:T(8,128)(2,1)S(1)}, bf16[2,64,128]{2,1,0:T(8,128)(2,1)S(1)}, u32[]{:S(2)}, u32[]{:S(2)}) collective-permute-start(bf16[2,64,128]{2,1,0:T(8,128)(2,1)S(1)} %get-tuple-element.54), channel_id=1, source_target_pairs={{0,4},{1,5},{2,6},{3,7},{4,0},{5,1},{6,2},{7,3},{8,12},{9,13},{10,... | collective-permute-start | bytes 98312 | tf_op jit(solution)/shard_map/ppermute | solution.py:422
  23.6 3.1 %collective-permute-start.11 = (bf16[2,64,128]{2,1,0:T(8,128)(2,1)S(1)}, bf16[2,64,128]{2,1,0:T(8,128)(2,1)S(1)}, u32[]{:S(2)}, u32[]{:S(2)}) collective-permute-start(bf16[2,64,128]{2,1,0:T(8,128)(2,1)S(1)} %get-tuple-element.51.refs_0_), channel_id=1, source_target_pairs={{0,1},{1,0},{2,3},{3,2},{4,5},{5,4},{6,7},{7,6},{8,9},{9,8},{10,11... | collective-permute-start | bytes 98312 | tf_op jit(solution)/shard_map/ppermute | solution.py:425
  24.9 1.8 %collective-permute-start.12 = (bf16[2,64,128]{2,1,0:T(8,128)(2,1)S(1)}, bf16[2,64,128]{2,1,0:T(8,128)(2,1)S(1)}, u32[]{:S(2)}, u32[]{:S(2)}) collective-permute-start(bf16[2,64,128]{2,1,0:T(8,128)(2,1)S(1)} %collective-permute-done.8.refs_1_), channel_id=1, source_target_pairs={{0,1},{1,0},{2,3},{3,2},{4,5},{5,4},{6,7},{7,6},{8,9},{9,8},{10,11... | collective-permute-start | bytes 98312 | tf_op jit(solution)/shard_map/ppermute | solution.py:425
  26.2 1.2 %collective-permute-start.13 = (bf16[2,64,128]{2,1,0:T(8,128)(2,1)S(1)}, bf16[2,64,128]{2,1,0:T(8,128)(2,1)S(1)}, u32[]{:S(2)}, u32[]{:S(2)}) collective-permute-start(bf16[2,64,128]{2,1,0:T(8,128)(2,1)S(1)} %collective-permute-done.9.refs_2_), channel_id=1, source_target_pairs={{0,1},{1,0},{2,3},{3,2},{4,5},{5,4},{6,7},{7,6},{8,9},{9,8},{10,11... | collective-permute-start | bytes 98312 | tf_op jit(solution)/shard_map/ppermute | solution.py:425
  26.7 1.2 %collective-permute-start.14 = (bf16[2,64,128]{2,1,0:T(8,128)(2,1)S(1)}, bf16[2,64,128]{2,1,0:T(8,128)(2,1)S(1)}, u32[]{:S(2)}, u32[]{:S(2)}) collective-permute-start(bf16[2,64,128]{2,1,0:T(8,128)(2,1)S(1)} %collective-permute-done.10.refs_3_), channel_id=1, source_target_pairs={{0,1},{1,0},{2,3},{3,2},{4,5},{5,4},{6,7},{7,6},{8,9},{9,8},{10,11... | collective-permute-start | bytes 98312 | tf_op jit(solution)/shard_map/ppermute | solution.py:425
  28.3 6.5 %collective-permute-start.15 = (bf16[64,384]{1,0:T(8,128)(2,1)S(1)}, bf16[64,384]{1,0:T(8,128)(2,1)S(1)}, u32[]{:S(2)}, u32[]{:S(2)}) collective-permute-start(bf16[64,384]{1,0:T(8,128)(2,1)S(1)} %get-tuple-element.57), channel_id=1, source_target_pairs={{0,8},{8,16},{16,24},{24,0},{1,9},{9,17},{17,25},{25,1},{2,10},{10... | collective-permute-start | bytes 147464 | tf_op jit(solution)/shard_map/ppermute | solution.py:519
  28.4 7.6 %collective-permute-start.16 = (bf16[64,384]{1,0:T(8,128)(2,1)S(1)}, bf16[64,384]{1,0:T(8,128)(2,1)S(1)}, u32[]{:S(2)}, u32[]{:S(2)}) collective-permute-start(bf16[64,384]{1,0:T(8,128)(2,1)S(1)} %get-tuple-element.58), channel_id=1, source_target_pairs={{0,16},{8,24},{16,0},{24,8},{1,17},{9,25},{17,1},{25,9},{2,18},{10... | collective-permute-start | bytes 147464 | tf_op jit(solution)/shard_map/ppermute | solution.py:519
  30.8 5.2 %collective-permute-start.17 = (bf16[64,384]{1,0:T(8,128)(2,1)S(1)}, bf16[64,384]{1,0:T(8,128)(2,1)S(1)}, u32[]{:S(2)}, u32[]{:S(2)}) collective-permute-start(bf16[64,384]{1,0:T(8,128)(2,1)S(1)} %get-tuple-element.59), channel_id=1, source_target_pairs={{0,24},{8,0},{16,8},{24,16},{1,25},{9,1},{17,9},{25,17},{2,26},{10... | collective-permute-start | bytes 147464 | tf_op jit(solution)/shard_map/ppermute | solution.py:519

commit v7 on v6

--- a/solution.py
+++ b/solution.py
@@ -167,7 +167,7 @@
 def joint_scan(step_ref, value_ref, rates_ref, pick_ref, ends_ref, out_ref):
     positions, lines, channels = out_ref.shape
     state = rates_ref.shape[0]
-    size = math.gcd(positions, 8)
+    size = math.gcd(positions, 16)
     held = [jnp.zeros((lines, channels), F32)] * state
     for first in range(0, positions, size):
         steps = [step_ref[first + p] for p in range(size)]

time: 39.4 us -> 39.4 us (level)
  Pallas kernels: 8.85 us -> 9.61 us
  waiting for transfers between devices: 16.1 us -> 15.4 us
    ppermute x1, waiting for transfers between devices: 2.57 us -> 1.8 us  [local(): lax.ppermute(tail, 'row', [(i, (i + 1) % n_row) for i in range(n_row)])]
    pallas_call x6, Pallas kernels: 8.85 us -> 9.61 us  [call(): pl.pallas_call(kernel, name=name, out_shape=outs, in_specs=[smem()] * sca...]
  transfers between devices with their start and end apart: 18 -> 18, of which waited for: 12 -> 12; matrix products, arithmetic and copies ran while one was open for 0% -> 0% of each run, Pallas kernels for 4% -> 6%
where the time goes in v7:
time: 39.4 us; the launch traced here: 39.3 us
  waiting for transfers between devices  15.4 us (39%)
  starting transfers between devices  14.2 us (36%)
  Pallas kernels  9.61 us (24%)
    pallas_call x6, Pallas kernels, call(): pl.pallas_call(kernel, name=name, out_shape=outs, in_specs=[smem()] * sca...  9.61 us
    ppermute x6, starting transfers between devices, exchange(): lax.ppermute(piece, 'col', [(i, place(i, s, 0)) for i in range(n_col)])  8.19 us
    ppermute x6, waiting for transfers between devices, exchange(): lax.ppermute(piece, 'col', [(i, place(i, s, 0)) for i in range(n_col)])  7.68 us
    ppermute x3, starting transfers between devices, local(): lax.ppermute(pieces[s], 'row', [(i, (i + s) % n_row) for i in range(n_row)])  3.87 us
    ppermute x3, waiting for transfers between devices, local(): lax.ppermute(pieces[s], 'row', [(i, (i + s) % n_row) for i in range(n_row)])  3.75 us
    ppermute x8, waiting for transfers between devices, exchange(): lax.ppermute(piece, 'col', [(i, i ^ 1) for i in range(n_col)])  2.14 us
    ppermute x1, waiting for transfers between devices, local(): lax.ppermute(tail, 'row', [(i, (i + 1) % n_row) for i in range(n_row)])  1.8 us
    ppermute x1, starting transfers between devices, local(): lax.ppermute(tail, 'row', [(i, (i + 1) % n_row) for i in range(n_row)])  1.62 us
  transfers between devices with their start and end apart: 18, of which 12 were waited for; matrix products, arithmetic and copies ran while one was open for 0% of the time, Pallas kernels for 6%

profile of v7, /device:TPU:0, one launch (start us, length us, event | category | flops | bytes accessed | tf_op | source)
XLA Modules:
  0.0 39.3 jit_solution(7285001033223121823)
XLA Ops:
  0.0 1.7 %pack.1 = (bf16[2,64,384]{2,1,0:T(8,128)(2,1)S(1)}, bf16[2,64,384]{2,1,0:T(8,128)(2,1)S(1)}, bf16[2,64,384]{2,1,0:T(8,128)(2,1)S(1)}, bf16[2,64,384]{2,1,0:T(8,1...) custom-call(s32[1]{0:T(128)} %bitcast.1.spot_ref, ...), custom_call_target="tpu_custom_call" | custom-call | tf_op jit(solution)/shard_map/pack/pallas_call | solution.py:371
  1.7 4.0 %collective-permute-start = (bf16[2,64,384]{2,1,0:T(8,128)(2,1)S(1)}, bf16[2,64,384]{2,1,0:T(8,128)(2,1)S(1)}, u32[]{:S(2)}, u32[]{:S(2)}) collective-permute-start(bf16[2,64,384]{2,1,0:T(8,128)(2,1)S(1)} %get-tuple-element.35), channel_id=1, source_target_pairs={{0,6},{1,7},{2,4},{3,5},{4,2},{5,3},{6,0},{7,1},{8,14},{9,15},{10,... | collective-permute-start | bytes 294920 | tf_op jit(solution)/shard_map/ppermute | solution.py:422
  5.7 0.5 %collective-permute-start.1 = (bf16[2,64,384]{2,1,0:T(8,128)(2,1)S(1)}, bf16[2,64,384]{2,1,0:T(8,128)(2,1)S(1)}, u32[]{:S(2)}, u32[]{:S(2)}) collective-permute-start(bf16[2,64,384]{2,1,0:T(8,128)(2,1)S(1)} %get-tuple-element.36), channel_id=1, source_target_pairs={{0,2},{1,3},{2,0},{3,1},{4,6},{5,7},{6,4},{7,5},{8,10},{9,11},{10,... | collective-permute-start | bytes 294920 | tf_op jit(solution)/shard_map/ppermute | solution.py:422
  6.3 2.9 %collective-permute-done.refs_1_ = bf16[2,64,384]{2,1,0:T(8,128)(2,1)S(1)} collective-permute-done((bf16[2,64,384]{2,1,0:T(8,128)(2,1)S(1)}, bf16[2,64,384]{2,1,0:T(8,128)(2,1)S(1)}, u32[]{:S(2)}, u32[]{:S(2)}) %collective-permute-start) | collective-permute-done | bytes 98336 | tf_op jit(solution)/shard_map/ppermute | solution.py:422
  9.2 1.7 %collective-permute-done.1.refs_2_ = bf16[2,64,384]{2,1,0:T(8,128)(2,1)S(1)} collective-permute-done((bf16[2,64,384]{2,1,0:T(8,128)(2,1)S(1)}, bf16[2,64,384]{2,1,0:T(8,128)(2,1)S(1)}, u32[]{:S(2)}, u32[]{:S(2)}) %collective-permute-start.1) | collective-permute-done | bytes 98336 | tf_op jit(solution)/shard_map/ppermute | solution.py:422
  10.9 0.5 %collective-permute-start.6 = (bf16[2,64,384]{2,1,0:T(8,128)(2,1)S(1)}, bf16[2,64,384]{2,1,0:T(8,128)(2,1)S(1)}, u32[]{:S(2)}, u32[]{:S(2)}) collective-permute-start(bf16[2,64,384]{2,1,0:T(8,128)(2,1)S(1)} %collective-permute-done.2.refs_3_), channel_id=1, source_target_pairs={{0,1},{1,0},{2,3},{3,2},{4,5},{5,4},{6,7},{7,6},{8,9},{9,8},{10,11... | collective-permute-start | bytes 294920 | tf_op jit(solution)/shard_map/ppermute | solution.py:425
  11.4 0.8 %collective-permute-done.5.refs_6_ = bf16[2,64,384]{2,1,0:T(8,128)(2,1)S(1)} collective-permute-done((bf16[2,64,384]{2,1,0:T(8,128)(2,1)S(1)}, bf16[2,64,384]{2,1,0:T(8,128)(2,1)S(1)}, u32[]{:S(2)}, u32[]{:S(2)}) %collective-permute-start.5) | collective-permute-done | bytes 98336 | tf_op jit(solution)/shard_map/ppermute | solution.py:425
  12.3 1.6 %upper_rows.1 = (bf16[64,8,128]{2,1,0:T(8,128)(2,1)S(1)}, bf16[2,64,128]{2,1,0:T(8,128)(2,1)S(1)}, bf16[128,256]{1,0:T(8,128)(2,1)S(1)}, f32[16,8,128]{2,1,0:T(8...) custom-call(s32[1]{0:T(128)} %bitcast.1.spot_ref, ...), custom_call_target="tpu_custom_call" | custom-call | tf_op jit(solution)/shard_map/upper_rows/pallas_call | solution.py:371
  14.0 1.6 %collective-permute-start.7 = (bf16[2,64,128]{2,1,0:T(8,128)(2,1)S(1)}, bf16[2,64,128]{2,1,0:T(8,128)(2,1)S(1)}, u32[]{:S(2)}, u32[]{:S(2)}) collective-permute-start(bf16[2,64,128]{2,1,0:T(8,128)(2,1)S(1)} %get-tuple-element.48), channel_id=1, source_target_pairs={{0,8},{8,16},{16,24},{24,0},{1,9},{9,17},{17,25},{25,1},{2,10},{10... | collective-permute-start | bytes 98312 | tf_op jit(solution)/shard_map/ppermute | solution.py:479
  15.6 2.3 %lower_rows.1 = (bf16[64,8,128]{2,1,0:T(8,128)(2,1)S(1)}, f32[3,3,128]{2,1,0:T(4,128)S(1)}, f32[1,128]{1,0:T(1,128)S(1)}, bf16[1024,128]{1,0:T(8,128)(2,1)S(1)},...) custom-call(bf16[64,8,384]{2,1,0:T(8,128)(2,1)S(1)} %get-tuple-element.42.got_ref, ...), custom_call_target="tpu_custom_call" | custom-call | tf_op jit(solution)/shard_map/lower_rows/pallas_call | solution.py:371
  17.9 1.8 %collective-permute-done.7.above_ref = bf16[2,64,128]{2,1,0:T(8,128)(2,1)S(1)} collective-permute-done((bf16[2,64,128]{2,1,0:T(8,128)(2,1)S(1)}, bf16[2,64,128]{2,1,0:T(8,128)(2,1)S(1)}, u32[]{:S(2)}, u32[]{:S(2)}) %collective-permute-start.7) | collective-permute-done | bytes 32800 | tf_op jit(solution)/shard_map/ppermute | solution.py:479
  20.0 2.2 %collective-permute-start.8 = (bf16[2,64,128]{2,1,0:T(8,128)(2,1)S(1)}, bf16[2,64,128]{2,1,0:T(8,128)(2,1)S(1)}, u32[]{:S(2)}, u32[]{:S(2)}) collective-permute-start(bf16[2,64,128]{2,1,0:T(8,128)(2,1)S(1)} %get-tuple-element.52), channel_id=1, source_target_pairs={{0,6},{1,7},{2,4},{3,5},{4,2},{5,3},{6,0},{7,1},{8,14},{9,15},{10,... | collective-permute-start | bytes 98312 | tf_op jit(solution)/shard_map/ppermute | solution.py:422
  22.2 0.5 %collective-permute-start.9 = (bf16[2,64,128]{2,1,0:T(8,128)(2,1)S(1)}, bf16[2,64,128]{2,1,0:T(8,128)(2,1)S(1)}, u32[]{:S(2)}, u32[]{:S(2)}) collective-permute-start(bf16[2,64,128]{2,1,0:T(8,128)(2,1)S(1)} %get-tuple-element.53), channel_id=1, source_target_pairs={{0,2},{1,3},{2,0},{3,1},{4,6},{5,7},{6,4},{7,5},{8,10},{9,11},{10,... | collective-permute-start | bytes 98312 | tf_op jit(solution)/shard_map/ppermute | solution.py:422
  22.8 0.8 %collective-permute-start.10 = (bf16[2,64,128]{2,1,0:T(8,128)(2,1)S(1)}, bf16[2,64,128]{2,1,0:T(8,128)(2,1)S(1)}, u32[]{:S(2)}, u32[]{:S(2)}) collective-permute-start(bf16[2,64,128]{2,1,0:T(8,128)(2,1)S(1)} %get-tuple-element.54), channel_id=1, source_target_pairs={{0,4},{1,5},{2,6},{3,7},{4,0},{5,1},{6,2},{7,3},{8,12},{9,13},{10,... | collective-permute-start | bytes 98312 | tf_op jit(solution)/shard_map/ppermute | solution.py:422
  23.6 1.3 %collective-permute-done.8.refs_1_ = bf16[2,64,128]{2,1,0:T(8,128)(2,1)S(1)} collective-permute-done((bf16[2,64,128]{2,1,0:T(8,128)(2,1)S(1)}, bf16[2,64,128]{2,1,0:T(8,128)(2,1)S(1)}, u32[]{:S(2)}, u32[]{:S(2)}) %collective-permute-start.8) | collective-permute-done | bytes 32800 | tf_op jit(solution)/shard_map/ppermute | solution.py:422
  24.9 1.2 %collective-permute-done.9.refs_2_ = bf16[2,64,128]{2,1,0:T(8,128)(2,1)S(1)} collective-permute-done((bf16[2,64,128]{2,1,0:T(8,128)(2,1)S(1)}, bf16[2,64,128]{2,1,0:T(8,128)(2,1)S(1)}, u32[]{:S(2)}, u32[]{:S(2)}) %collective-permute-start.9) | collective-permute-done | bytes 32800 | tf_op jit(solution)/shard_map/ppermute | solution.py:422
  26.2 0.5 %collective-permute-done.10.refs_3_ = bf16[2,64,128]{2,1,0:T(8,128)(2,1)S(1)} collective-permute-done((bf16[2,64,128]{2,1,0:T(8,128)(2,1)S(1)}, bf16[2,64,128]{2,1,0:T(8,128)(2,1)S(1)}, u32[]{:S(2)}, u32[]{:S(2)}) %collective-permute-start.10) | collective-permute-done | bytes 32800 | tf_op jit(solution)/shard_map/ppermute | solution.py:422
  26.7 0.7 %collective-permute-done.13.refs_6_ = bf16[2,64,128]{2,1,0:T(8,128)(2,1)S(1)} collective-permute-done((bf16[2,64,128]{2,1,0:T(8,128)(2,1)S(1)}, bf16[2,64,128]{2,1,0:T(8,128)(2,1)S(1)}, u32[]{:S(2)}, u32[]{:S(2)}) %collective-permute-start.13) | collective-permute-done | bytes 32800 | tf_op jit(solution)/shard_map/ppermute | solution.py:425
  27.4 0.5 %collective-permute-done.14.refs_7_ = bf16[2,64,128]{2,1,0:T(8,128)(2,1)S(1)} collective-permute-done((bf16[2,64,128]{2,1,0:T(8,128)(2,1)S(1)}, bf16[2,64,128]{2,1,0:T(8,128)(2,1)S(1)}, u32[]{:S(2)}, u32[]{:S(2)}) %collective-permute-start.14) | collective-permute-done | bytes 32800 | tf_op jit(solution)/shard_map/ppermute | solution.py:425
  28.4 2.4 %collective-permute-start.16 = (bf16[64,384]{1,0:T(8,128)(2,1)S(1)}, bf16[64,384]{1,0:T(8,128)(2,1)S(1)}, u32[]{:S(2)}, u32[]{:S(2)}) collective-permute-start(bf16[64,384]{1,0:T(8,128)(2,1)S(1)} %get-tuple-element.58), channel_id=1, source_target_pairs={{0,16},{8,24},{16,0},{24,8},{1,17},{9,25},{17,1},{25,9},{2,18},{10... | collective-permute-start | bytes 147464 | tf_op jit(solution)/shard_map/ppermute | solution.py:519
  30.8 1.5 %collective-permute-start.17 = (bf16[64,384]{1,0:T(8,128)(2,1)S(1)}, bf16[64,384]{1,0:T(8,128)(2,1)S(1)}, u32[]{:S(2)}, u32[]{:S(2)}) collective-permute-start(bf16[64,384]{1,0:T(8,128)(2,1)S(1)} %get-tuple-element.59), channel_id=1, source_target_pairs={{0,24},{8,0},{16,8},{24,16},{1,25},{9,1},{17,9},{25,17},{2,26},{10... | collective-permute-start | bytes 147464 | tf_op jit(solution)/shard_map/ppermute | solution.py:519
  32.2 2.6 %collective-permute-done.15.refs_1_ = bf16[64,384]{1,0:T(8,128)(2,1)S(1)} collective-permute-done((bf16[64,384]{1,0:T(8,128)(2,1)S(1)}, bf16[64,384]{1,0:T(8,128)(2,1)S(1)}, u32[]{:S(2)}, u32[]{:S(2)}) %collective-permute-start.15) | collective-permute-done | bytes 49184 | tf_op jit(solution)/shard_map/ppermute | solution.py:519
  34.8 1.1 %collective-permute-done.16.refs_2_ = bf16[64,384]{1,0:T(8,128)(2,1)S(1)} collective-permute-done((bf16[64,384]{1,0:T(8,128)(2,1)S(1)}, bf16[64,384]{1,0:T(8,128)(2,1)S(1)}, u32[]{:S(2)}, u32[]{:S(2)}) %collective-permute-start.16) | collective-permute-done | bytes 49184 | tf_op jit(solution)/shard_map/ppermute | solution.py:519
  36.0 3.3 %col_scan.1 = bf16[32,8,256]{2,1,0:T(8,128)(2,1)} custom-call(s32[1]{0:T(128)} %bitcast.me_ref, bf16[64,384]{1,0:T(8,128)(2,1)S(1)} %get-tuple-element.56.refs_0_, bf16[64,384]{1,0:T(8,128)(2,1)S(1)} %collective-permute-done.15.refs_1_, bf16[64,384]{1,0:T(8,128)(2,1)S(1)} %collective-permute-done.16.refs_2_, ...), custom_call_target="tpu_custom_call" | custom-call | tf_op jit(solution)/shard_map/col_scan/pallas_call | solution.py:371
  (18 shorter events, 1.1 us)
Async XLA Ops:
  1.7 7.5 %collective-permute-start = (bf16[2,64,384]{2,1,0:T(8,128)(2,1)S(1)}, bf16[2,64,384]{2,1,0:T(8,128)(2,1)S(1)}, u32[]{:S(2)}, u32[]{:S(2)}) collective-permute-start(bf16[2,64,384]{2,1,0:T(8,128)(2,1)S(1)} %get-tuple-element.35), channel_id=1, source_target_pairs={{0,6},{1,7},{2,4},{3,5},{4,2},{5,3},{6,0},{7,1},{8,14},{9,15},{10,... | collective-permute-start | bytes 294920 | tf_op jit(solution)/shard_map/ppermute | solution.py:422
  5.7 5.2 %collective-permute-start.1 = (bf16[2,64,384]{2,1,0:T(8,128)(2,1)S(1)}, bf16[2,64,384]{2,1,0:T(8,128)(2,1)S(1)}, u32[]{:S(2)}, u32[]{:S(2)}) collective-permute-start(bf16[2,64,384]{2,1,0:T(8,128)(2,1)S(1)} %get-tuple-element.36), channel_id=1, source_target_pairs={{0,2},{1,3},{2,0},{3,1},{4,6},{5,7},{6,4},{7,5},{8,10},{9,11},{10,... | collective-permute-start | bytes 294920 | tf_op jit(solution)/shard_map/ppermute | solution.py:422
  6.2 4.7 %collective-permute-start.2 = (bf16[2,64,384]{2,1,0:T(8,128)(2,1)S(1)}, bf16[2,64,384]{2,1,0:T(8,128)(2,1)S(1)}, u32[]{:S(2)}, u32[]{:S(2)}) collective-permute-start(bf16[2,64,384]{2,1,0:T(8,128)(2,1)S(1)} %get-tuple-element.37), channel_id=1, source_target_pairs={{0,4},{1,5},{2,6},{3,7},{4,0},{5,1},{6,2},{7,3},{8,12},{9,13},{10,... | collective-permute-start | bytes 294920 | tf_op jit(solution)/shard_map/ppermute | solution.py:422
  6.3 5.1 %collective-permute-start.3 = (bf16[2,64,384]{2,1,0:T(8,128)(2,1)S(1)}, bf16[2,64,384]{2,1,0:T(8,128)(2,1)S(1)}, u32[]{:S(2)}, u32[]{:S(2)}) collective-permute-start(bf16[2,64,384]{2,1,0:T(8,128)(2,1)S(1)} %get-tuple-element.34.refs_0_), channel_id=1, source_target_pairs={{0,1},{1,0},{2,3},{3,2},{4,5},{5,4},{6,7},{7,6},{8,9},{9,8},{10,11... | collective-permute-start | bytes 294920 | tf_op jit(solution)/shard_map/ppermute | solution.py:425
  9.2 2.3 %collective-permute-start.4 = (bf16[2,64,384]{2,1,0:T(8,128)(2,1)S(1)}, bf16[2,64,384]{2,1,0:T(8,128)(2,1)S(1)}, u32[]{:S(2)}, u32[]{:S(2)}) collective-permute-start(bf16[2,64,384]{2,1,0:T(8,128)(2,1)S(1)} %collective-permute-done.refs_1_), channel_id=1, source_target_pairs={{0,1},{1,0},{2,3},{3,2},{4,5},{5,4},{6,7},{7,6},{8,9},{9,8},{10,11... | collective-permute-start | bytes 294920 | tf_op jit(solution)/shard_map/ppermute | solution.py:425
  10.9 1.3 %collective-permute-start.5 = (bf16[2,64,384]{2,1,0:T(8,128)(2,1)S(1)}, bf16[2,64,384]{2,1,0:T(8,128)(2,1)S(1)}, u32[]{:S(2)}, u32[]{:S(2)}) collective-permute-start(bf16[2,64,384]{2,1,0:T(8,128)(2,1)S(1)} %collective-permute-done.1.refs_2_), channel_id=1, source_target_pairs={{0,1},{1,0},{2,3},{3,2},{4,5},{5,4},{6,7},{7,6},{8,9},{9,8},{10,11... | collective-permute-start | bytes 294920 | tf_op jit(solution)/shard_map/ppermute | solution.py:425
  10.9 1.5 %collective-permute-start.6 = (bf16[2,64,384]{2,1,0:T(8,128)(2,1)S(1)}, bf16[2,64,384]{2,1,0:T(8,128)(2,1)S(1)}, u32[]{:S(2)}, u32[]{:S(2)}) collective-permute-start(bf16[2,64,384]{2,1,0:T(8,128)(2,1)S(1)} %collective-permute-done.2.refs_3_), channel_id=1, source_target_pairs={{0,1},{1,0},{2,3},{3,2},{4,5},{5,4},{6,7},{7,6},{8,9},{9,8},{10,11... | collective-permute-start | bytes 294920 | tf_op jit(solution)/shard_map/ppermute | solution.py:425
  14.0 5.8 %collective-permute-start.7 = (bf16[2,64,128]{2,1,0:T(8,128)(2,1)S(1)}, bf16[2,64,128]{2,1,0:T(8,128)(2,1)S(1)}, u32[]{:S(2)}, u32[]{:S(2)}) collective-permute-start(bf16[2,64,128]{2,1,0:T(8,128)(2,1)S(1)} %get-tuple-element.48), channel_id=1, source_target_pairs={{0,8},{8,16},{16,24},{24,0},{1,9},{9,17},{17,25},{25,1},{2,10},{10... | collective-permute-start | bytes 98312 | tf_op jit(solution)/shard_map/ppermute | solution.py:479
  20.0 4.9 %collective-permute-start.8 = (bf16[2,64,128]{2,1,0:T(8,128)(2,1)S(1)}, bf16[2,64,128]{2,1,0:T(8,128)(2,1)S(1)}, u32[]{:S(2)}, u32[]{:S(2)}) collective-permute-start(bf16[2,64,128]{2,1,0:T(8,128)(2,1)S(1)} %get-tuple-element.52), channel_id=1, source_target_pairs={{0,6},{1,7},{2,4},{3,5},{4,2},{5,3},{6,0},{7,1},{8,14},{9,15},{10,... | collective-permute-start | bytes 98312 | tf_op jit(solution)/shard_map/ppermute | solution.py:422
  22.2 3.9 %collective-permute-start.9 = (bf16[2,64,128]{2,1,0:T(8,128)(2,1)S(1)}, bf16[2,64,128]{2,1,0:T(8,128)(2,1)S(1)}, u32[]{:S(2)}, u32[]{:S(2)}) collective-permute-start(bf16[2,64,128]{2,1,0:T(8,128)(2,1)S(1)} %get-tuple-element.53), channel_id=1, source_target_pairs={{0,2},{1,3},{2,0},{3,1},{4,6},{5,7},{6,4},{7,5},{8,10},{9,11},{10,... | collective-permute-start | bytes 98312 | tf_op jit(solution)/shard_map/ppermute | solution.py:422
  22.8 3.9 %collective-permute-start.10 = (bf16[2,64,128]{2,1,0:T(8,128)(2,1)S(1)}, bf16[2,64,128]{2,1,0:T(8,128)(2,1)S(1)}, u32[]{:S(2)}, u32[]{:S(2)}) collective-permute-start(bf16[2,64,128]{2,1,0:T(8,128)(2,1)S(1)} %get-tuple-element.54), channel_id=1, source_target_pairs={{0,4},{1,5},{2,6},{3,7},{4,0},{5,1},{6,2},{7,3},{8,12},{9,13},{10,... | collective-permute-start | bytes 98312 | tf_op jit(solution)/shard_map/ppermute | solution.py:422
  23.6 3.1 %collective-permute-start.11 = (bf16[2,64,128]{2,1,0:T(8,128)(2,1)S(1)}, bf16[2,64,128]{2,1,0:T(8,128)(2,1)S(1)}, u32[]{:S(2)}, u32[]{:S(2)}) collective-permute-start(bf16[2,64,128]{2,1,0:T(8,128)(2,1)S(1)} %get-tuple-element.51.refs_0_), channel_id=1, source_target_pairs={{0,1},{1,0},{2,3},{3,2},{4,5},{5,4},{6,7},{7,6},{8,9},{9,8},{10,11... | collective-permute-start | bytes 98312 | tf_op jit(solution)/shard_map/ppermute | solution.py:425
  24.9 1.8 %collective-permute-start.12 = (bf16[2,64,128]{2,1,0:T(8,128)(2,1)S(1)}, bf16[2,64,128]{2,1,0:T(8,128)(2,1)S(1)}, u32[]{:S(2)}, u32[]{:S(2)}) collective-permute-start(bf16[2,64,128]{2,1,0:T(8,128)(2,1)S(1)} %collective-permute-done.8.refs_1_), channel_id=1, source_target_pairs={{0,1},{1,0},{2,3},{3,2},{4,5},{5,4},{6,7},{7,6},{8,9},{9,8},{10,11... | collective-permute-start | bytes 98312 | tf_op jit(solution)/shard_map/ppermute | solution.py:425
  26.2 1.2 %collective-permute-start.13 = (bf16[2,64,128]{2,1,0:T(8,128)(2,1)S(1)}, bf16[2,64,128]{2,1,0:T(8,128)(2,1)S(1)}, u32[]{:S(2)}, u32[]{:S(2)}) collective-permute-start(bf16[2,64,128]{2,1,0:T(8,128)(2,1)S(1)} %collective-permute-done.9.refs_2_), channel_id=1, source_target_pairs={{0,1},{1,0},{2,3},{3,2},{4,5},{5,4},{6,7},{7,6},{8,9},{9,8},{10,11... | collective-permute-start | bytes 98312 | tf_op jit(solution)/shard_map/ppermute | solution.py:425
  26.7 1.2 %collective-permute-start.14 = (bf16[2,64,128]{2,1,0:T(8,128)(2,1)S(1)}, bf16[2,64,128]{2,1,0:T(8,128)(2,1)S(1)}, u32[]{:S(2)}, u32[]{:S(2)}) collective-permute-start(bf16[2,64,128]{2,1,0:T(8,128)(2,1)S(1)} %collective-permute-done.10.refs_3_), channel_id=1, source_target_pairs={{0,1},{1,0},{2,3},{3,2},{4,5},{5,4},{6,7},{7,6},{8,9},{9,8},{10,11... | collective-permute-start | bytes 98312 | tf_op jit(solution)/shard_map/ppermute | solution.py:425
  28.3 6.5 %collective-permute-start.15 = (bf16[64,384]{1,0:T(8,128)(2,1)S(1)}, bf16[64,384]{1,0:T(8,128)(2,1)S(1)}, u32[]{:S(2)}, u32[]{:S(2)}) collective-permute-start(bf16[64,384]{1,0:T(8,128)(2,1)S(1)} %get-tuple-element.57), channel_id=1, source_target_pairs={{0,8},{8,16},{16,24},{24,0},{1,9},{9,17},{17,25},{25,1},{2,10},{10... | collective-permute-start | bytes 147464 | tf_op jit(solution)/shard_map/ppermute | solution.py:519
  28.4 7.6 %collective-permute-start.16 = (bf16[64,384]{1,0:T(8,128)(2,1)S(1)}, bf16[64,384]{1,0:T(8,128)(2,1)S(1)}, u32[]{:S(2)}, u32[]{:S(2)}) collective-permute-start(bf16[64,384]{1,0:T(8,128)(2,1)S(1)} %get-tuple-element.58), channel_id=1, source_target_pairs={{0,16},{8,24},{16,0},{24,8},{1,17},{9,25},{17,1},{25,9},{2,18},{10... | collective-permute-start | bytes 147464 | tf_op jit(solution)/shard_map/ppermute | solution.py:519
  30.8 5.2 %collective-permute-start.17 = (bf16[64,384]{1,0:T(8,128)(2,1)S(1)}, bf16[64,384]{1,0:T(8,128)(2,1)S(1)}, u32[]{:S(2)}, u32[]{:S(2)}) collective-permute-start(bf16[64,384]{1,0:T(8,128)(2,1)S(1)} %get-tuple-element.59), channel_id=1, source_target_pairs={{0,24},{8,0},{16,8},{24,16},{1,25},{9,1},{17,9},{25,17},{2,26},{10... | collective-permute-start | bytes 147464 | tf_op jit(solution)/shard_map/ppermute | solution.py:519
